TPU v7x, 32 devices: a whole 2x2x4 slice. The times are simulated.
32 devices in a mesh: batch: 4 (over x, core), seq: 8 (over z, y).
Axes of the slice: x: 2, y: 2, z: 4, core: 2. Of those that a mesh axis runs over, the one named last changes fastest.
Arguments:
- inputs: bfloat16 [16, 2048, 512], P('batch', 'seq'), may hold values from -6 to 6
- cotangent: float32 [16, 2048, 512], P('batch', 'seq'), may hold values from -6 to 6
- query_weight: bfloat16 [512, 512], P('seq', 'batch'), may hold values from -0.25 to 0.25
- key_weight: bfloat16 [512, 512], P('seq', 'batch'), may hold values from -0.25 to 0.25
- value_weight: bfloat16 [512, 512], P('seq', 'batch'), may hold values from -0.25 to 0.25
- out_weight: bfloat16 [512, 512], P('seq', 'batch'), may hold values from -0.75 to 0.75
- up_weight: bfloat16 [512, 2048], P('seq', 'batch'), may hold values from -0.25 to 0.25
- down_weight: bfloat16 [2048, 512], P('seq', 'batch'), may hold values from -0.125 to 0.125
- norm1_gain: bfloat16 [512], P('seq'), may hold values from 0.5 to 1.5
- norm1_bias: bfloat16 [512], P('seq'), may hold values from -0.59765625 to 0.59765625
- norm2_gain: bfloat16 [512], P('seq'), may hold values from 0.5 to 1.5
- norm2_bias: bfloat16 [512], P('seq'), may hold values from -0.59765625 to 0.59765625
- out_bias: bfloat16 [512], P('seq'), may hold values from -0.59765625 to 0.59765625
- up_bias: bfloat16 [2048], P('seq'), may hold values from -0.59765625 to 0.59765625
- down_bias: bfloat16 [512], P('seq'), may hold values from -0.59765625 to 0.59765625
Outputs:
- outputs: bfloat16 [16, 2048, 512], P('batch', 'seq')
- input_grad: float32 [16, 2048, 512], P('batch', 'seq')
- query_grad: float32 [512, 512], P('seq', 'batch')
- key_grad: float32 [512, 512], P('seq', 'batch')
- value_grad: float32 [512, 512], P('seq', 'batch')
- out_grad: float32 [512, 512], P('seq', 'batch')
- up_grad: float32 [512, 2048], P('seq', 'batch')
- down_grad: float32 [2048, 512], P('seq', 'batch')
- norm1_gain_grad: float32 [512], P('seq')
- norm1_bias_grad: float32 [512], P('seq')
- norm2_gain_grad: float32 [512], P('seq')
- norm2_bias_grad: float32 [512], P('seq')
- out_bias_grad: float32 [512], P('seq')
- up_bias_grad: float32 [2048], P('seq')
- down_bias_grad: float32 [512], P('seq')
All inputs are finite; a program needn't handle non-finite values.
Results may differ from a plain program's by a relative error of at most 0.014.
Values may be sent and summed in bfloat16 or wider, within the bound.
No kernel may reach another device: no remote copies, remote signals or barrier semaphores. Data moves between devices by JAX's collectives and lax.ppermute only.
A program may use at most 128 MiB of HBM per device.

v0:
```python
import jax
import jax.numpy as jnp
from jax import lax
from jax.experimental import pallas as pl
from jax.experimental.pallas import tpu as pltpu
from jax.sharding import PartitionSpec as P

HEADS = 8
HEAD = 64
VEC_ROWS = 32
F32 = jnp.float32
BF16 = jnp.bfloat16


def swap(array, axis, bit):
    count = lax.axis_size(axis)
    return lax.ppermute(array, axis, [(i, i ^ bit) for i in range(count)])


def bits_down(count):
    return [1 << k for k in range(count.bit_length() - 2, -1, -1)]


def outer_stages():
    seq = [("seq", bit) for bit in bits_down(lax.axis_size("seq")) if bit > 1]
    batch = [("batch", bit) for bit in bits_down(lax.axis_size("batch")) if bit > 2]
    return batch + seq


def relative_ids(stages):
    ids = [(0, 0)]
    for axis, bit in stages:
        moved = [(s ^ bit, b) if axis == "seq" else (s, b ^ bit) for s, b in ids]
        ids = ids + moved
    return ids


X_STAGE = ("batch", 2)
Y_STAGE = ("seq", 1)
CORE = ("batch", 1)


def gather_all(pack):
    rows = pack.shape[0]
    half = rows // 2
    state = pack[None]
    outer = outer_stages()
    for stage in outer:
        state = jnp.concatenate([state, swap(state, *stage)], 0)
    pieces = []
    for first, order in ((0, (X_STAGE, Y_STAGE)), (half, (Y_STAGE, X_STAGE))):
        part = state[:, first : first + half]
        part = jnp.concatenate([part, swap(part, *order[0])], 0)
        far = swap(part, *order[1])
        ids = relative_ids(outer + [order[0]])
        full = relative_ids(outer + list(order))
        far_ids = full[len(ids) :]
        for piece, names in ((part, ids), (far, far_ids)):
            pieces.append((piece, names, first))
            pieces.append((swap(piece, *CORE), [(s, b ^ 1) for s, b in names], first))
    return pieces


def place():
    return jnp.stack([lax.axis_index("seq"), lax.axis_index("batch")]).astype(jnp.int32)


def cuts(segments, first, half):
    found = []
    at = 0
    for name, rows in segments:
        low, high = max(at, first), min(at + rows, first + half)
        if low < high:
            found.append((name, low - at, low - first, high - low))
        at += rows
    return found


def unpack(pieces, segments, targets, shapes):
    arrays = [piece for piece, _, _ in pieces]

    def kernel(spot, *refs):
        ins, outs = refs[: len(arrays)], refs[len(arrays) :]
        for ref, (piece, names, first) in zip(ins, pieces):
            for p, (sr, br) in enumerate(names):
                s, b = spot[0] ^ sr, spot[1] ^ br
                for name, row, here, size in cuts(segments, first, piece.shape[1]):
                    if name == "vec" and br != 0:
                        continue
                    number, top, left = targets(name, row, s, b)
                    outs[number][
                        pl.ds(pl.multiple_of(top, 16), size), pl.ds(pl.multiple_of(left, 128), 128)
                    ] = ref[p, here : here + size, :]

    return pl.pallas_call(
        kernel,
        out_shape=[jax.ShapeDtypeStruct(shape, BF16) for shape in shapes],
        in_specs=[pl.BlockSpec(memory_space=pltpu.SMEM)]
        + [pl.BlockSpec(memory_space=pltpu.VMEM) for _ in arrays],
        out_specs=[pl.BlockSpec(memory_space=pltpu.VMEM) for _ in shapes],
    )(place(), *arrays)


def pack_order():
    outer = outer_stages()
    return [
        relative_ids(outer + [Y_STAGE, X_STAGE, CORE]),
        relative_ids(outer + [X_STAGE, Y_STAGE, CORE]),
    ]


def write_packed(spot, ins, vec_block, outs, segments, targets, orders):
    half = sum(size for _, size in segments) // 2
    for out, names, first in zip(outs, orders, (0, half)):
        for p, (sr, br) in enumerate(names):
            s, b = spot[0] ^ sr, spot[1] ^ br
            for name, row, here, size in cuts(segments, first, half):
                if name == "vec":
                    out[p, here : here + size, :] = vec_block(s)
                else:
                    number, top, left = targets(name, row, s, b)
                    out[p, here : here + size, :] = ins[number][
                        pl.ds(pl.multiple_of(top, 16), size), pl.ds(pl.multiple_of(left, 128), 128)
                    ].astype(BF16)


def add_low(mine, theirs):
    return (mine.astype(F32) + theirs.astype(F32)).astype(BF16)


def join_pair(array):
    count = VEC_ROWS // 2
    return array[..., -VEC_ROWS:-count, :].astype(F32) + array[..., -count:, :].astype(F32)


def split_pair(total):
    high = lax.reduce_precision(total, 8, 7)
    return [high.astype(BF16), (total - high).astype(BF16)]


def add_pairs(mine, theirs):
    total = join_pair(mine) + join_pair(theirs)
    low = add_low(mine[..., :-VEC_ROWS, :], theirs[..., :-VEC_ROWS, :])
    return jnp.concatenate([low] + split_pair(total), -2)


def reduce_all(halves, pairs):
    outer = outer_stages()[::-1]
    done = []
    for k, (state, order) in enumerate(
        zip(halves, ((CORE, X_STAGE, Y_STAGE), (CORE, Y_STAGE, X_STAGE)))
    ):
        add = add_pairs if pairs and k == 1 else add_low
        stages = list(order) + outer
        for stage in stages:
            count = state.shape[0] // 2
            theirs = swap(state[count:], *stage)
            mine = state[:count]
            if stage is stages[-1]:
                if add is add_pairs:
                    total = join_pair(mine) + join_pair(theirs)
                    body = mine[:, :-VEC_ROWS].astype(F32) + theirs[:, :-VEC_ROWS].astype(F32)
                    state = jnp.concatenate([body, total], 1)
                else:
                    state = mine.astype(F32) + theirs.astype(F32)
            else:
                state = add(mine, theirs)
        done.append(state[0])
    return jnp.concatenate(done, 0)


def seq_stages():
    return [("seq", bit) for bit in bits_down(lax.axis_size("seq"))]


def gather_seq(array):
    state = array[None]
    for stage in seq_stages():
        state = jnp.concatenate([state, swap(state, *stage)], 0)
    return state


def reduce_seq(state):
    for stage in seq_stages()[::-1]:
        count = state.shape[0] // 2
        theirs = swap(state[count:], *stage)
        total = state[:count].astype(F32) + theirs.astype(F32)
        state = total if count == 1 else total.astype(BF16)
    return state[0]


def whole_tiles(weights, vectors):
    return (
        all(w.shape[0] % 16 == 0 and w.shape[1] % 128 == 0 for w in weights)
        and all(128 % v.shape[0] == 0 or v.shape[0] % 128 == 0 for v in vectors)
        and sum(v.shape[0] for v in vectors) % 128 == 0
    )


def columns(weights):
    return [
        ((i, c), weight.shape[0])
        for i, weight in enumerate(weights)
        for c in range(weight.shape[1] // 128)
    ]


def packed(weights):
    return [
        weight[:, c : c + 128] for weight in weights for c in range(0, weight.shape[1], 128)
    ]


def spots(weights):
    def targets(name, row, s, b):
        if name == "vec":
            return (len(weights), s * VEC_ROWS + row, 0)
        i, c = name
        rows, width = weights[i].shape
        return (i, s * rows + row, b * width + c * 128)

    return targets


def whole(weights):
    return [
        (w.shape[0] * lax.axis_size("seq"), w.shape[1] * lax.axis_size("batch")) for w in weights
    ]


def gather_group(weights, vectors, after=None):
    blocks = packed(weights)
    segments = columns(weights)
    shapes = whole(weights)
    if vectors:
        flat = jnp.concatenate(vectors).reshape(-1, 128)
        blocks = blocks + [jnp.pad(flat, ((0, VEC_ROWS - flat.shape[0]), (0, 0)))]
        segments = segments + [("vec", VEC_ROWS)]
        shapes = shapes + [(lax.axis_size("seq") * VEC_ROWS, 128)]
    block = jnp.concatenate(blocks, 0)
    if after is not None:
        block = lax.optimization_barrier((block, after))[0]
    pieces = gather_all(block)
    return unpack(pieces, segments, spots(weights), shapes), pieces[-1][0]


def gather_weights(weights, vectors):
    if not whole_tiles(weights, vectors):
        wide = [lax.all_gather(w, "batch", axis=1, tiled=True) for w in weights]
        wide = [lax.all_gather(w, "seq", axis=0, tiled=True) for w in wide]
        return wide, [lax.all_gather(v, "seq", axis=0, tiled=True) for v in vectors]
    first, last = gather_group(weights[:3], vectors)
    second, _ = gather_group(weights[3:], [], last)
    sizes = [v.shape[0] for v in vectors]
    flat = first[3].reshape(lax.axis_size("seq"), VEC_ROWS * 128)
    wide = []
    at = 0
    for size in sizes:
        wide.append(flat[:, at : at + size].reshape(-1))
        at += size
    return first[:3] + second, wide


def reduce_group(weights, halves, sizes):
    rows = reduce_all(halves, True)
    outs = []
    at = 0
    for weight in weights:
        parts = []
        for _ in range(weight.shape[1] // 128):
            parts.append(rows[at : at + weight.shape[0]])
            at += weight.shape[0]
        outs.append(parts[0] if len(parts) == 1 else jnp.concatenate(parts, 1))
    lanes = rows[at:]
    row = 0
    for size in sizes:
        if size < 128:
            part = lax.axis_index("seq") % (128 // size)
            outs.append(lax.dynamic_slice(lanes[row], (part * size,), (size,)))
            row += 1
        else:
            outs.append(lanes[row : row + size // 128].reshape(-1))
            row += size // 128
    return outs


def reduce_plain(weights, grads, vectors):
    outs = [
        lax.psum_scatter(g.astype(BF16), "batch", scatter_dimension=1, tiled=True).astype(F32)
        for g in grads
    ]
    outs = outs + list(lax.psum(tuple(vectors), "batch"))
    return [lax.psum_scatter(o, "seq", scatter_dimension=0, tiled=True) for o in outs]


def dot(left, right, a=1, b=0):
    return lax.dot_general(left, right, (((a,), (b,)), ((), ())), preferred_element_type=F32)


def norm_parts(values):
    centred = values - jnp.mean(values, -1, keepdims=True)
    scale = lax.rsqrt(jnp.mean(centred * centred, -1, keepdims=True) + 1e-05)
    return centred * scale, scale


def norm_back(grad, unit, scale, gain):
    inner = grad * gain
    pull = jnp.mean(inner, -1, keepdims=True)
    twist = jnp.mean(inner * unit, -1, keepdims=True)
    return scale * (inner - pull - unit * twist)


def gelu_pair(values):
    bell = jnp.exp(-0.5 * values * values)
    t = 1.0 / (1.0 + (0.3275911 * 0.5**0.5) * jnp.abs(values))
    poly = 1.061405429 * 0.5
    for factor in (-1.453152027, 1.421413741, -0.284496736, 0.254829592):
        poly = poly * t + factor * 0.5
    below = poly * t * bell
    share = jnp.where(values < 0, below, 1.0 - below)
    return values * share, share + values * bell * 0.3989422804014327


def full(shape):
    return pl.BlockSpec(shape, lambda i: (0,) * len(shape))


def each(shape):
    return pl.BlockSpec((1,) + tuple(shape[1:]), lambda i: (i,) + (0,) * (len(shape) - 1))


def project(inputs, w_query, w_key, w_value, gain, shift):
    count, rows, width = inputs.shape
    half = rows // 2

    def kernel(x_ref, q_ref, k_ref, v_ref, gain_ref, shift_ref, out_ref, pooled_ref):
        unit, _ = norm_parts(x_ref[0].astype(F32))
        normed = (unit * gain_ref[...] + shift_ref[...]).astype(BF16)
        out_ref[0, :, :width] = dot(normed, q_ref[...]).astype(BF16)
        for k, ref in enumerate((k_ref, v_ref)):
            product = dot(normed, ref[...])
            out_ref[0, :, (k + 1) * width : (k + 2) * width] = product.astype(BF16)
            for j in range(2):
                mean = jnp.sum(product[j * half : (j + 1) * half], 0, keepdims=True) / half
                pooled_ref[0, j : j + 1, k * width : (k + 1) * width] = mean.astype(BF16)

    shapes = [(count, rows, 3 * width), (count, 2, 2 * width)]
    return pl.pallas_call(
        kernel,
        grid=(count,),
        in_specs=[each(inputs.shape)] + [full((width, width))] * 3 + [full((1, width))] * 2,
        out_specs=[each(shape) for shape in shapes],
        out_shape=[jax.ShapeDtypeStruct(shape, BF16) for shape in shapes],
    )(inputs, w_query, w_key, w_value, gain, shift)


def head_mask(rows, lane_half):
    lane = lax.broadcasted_iota(jnp.int32, (rows, 2 * HEAD), 1)
    return (lane < HEAD) if lane_half == 0 else (lane >= HEAD)


def only(array, lane_half):
    return jnp.where(head_mask(array.shape[0], lane_half), array, jnp.zeros_like(array))


def scores_of(keys, query, visible, rows):
    scores = dot(keys, query, 1, 1) * HEAD ** (-0.5)
    far = jnp.where(visible > 0, scores[rows:], -1e30)
    return jnp.concatenate([scores[:rows], far], 0)


def attend(qkv, summaries, visible, inputs, w_out, bias_out):
    count, rows, width = inputs.shape
    far = summaries.shape[1]

    def kernel(qkv_ref, sum_ref, vis_ref, x_ref, w_ref, bias_ref, mixed_ref, lse_ref, middle_ref):
        seen = vis_ref[...]
        for pair in range(HEADS // 2):
            at = pair * 2 * HEAD
            query = qkv_ref[0, :, at : at + 2 * HEAD]
            keys = jnp.concatenate(
                [
                    qkv_ref[0, :, width + at : width + at + 2 * HEAD],
                    sum_ref[0, :, at : at + 2 * HEAD],
                ],
                0,
            )
            values = jnp.concatenate(
                [
                    qkv_ref[0, :, 2 * width + at : 2 * width + at + 2 * HEAD],
                    sum_ref[0, :, width + at : width + at + 2 * HEAD],
                ],
                0,
            )
            total = None
            for side in range(2):
                scores = scores_of(keys, only(query, side), seen, rows)
                top = jnp.max(scores, 0, keepdims=True)
                powers = jnp.exp(scores - top)
                mass = jnp.sum(powers, 0, keepdims=True)
                head = 2 * pair + side
                lse_ref[0, head : head + 1, :] = top + jnp.log(mass)
                probs = (powers * (1.0 / mass)).astype(BF16)
                part = dot(only(values, side), probs, 0, 0)
                total = part if total is None else total + part
            mixed_ref[0, :, at : at + 2 * HEAD] = total.T.astype(BF16)
        branch = dot(mixed_ref[0], w_ref[...]) + bias_ref[...]
        middle_ref[0] = x_ref[0].astype(F32) + branch

    return pl.pallas_call(
        kernel,
        grid=(count,),
        in_specs=[
            each(qkv.shape),
            each(summaries.shape),
            full((far, rows)),
            each(inputs.shape),
            full((width, width)),
            full((1, width)),
        ],
        out_specs=[each(inputs.shape), each((count, HEADS, rows)), each(inputs.shape)],
        out_shape=[
            jax.ShapeDtypeStruct(inputs.shape, BF16),
            jax.ShapeDtypeStruct((count, HEADS, rows), F32),
            jax.ShapeDtypeStruct(inputs.shape, F32),
        ],
    )(qkv, summaries, visible, inputs, w_out, bias_out)


def split_rows(total):
    high = total.astype(BF16).astype(F32)
    return high, total - high


def vector_block(narrow, wide, per):
    def block(s):
        left = pl.multiple_of(s * per // 128 * 128, 128)
        found = narrow[:, pl.ds(left, 128)]
        if wide is not None:
            step = wide.shape[1] // narrow.shape[1] * per
            for k in range(step // 128):
                chunk = wide[:, pl.ds(pl.multiple_of(s * step + k * 128, 128), 128)]
                row = lax.broadcasted_iota(jnp.int32, chunk.shape, 0)
                keep = (row % (VEC_ROWS // 2)) == 4 + k
                found = found + jnp.where(keep, chunk, 0.0)
        return found.astype(BF16)

    return block


def feed(
    middle, cotangent, mixed, w_out, w_up, w_down, gain, shift, bias_up, bias_down, shards, tiles
):
    count, rows, width = middle.shape
    hidden_width = w_up.shape[1]
    step = 512
    grads = [(width, width), (width, hidden_width), (hidden_width, width)]
    segments = columns(shards) + [("vec", VEC_ROWS)]
    targets = spots(shards)
    orders = pack_order() if tiles else None
    half = sum(size for _, size in segments) // 2
    per = width // lax.axis_size("seq")

    def kernel(spot, middle_ref, cot_ref, mixed_ref, wo_ref, wu_ref, wd_ref, gain_ref, shift_ref,
               bu_ref, bd_ref, out_ref, mgrad_ref, xgrad_ref, narrow_ref, wide_ref, *rest):
        if tiles:
            packs, (go_ref, gu_ref, gd_ref, high_ref, long_ref) = rest[:2], rest[2:]
        else:
            go_ref, gu_ref, gd_ref = rest
        step_id = pl.program_id(0)

        @pl.when(step_id == 0)
        def _():
            for ref in (go_ref, gu_ref, gd_ref, narrow_ref, wide_ref):
                ref[...] = jnp.zeros_like(ref)

        middle = middle_ref[0]
        cot = cot_ref[0]
        tangent = cot.astype(BF16)
        unit, scale = norm_parts(middle)
        normed = (unit * gain_ref[...] + shift_ref[...]).astype(BF16)
        flipped = normed.T
        final = middle + bd_ref[...]
        back = None
        for at in range(0, hidden_width, step):
            here = slice(at, at + step)
            hidden = dot(normed, wu_ref[:, here]) + bu_ref[:, here]
            active, slope = gelu_pair(hidden)
            active = active.astype(BF16)
            final = final + dot(active, wd_ref[here, :])
            gd_ref[here, :] += dot(active, tangent, 0, 0)
            grad = (dot(tangent, wd_ref[here, :], 1, 1) * slope).astype(BF16)
            gu_ref[:, here] += dot(flipped, grad)
            wide_ref[0:1, here] += jnp.sum(grad.astype(F32), 0, keepdims=True)
            part = dot(grad, wu_ref[:, here], 1, 1)
            back = part if back is None else back + part
        out_ref[0] = final.astype(BF16)
        narrow_ref[0:1, :] += jnp.sum(back * unit, 0, keepdims=True)
        narrow_ref[1:2, :] += jnp.sum(back, 0, keepdims=True)
        middle_grad = cot + norm_back(back, unit, scale, gain_ref[...])
        mgrad_ref[0] = middle_grad
        branch = middle_grad.astype(BF16)
        narrow_ref[2:3, :] += jnp.sum(branch.astype(F32), 0, keepdims=True)
        narrow_ref[3:4, :] += jnp.sum(tangent.astype(F32), 0, keepdims=True)
        go_ref[...] += dot(mixed_ref[0], branch, 0, 0)
        xgrad_ref[0] = dot(branch, wo_ref[...], 1, 1).astype(BF16)

        if tiles:

            @pl.when(step_id == count - 1)
            def _():
                for ref, source, k in ((high_ref, narrow_ref, 8), (long_ref, wide_ref, 1)):
                    high, low = split_rows(source[...])
                    zero = jnp.zeros((8, source.shape[1]), F32)
                    if k == 1:
                        high = jnp.broadcast_to(high[0:1], zero.shape)
                        low = jnp.broadcast_to(low[0:1], zero.shape)
                    ref[...] = jnp.concatenate([high, zero, low, zero], 0)
                write_packed(
                    spot,
                    (go_ref, gu_ref, gd_ref),
                    vector_block(high_ref, long_ref, per),
                    packs,
                    segments,
                    targets,
                    orders,
                )

    block = middle.shape
    out_shape = [
        jax.ShapeDtypeStruct(block, BF16),
        jax.ShapeDtypeStruct(block, F32),
        jax.ShapeDtypeStruct(block, BF16),
        jax.ShapeDtypeStruct((8, width), F32),
        jax.ShapeDtypeStruct((8, hidden_width), F32),
    ]
    out_specs = [each(block)] * 3 + [full((8, width)), full((8, hidden_width))]
    scratch = []
    if tiles:
        out_shape += [jax.ShapeDtypeStruct((len(names), half, 128), BF16) for names in orders]
        out_specs += [full((len(names), half, 128)) for names in orders]
        scratch = [pltpu.VMEM(shape, F32) for shape in grads]
        scratch += [pltpu.VMEM((VEC_ROWS, width), F32), pltpu.VMEM((VEC_ROWS, hidden_width), F32)]
    else:
        out_shape += [jax.ShapeDtypeStruct(shape, F32) for shape in grads]
        out_specs += [full(shape) for shape in grads]
    return pl.pallas_call(
        kernel,
        grid=(count,),
        in_specs=[pl.BlockSpec(memory_space=pltpu.SMEM)]
        + [each(block)] * 3
        + [full(shape) for shape in ((width, width), (width, hidden_width), (hidden_width, width))]
        + [full((1, width)), full((1, width)), full((1, hidden_width)), full((1, width))],
        out_specs=out_specs,
        out_shape=out_shape,
        scratch_shapes=scratch,
    )(
        place(), middle, cotangent, mixed, w_out, w_up, w_down, gain, shift, bias_up, bias_down
    )


def attend_back(qkv, summaries, visible, lse, mixed_grad):
    count, rows, width = mixed_grad.shape
    far = summaries.shape[1]

    def kernel(qkv_ref, sum_ref, vis_ref, lse_ref, grad_ref, dq_ref, dk_ref, dv_ref, far_ref):
        seen = vis_ref[...]
        for pair in range(HEADS // 2):
            at = pair * 2 * HEAD
            lanes = slice(at, at + 2 * HEAD)
            query = qkv_ref[0, :, lanes]
            pull = grad_ref[0, :, lanes]
            keys = jnp.concatenate(
                [qkv_ref[0, :, width + at : width + at + 2 * HEAD], sum_ref[0, :, lanes]], 0
            )
            values = jnp.concatenate(
                [
                    qkv_ref[0, :, 2 * width + at : 2 * width + at + 2 * HEAD],
                    sum_ref[0, :, width + at : width + at + 2 * HEAD],
                ],
                0,
            )
            d_query = d_keys = d_values = 0.0
            for side in range(2):
                head = 2 * pair + side
                own = only(query, side)
                own_pull = only(pull, side)
                scores = scores_of(keys, own, seen, rows)
                probs = jnp.exp(scores - lse_ref[0, head : head + 1, :])
                dots = dot(values, own_pull, 1, 1)
                centre = jnp.sum(probs * dots, 0, keepdims=True)
                slope = (probs * (dots - centre)).astype(BF16)
                d_values = d_values + dot(probs.astype(BF16), own_pull)
                d_keys = d_keys + dot(slope, own)
                d_query = d_query + dot(only(keys, side), slope, 0, 0)
            d_keys = d_keys * HEAD ** (-0.5)
            dq_ref[0, :, lanes] = (d_query * HEAD ** (-0.5)).T.astype(BF16)
            dk_ref[0, :, lanes] = d_keys[:rows]
            dv_ref[0, :, lanes] = d_values[:rows]
            far_ref[0, :, lanes] = d_keys[rows:].astype(BF16)
            far_ref[0, :, width + at : width + at + 2 * HEAD] = d_values[rows:].astype(BF16)

    block = mixed_grad.shape
    return pl.pallas_call(
        kernel,
        grid=(count,),
        in_specs=[
            each(qkv.shape),
            each(summaries.shape),
            full((far, rows)),
            each(lse.shape),
            each(block),
        ],
        out_specs=[each(block)] * 3 + [each(summaries.shape)],
        out_shape=[
            jax.ShapeDtypeStruct(block, BF16),
            jax.ShapeDtypeStruct(block, F32),
            jax.ShapeDtypeStruct(block, F32),
            jax.ShapeDtypeStruct(summaries.shape, BF16),
        ],
    )(qkv, summaries, visible, lse, mixed_grad)


def project_back(
    inputs, d_query, d_keys, d_values, owned, weights, gain, shift, middle_grad, shards, tiles
):
    count, rows, width = inputs.shape
    half_span = rows // 2
    segments = columns(shards) + [("vec", VEC_ROWS)]
    targets = spots(shards)
    orders = pack_order() if tiles else None
    half = sum(size for _, size in segments) // 2
    per = width // lax.axis_size("seq")

    def kernel(spot, x_ref, dq_ref, dk_ref, dv_ref, own_ref, wq_ref, wk_ref, wv_ref, gain_ref,
               shift_ref, mgrad_ref, igrad_ref, narrow_ref, *rest):
        if tiles:
            packs, (gq_ref, gk_ref, gv_ref, high_ref) = rest[:2], rest[2:]
        else:
            gq_ref, gk_ref, gv_ref = rest
        step_id = pl.program_id(0)

        @pl.when(step_id == 0)
        def _():
            for ref in (gq_ref, gk_ref, gv_ref, narrow_ref):
                ref[...] = jnp.zeros_like(ref)

        unit, scale = norm_parts(x_ref[0].astype(F32))
        flipped = (unit * gain_ref[...] + shift_ref[...]).astype(BF16).T
        back = dot(dq_ref[0], wq_ref[...], 1, 1)
        gq_ref[...] += dot(flipped, dq_ref[0])
        for k, (direct, w_ref, g_ref) in enumerate(
            ((dk_ref, wk_ref, gk_ref), (dv_ref, wv_ref, gv_ref))
        ):
            act = jnp.concatenate(
                [
                    direct[0, j * half_span : (j + 1) * half_span, :]
                    + own_ref[0, j : j + 1, k * width : (k + 1) * width] / half_span
                    for j in range(2)
                ],
                0,
            ).astype(BF16)
            g_ref[...] += dot(flipped, act)
            back = back + dot(act, w_ref[...], 1, 1)
        narrow_ref[0:1, :] += jnp.sum(back * unit, 0, keepdims=True)
        narrow_ref[1:2, :] += jnp.sum(back, 0, keepdims=True)
        igrad_ref[0] = mgrad_ref[0] + norm_back(back, unit, scale, gain_ref[...])

        if tiles:

            @pl.when(step_id == count - 1)
            def _():
                high, low = split_rows(narrow_ref[...])
                zero = jnp.zeros_like(high)
                high_ref[...] = jnp.concatenate([high, zero, low, zero], 0)
                write_packed(
                    spot,
                    (gq_ref, gk_ref, gv_ref),
                    vector_block(high_ref, None, per),
                    packs,
                    segments,
                    targets,
                    orders,
                )

    block = inputs.shape
    square = (width, width)
    out_shape = [jax.ShapeDtypeStruct(block, F32), jax.ShapeDtypeStruct((8, width), F32)]
    out_specs = [each(block), full((8, width))]
    scratch = []
    if tiles:
        out_shape += [jax.ShapeDtypeStruct((len(names), half, 128), BF16) for names in orders]
        out_specs += [full((len(names), half, 128)) for names in orders]
        scratch = [pltpu.VMEM(square, F32)] * 3 + [pltpu.VMEM((VEC_ROWS, width), F32)]
    else:
        out_shape += [jax.ShapeDtypeStruct(square, F32)] * 3
        out_specs += [full(square)] * 3
    return pl.pallas_call(
        kernel,
        grid=(count,),
        in_specs=[pl.BlockSpec(memory_space=pltpu.SMEM)]
        + [each(block)] * 4
        + [each(owned.shape)]
        + [full(square)] * 3
        + [full((1, width))] * 2
        + [each(block)],
        out_specs=out_specs,
        out_shape=out_shape,
        scratch_shapes=scratch,
    )(place(), inputs, d_query, d_keys, d_values, owned, *weights, gain, shift, middle_grad)


def local(
    inputs,
    cotangent,
    query_weight,
    key_weight,
    value_weight,
    out_weight,
    up_weight,
    down_weight,
    norm1_gain,
    norm1_bias,
    norm2_gain,
    norm2_bias,
    out_bias,
    up_bias,
    down_bias,
):
    shards = [query_weight, key_weight, value_weight, out_weight, up_weight, down_weight]
    slices = [norm1_gain, norm1_bias, norm2_gain, norm2_bias, out_bias, up_bias, down_bias]
    tiles = whole_tiles(shards, slices)
    wide, gathered = gather_weights(shards, slices)
    w_query, w_key, w_value, w_out, w_up, w_down = wide
    gain_one, bias_one, gain_two, bias_two, bias_out, bias_up, bias_down = [
        member.astype(F32)[None] for member in gathered
    ]
    count, rows, width = inputs.shape
    qkv, pooled = project(inputs, w_query, w_key, w_value, gain_one, bias_one)
    summaries = jnp.transpose(gather_seq(pooled), (1, 0, 2, 3)).reshape(count, -1, 2 * width)
    here = lax.axis_index("seq")
    marks = jnp.array([s for s, _ in relative_ids(seq_stages())], jnp.int32)
    visible = jnp.repeat((marks ^ here) < here, 2).astype(F32)
    visible = jnp.broadcast_to(visible[:, None], (visible.shape[0], rows))
    mixed, lse, middle = attend(qkv, summaries, visible, inputs, w_out, bias_out)
    outputs, middle_grad, mixed_grad, narrow_two, wide_two, *second = feed(
        middle,
        cotangent,
        mixed,
        w_out,
        w_up,
        w_down,
        gain_two,
        bias_two,
        bias_up,
        bias_down,
        shards[3:],
        tiles,
    )
    d_query, d_keys, d_values, terms = attend_back(qkv, summaries, visible, lse, mixed_grad)
    terms = jnp.transpose(terms.reshape(count, -1, 2, 2 * width), (1, 0, 2, 3))
    owned = reduce_seq(terms)
    input_grad, narrow_one, *first = project_back(
        inputs,
        d_query,
        d_keys,
        d_values,
        owned,
        (w_query, w_key, w_value),
        gain_one,
        bias_one,
        middle_grad,
        shards[:3],
        tiles,
    )
    if tiles:
        size = norm1_gain.shape[0]
        tail = reduce_group(shards[3:], second, [size] * 4 + [up_bias.shape[0]])
        front = reduce_group(shards[:3], first, [size] * 2)
        matrices = front[:3] + tail[:3]
        vectors = front[3:] + tail[3:6] + [tail[7], tail[6]]
    else:
        vectors = [
            narrow_one[0],
            narrow_one[1],
            narrow_two[0],
            narrow_two[1],
            narrow_two[2],
            wide_two[0],
            narrow_two[3],
        ]
        reduced = reduce_plain(shards, list(first) + list(second), vectors)
        matrices, vectors = reduced[:6], reduced[6:]
    return (outputs, input_grad, *matrices, *vectors)


def solution(mesh):
    placed = (
        P("batch", "seq", None),
        P("batch", "seq", None),
        P("seq", "batch"),
        P("seq", "batch"),
        P("seq", "batch"),
        P("seq", "batch"),
        P("seq", "batch"),
        P("seq", "batch"),
        P("seq"),
        P("seq"),
        P("seq"),
        P("seq"),
        P("seq"),
        P("seq"),
        P("seq"),
    )
    return jax.shard_map(
        local,
        mesh=mesh,
        in_specs=placed,
        out_specs=(
            P("batch", "seq", None),
            P("batch", "seq", None),
            P("seq", "batch"),
            P("seq", "batch"),
            P("seq", "batch"),
            P("seq", "batch"),
            P("seq", "batch"),
            P("seq", "batch"),
            P("seq"),
            P("seq"),
            P("seq"),
            P("seq"),
            P("seq"),
            P("seq"),
            P("seq"),
        ),
        check_vma=False,
    )
```

profile of v0, /device:TPU:0, one launch (start us, length us, event | category | flops | bytes accessed | tf_op | source)
XLA Modules:
  0.0 258.5 jit_solution(16958275508965354864)
XLA Ops:
  0.7 4.8 %concatenate.85 = bf16[640]{0:T(1024)(128)(2,1)S(1)} concatenate(bf16[64]{0:T(256)(128)(2,1)} %param.24, bf16[64]{0:T(256)(128)(2,1)} %param.25, bf16[64]{0:T(256)(128)(2,1)} %param.26, bf16[64]{0:T(256)(128)(2,1)} %param.27, bf16[64]{0:T(256)(128)(2,1)} %param.28, bf16[256]{0:T(256)(128)(2,1)} %param.29, bf16[64]{0:T(256)(128)(2,1)} %param.30), dimensions={0} | concatenate | bytes 2560 | tf_op jit(solution)/shard_map/concatenate | solution.py:236
  6.2 4.1 %collective-permute-start = (bf16[1,224,128]{2,1,0:T(8,128)(2,1)S(1)}, bf16[1,224,128]{2,1,0:T(8,128)(2,1)S(1)}, u32[]{:S(2)}, u32[]{:S(2)}) collective-permute-start(bf16[1,224,128]{2,1,0:T(8,128)(2,1)S(1)} %fusion.7), channel_id=1, source_target_pairs={{0,4},{1,5},{2,6},{3,7},{4,0},{5,1},{6,2},{7,3},{8,12},{9,13},{10,... | collective-permute-start | bytes 172040 | tf_op jit(solution)/shard_map/ppermute | solution.py:17
  10.3 2.8 %collective-permute-done = bf16[1,224,128]{2,1,0:T(8,128)(2,1)S(1)} collective-permute-done((bf16[1,224,128]{2,1,0:T(8,128)(2,1)S(1)}, bf16[1,224,128]{2,1,0:T(8,128)(2,1)S(1)}, u32[]{:S(2)}, u32[]{:S(2)}) %collective-permute-start) | collective-permute-done | bytes 57376 | tf_op jit(solution)/shard_map/ppermute | solution.py:17
  15.1 2.8 %collective-permute-done.1 = bf16[2,224,128]{2,1,0:T(8,128)(2,1)S(1)} collective-permute-done((bf16[2,224,128]{2,1,0:T(8,128)(2,1)S(1)}, bf16[2,224,128]{2,1,0:T(8,128)(2,1)S(1)}, u32[]{:S(2)}, u32[]{:S(2)}) %collective-permute-start.1) | collective-permute-done | bytes 114720 | tf_op jit(solution)/shard_map/ppermute | solution.py:17
  18.0 1.8 collective-permute-start.6
  19.8 3.0 %collective-permute-done.6 = bf16[4,112,128]{2,1,0:T(8,128)(2,1)S(1)} collective-permute-done((bf16[4,112,128]{2,1,0:T(8,128)(2,1)S(1)}, bf16[4,112,128]{2,1,0:T(8,128)(2,1)S(1)}, u32[]{:S(2)}, u32[]{:S(2)}) %collective-permute-start.6) | collective-permute-done | bytes 114720 | tf_op jit(solution)/shard_map/ppermute | solution.py:17
  22.9 1.8 collective-permute-start.8
  24.7 4.3 %collective-permute-done.8.refs_6_ = bf16[8,112,128]{2,1,0:T(8,128)(2,1)S(1)} collective-permute-done((bf16[8,112,128]{2,1,0:T(8,128)(2,1)S(1)}, bf16[8,112,128]{2,1,0:T(8,128)(2,1)S(1)}, u32[]{:S(2)}, u32[]{:S(2)}) %collective-permute-start.8) | collective-permute-done | bytes 229408 | tf_op jit(solution)/shard_map/ppermute | solution.py:17
  30.5 2.5 collective-permute-start.13
  32.9 7.5 %collective-permute-done.13 = bf16[1,576,128]{2,1,0:T(8,128)(2,1)S(1)} collective-permute-done((bf16[1,576,128]{2,1,0:T(8,128)(2,1)S(1)}, bf16[1,576,128]{2,1,0:T(8,128)(2,1)S(1)}, u32[]{:S(2)}, u32[]{:S(2)}) %collective-permute-start.13) | collective-permute-done | bytes 147488 | tf_op jit(solution)/shard_map/ppermute | solution.py:17
  41.0 7.7 %collective-permute-done.14 = bf16[2,576,128]{2,1,0:T(8,128)(2,1)S(1)} collective-permute-done((bf16[2,576,128]{2,1,0:T(8,128)(2,1)S(1)}, bf16[2,576,128]{2,1,0:T(8,128)(2,1)S(1)}, u32[]{:S(2)}, u32[]{:S(2)}) %collective-permute-start.14) | collective-permute-done | bytes 294944 | tf_op jit(solution)/shard_map/ppermute | solution.py:17
  48.8 1.8 collective-permute-start.15
  50.9 1.7 collective-permute-start.19
  52.7 6.0 %collective-permute-done.2 = bf16[4,112,128]{2,1,0:T(8,128)(2,1)S(1)} collective-permute-done((bf16[4,112,128]{2,1,0:T(8,128)(2,1)S(1)}, bf16[4,112,128]{2,1,0:T(8,128)(2,1)S(1)}, u32[]{:S(2)}, u32[]{:S(2)}) %collective-permute-start.2) | collective-permute-done | bytes 114720 | tf_op jit(solution)/shard_map/ppermute | solution.py:17
  58.7 1.8 collective-permute-start.4
  61.0 1.8 collective-permute-start.21
  63.3 3.9 %collective-permute-done.4.refs_2_ = bf16[8,112,128]{2,1,0:T(8,128)(2,1)S(1)} collective-permute-done((bf16[8,112,128]{2,1,0:T(8,128)(2,1)S(1)}, bf16[8,112,128]{2,1,0:T(8,128)(2,1)S(1)}, u32[]{:S(2)}, u32[]{:S(2)}) %collective-permute-start.4) | collective-permute-done | bytes 229408 | tf_op jit(solution)/shard_map/ppermute | solution.py:17
  68.9 3.1 %shard_map.271 = (bf16[512,512]{1,0:T(8,128)(2,1)}, bf16[512,512]{1,0:T(8,128)(2,1)}, bf16[512,512]{1,0:T(8,128)(2,1)}, bf16[256,128]{1,0:T(8,128)(2,1)}) custom-call(s32[2]{0:T(128)} %pad_add_fusion.spot, bf16[8,112,128]{2,1,0:T(8,128)(2,1)} %copy-done.7, bf16[8,112,128]{2,1,0:T(8,128)(2,1)} %copy-done.14, bf16[8,112,128]{2,1,0:T(8,128)(2,1)} %copy-done.13, ...), custom_call_target="tpu_custom_call" | custom-call | tf_op jit(solution)/shard_map/pallas_call | solution.py:95
  74.2 6.0 %shard_map.272 = (bf16[4,256,1536]{2,1,0:T(8,128)(2,1)}, bf16[4,2,1024]{2,1,0:T(2,128)(2,1)}) custom-call(bf16[4,256,512]{2,1,0:T(8,128)(2,1)} %x_ref.5, bf16[512,512]{1,0:T(8,128)(2,1)} %get-tuple-element.40.q_ref.wq_ref, bf16[512,512]{1,0:T(8,128)(2,1)} %get-tuple-element.41.k_ref.wk_ref, bf16[512,512]{1,0:T(8,128)(2,1)} %get-tuple-element.42.v_ref.wv_ref, ...), custom_call_target="tpu_custom_call" | custom-call | tf_op jit(solution)/shard_map/pallas_call | solution.py:348
  80.2 3.9 %collective-permute-start.10 = (bf16[1,4,2,1024]{3,2,1,0:T(2,128)(2,1)}, bf16[1,4,2,1024]{3,2,1,0:T(2,128)(2,1)S(1)}, u32[]{:S(2)}, u32[]{:S(2)}) collective-permute-start(bf16[1,4,2,1024]{3,2,1,0:T(2,128)(2,1)} %bitcast.61), channel_id=1, source_target_pairs={{0,4},{1,5},{2,6},{3,7},{4,0},{5,1},{6,2},{7,3},{8,12},{9,13},{10,... | collective-permute-start | bytes 49160 | tf_op jit(solution)/shard_map/ppermute | solution.py:17
  84.1 1.9 collective-permute-done.10
  99.1 5.5 %shard_map.273 = (bf16[512,512]{1,0:T(8,128)(2,1)}, bf16[512,2048]{1,0:T(8,128)(2,1)}, bf16[2048,512]{1,0:T(8,128)(2,1)}) custom-call(s32[2]{0:T(128)} %pad_add_fusion.spot, bf16[8,288,128]{2,1,0:T(8,128)(2,1)} %copy-done.2, bf16[8,288,128]{2,1,0:T(8,128)(2,1)} %copy-done.10, bf16[8,288,128]{2,1,0:T(8,128)(2,1)} %copy-done.8, ...), custom_call_target="tpu_custom_call" | custom-call | tf_op jit(solution)/shard_map/pallas_call | solution.py:95
  105.3 8.9 %shard_map.274 = (bf16[4,256,512]{2,1,0:T(8,128)(2,1)}, f32[4,8,256]{2,1,0:T(8,128)}, f32[4,256,512]{2,1,0:T(8,128)}) custom-call(bf16[4,256,1536]{2,1,0:T(8,128)(2,1)} %get-tuple-element.44.qkv_ref, bf16[4,16,1024]{2,1,0:T(8,128)(2,1)} %reshape.174.sum_ref, f32[16,256]{1,0:T(8,128)} %broadcast_in_dim.13.vis_ref, bf16[4,256,512]{2,1,0:T(8,128)(2,1)} %x_ref.5, ...), custom_call_target="tpu_custom_call" | custom-call | tf_op jit(solution)/shard_map/pallas_call | solution.py:410
  114.1 33.6 %shard_map.275 = (bf16[4,256,512]{2,1,0:T(8,128)(2,1)}, f32[4,256,512]{2,1,0:T(8,128)}, bf16[4,256,512]{2,1,0:T(8,128)(2,1)}, f32[8,512]{1,0:T(8,128)}, f32[8,20...) custom-call(s32[2]{0:T(128)} %pad_add_fusion.spot, ...), custom_call_target="tpu_custom_call" | custom-call | tf_op jit(solution)/shard_map/pallas_call | solution.py:547
  147.7 12.0 %shard_map.276 = (bf16[4,256,512]{2,1,0:T(8,128)(2,1)}, f32[4,256,512]{2,1,0:T(8,128)}, f32[4,256,512]{2,1,0:T(8,128)}, bf16[4,16,1024]{2,1,0:T(8,128)(2,1)}) custom-call(bf16[4,256,1536]{2,1,0:T(8,128)(2,1)} %get-tuple-element.44.qkv_ref, bf16[4,16,1024]{2,1,0:T(8,128)(2,1)} %reshape.174.sum_ref, f32[16,256]{1,0:T(8,128)} %broadcast_in_dim.13.vis_ref, ...), custom_call_target="tpu_custom_call" | custom-call | tf_op jit(solution)/shard_map/pallas_call | solution.py:604
  162.0 3.2 %collective-permute-done.23 = bf16[4,4,2,1024]{3,2,1,0:T(2,128)(2,1)S(1)} collective-permute-done((bf16[4,4,2,1024]{3,2,1,0:T(2,128)(2,1)S(1)}, bf16[4,4,2,1024]{3,2,1,0:T(2,128)(2,1)S(1)}, u32[]{:S(2)}, u32[]{:S(2)}) %collective-permute-start.23) | collective-permute-done | bytes 65568 | tf_op jit(solution)/shard_map/ppermute | solution.py:17
  166.9 2.4 collective-permute-done.24
  169.4 3.0 %collective-permute-start.25 = (bf16[1,4,2,1024]{3,2,1,0:T(2,128)(2,1)S(1)}, bf16[1,4,2,1024]{3,2,1,0:T(2,128)(2,1)S(1)}, u32[]{:S(2)}, u32[]{:S(2)}) collective-permute-start(bf16[1,4,2,1024]{3,2,1,0:T(2,128)(2,1)S(1)} %slice.629), channel_id=1, source_target_pairs={{0,4},{1,5},{2,6},{3,7},{4,0},{5,1},{6,2},{7,3},{8,12},{9,13},{10,... | collective-permute-start | bytes 49160 | tf_op jit(solution)/shard_map/ppermute | solution.py:17
  172.4 1.7 collective-permute-done.25
  174.7 10.6 %shard_map.277 = (f32[4,256,512]{2,1,0:T(8,128)}, f32[8,512]{1,0:T(8,128)}, bf16[32,112,128]{2,1,0:T(8,128)(2,1)}, bf16[32,112,128]{2,1,0:T(8,128)(2,1)}) custom-call(s32[2]{0:T(128)} %pad_add_fusion.spot, bf16[4,256,512]{2,1,0:T(8,128)(2,1)} %x_ref.5, bf16[4,256,512]{2,1,0:T(8,128)(2,1)} %get-tuple-element.55.dq_ref, ...), custom_call_target="tpu_custom_call" | custom-call | tf_op jit(solution)/shard_map/pallas_call | solution.py:698
  191.2 2.6 %collective-permute-done.26 = bf16[16,112,128]{2,1,0:T(8,128)(2,1)S(1)} collective-permute-done((bf16[16,112,128]{2,1,0:T(8,128)(2,1)S(1)}, bf16[16,112,128]{2,1,0:T(8,128)(2,1)S(1)}, u32[]{:S(2)}, u32[]{:S(2)}) %collective-permute-start.26) | collective-permute-done | bytes 458784 | tf_op jit(solution)/shard_map/ppermute | solution.py:17
  194.0 1.7 collective-permute-start.27
  195.6 2.2 collective-permute-done.32
  199.6 2.9 %collective-permute-done.27 = bf16[8,112,128]{2,1,0:T(8,128)(2,1)S(1)} collective-permute-done((bf16[8,112,128]{2,1,0:T(8,128)(2,1)S(1)}, bf16[8,112,128]{2,1,0:T(8,128)(2,1)S(1)}, u32[]{:S(2)}, u32[]{:S(2)}) %collective-permute-start.27) | collective-permute-done | bytes 229408 | tf_op jit(solution)/shard_map/ppermute | solution.py:17
  204.5 1.7 collective-permute-start.34
  207.5 1.7 collective-permute-start.29
  209.4 3.0 %collective-permute-start.35 = (bf16[1,112,128]{2,1,0:T(8,128)(2,1)S(1)}, bf16[1,112,128]{2,1,0:T(8,128)(2,1)S(1)}, u32[]{:S(2)}, u32[]{:S(2)}) collective-permute-start(bf16[1,112,128]{2,1,0:T(8,128)(2,1)S(1)} %pad_maximum_fusion.26), channel_id=1, source_target_pairs={{0,4},{1,5},{2,6},{3,7},{4,0},{5,1},{6,2},{7,3},{8,12},{9,13},{10,... | collective-permute-start | bytes 86024 | tf_op jit(solution)/shard_map/ppermute | solution.py:17
  212.4 2.4 collective-permute-start.30
  215.4 1.8 collective-permute-done.30
  220.3 1.7 collective-permute-start.37
  222.0 8.7 %collective-permute-done.42 = bf16[8,304,128]{2,1,0:T(8,128)(2,1)S(1)} collective-permute-done((bf16[8,304,128]{2,1,0:T(8,128)(2,1)S(1)}, bf16[8,304,128]{2,1,0:T(8,128)(2,1)S(1)}, u32[]{:S(2)}, u32[]{:S(2)}) %collective-permute-start.42) | collective-permute-done | bytes 622624 | tf_op jit(solution)/shard_map/ppermute | solution.py:17
  230.9 1.7 collective-permute-start.43
  233.2 3.3 %collective-permute-done.37 = bf16[8,304,128]{2,1,0:T(8,128)(2,1)S(1)} collective-permute-done((bf16[8,304,128]{2,1,0:T(8,128)(2,1)S(1)}, bf16[8,304,128]{2,1,0:T(8,128)(2,1)S(1)}, u32[]{:S(2)}, u32[]{:S(2)}) %collective-permute-start.37) | collective-permute-done | bytes 622624 | tf_op jit(solution)/shard_map/ppermute | solution.py:17
  237.7 2.1 collective-permute-done.43
  239.9 1.8 collective-permute-start.44
  241.8 1.9 collective-permute-done.38
  247.5 2.2 collective-permute-done.39
  252.9 3.1 %collective-permute-done.40 = bf16[1,304,128]{2,1,0:T(8,128)(2,1)S(1)} collective-permute-done((bf16[1,304,128]{2,1,0:T(8,128)(2,1)S(1)}, bf16[1,304,128]{2,1,0:T(8,128)(2,1)S(1)}, u32[]{:S(2)}, u32[]{:S(2)}) %collective-permute-start.40) | collective-permute-done | bytes 77856 | tf_op jit(solution)/shard_map/ppermute | solution.py:17
  (199 shorter events, 55.0 us)
Async XLA Ops:
  0.7 28.3 %copy-start.17 = (bf16[256,128]{1,0:T(8,128)(2,1)S(1)}, bf16[256,128]{1,0:T(8,128)(2,1)}, u32[]{:S(2)}) copy-start(bf16[256,128]{1,0:T(8,128)(2,1)} %param.23) | copy-start | bytes 196612
  6.2 6.8 %collective-permute-start = (bf16[1,224,128]{2,1,0:T(8,128)(2,1)S(1)}, bf16[1,224,128]{2,1,0:T(8,128)(2,1)S(1)}, u32[]{:S(2)}, u32[]{:S(2)}) collective-permute-start(bf16[1,224,128]{2,1,0:T(8,128)(2,1)S(1)} %fusion.7), channel_id=1, source_target_pairs={{0,4},{1,5},{2,6},{3,7},{4,0},{5,1},{6,2},{7,3},{8,12},{9,13},{10,... | collective-permute-start | bytes 172040 | tf_op jit(solution)/shard_map/ppermute | solution.py:17
  13.1 4.9 %collective-permute-start.1 = (bf16[2,224,128]{2,1,0:T(8,128)(2,1)S(1)}, bf16[2,224,128]{2,1,0:T(8,128)(2,1)S(1)}, u32[]{:S(2)}, u32[]{:S(2)}) collective-permute-start(bf16[2,224,128]{2,1,0:T(8,128)(2,1)S(1)} %pad_maximum_fusion.18), channel_id=1, source_target_pairs={{0,2},{1,3},{2,0},{3,1},{4,6},{5,7},{6,4},{7,5},{8,10},{9,11},{10,... | collective-permute-start | bytes 344072 | tf_op jit(solution)/shard_map/ppermute | solution.py:17
  18.0 4.9 %collective-permute-start.6 = (bf16[4,112,128]{2,1,0:T(8,128)(2,1)S(1)}, bf16[4,112,128]{2,1,0:T(8,128)(2,1)S(1)}, u32[]{:S(2)}, u32[]{:S(2)}) collective-permute-start(bf16[4,112,128]{2,1,0:T(8,128)(2,1)S(1)} %get-tuple-element.79), channel_id=1, source_target_pairs={{0,1},{1,0},{2,3},{3,2},{4,5},{5,4},{6,7},{7,6},{8,9},{9,8},{10,11... | collective-permute-start | bytes 344072 | tf_op jit(solution)/shard_map/ppermute | solution.py:17
  22.9 39.9 %copy-start.6 = (bf16[8,112,128]{2,1,0:T(8,128)(2,1)}, bf16[8,112,128]{2,1,0:T(8,128)(2,1)S(1)}, u32[]{:S(2)}) copy-start(bf16[8,112,128]{2,1,0:T(8,128)(2,1)S(1)} %pad_maximum_fusion.12.refs_4_) | copy-start | bytes 688132
  22.9 6.1 %collective-permute-start.8 = (bf16[8,112,128]{2,1,0:T(8,128)(2,1)S(1)}, bf16[8,112,128]{2,1,0:T(8,128)(2,1)S(1)}, u32[]{:S(2)}, u32[]{:S(2)}) collective-permute-start(bf16[8,112,128]{2,1,0:T(8,128)(2,1)S(1)} %pad_maximum_fusion.12.refs_4_), channel_id=1, source_target_pairs={{0,16},{8,24},{16,0},{24,8},{1,17},{9,25},{17,1},{25,9},{2,18},{10... | collective-permute-start | bytes 688136 | tf_op jit(solution)/shard_map/ppermute | solution.py:17
  29.0 1.5 collective-permute-start.9
  30.5 9.9 %collective-permute-start.13 = (bf16[1,576,128]{2,1,0:T(8,128)(2,1)S(1)}, bf16[1,576,128]{2,1,0:T(8,128)(2,1)S(1)}, u32[]{:S(2)}, u32[]{:S(2)}) collective-permute-start(bf16[1,576,128]{2,1,0:T(8,128)(2,1)S(1)} %bitcast.55), channel_id=1, source_target_pairs={{0,4},{1,5},{2,6},{3,7},{4,0},{5,1},{6,2},{7,3},{8,12},{9,13},{10,... | collective-permute-start | bytes 442376 | tf_op jit(solution)/shard_map/ppermute | solution.py:17
  40.4 8.3 %collective-permute-start.14 = (bf16[2,576,128]{2,1,0:T(8,128)(2,1)S(1)}, bf16[2,576,128]{2,1,0:T(8,128)(2,1)S(1)}, u32[]{:S(2)}, u32[]{:S(2)}) collective-permute-start(bf16[2,576,128]{2,1,0:T(8,128)(2,1)S(1)} %pad_maximum_fusion.7), channel_id=1, source_target_pairs={{0,2},{1,3},{2,0},{3,1},{4,6},{5,7},{6,4},{7,5},{8,10},{9,11},{10,... | collective-permute-start | bytes 884744 | tf_op jit(solution)/shard_map/ppermute | solution.py:17
  48.8 11.7 %collective-permute-start.15 = (bf16[4,288,128]{2,1,0:T(8,128)(2,1)S(1)}, bf16[4,288,128]{2,1,0:T(8,128)(2,1)S(1)}, u32[]{:S(2)}, u32[]{:S(2)}) collective-permute-start(bf16[4,288,128]{2,1,0:T(8,128)(2,1)S(1)} %get-tuple-element.72), channel_id=1, source_target_pairs={{0,16},{8,24},{16,0},{24,8},{1,17},{9,25},{17,1},{25,9},{2,18},{10... | collective-permute-start | bytes 884744 | tf_op jit(solution)/shard_map/ppermute | solution.py:17
  50.6 8.1 %collective-permute-start.2 = (bf16[4,112,128]{2,1,0:T(8,128)(2,1)S(1)}, bf16[4,112,128]{2,1,0:T(8,128)(2,1)S(1)}, u32[]{:S(2)}, u32[]{:S(2)}) collective-permute-start(bf16[4,112,128]{2,1,0:T(8,128)(2,1)S(1)} %get-tuple-element.80), channel_id=1, source_target_pairs={{0,16},{8,24},{16,0},{24,8},{1,17},{9,25},{17,1},{25,9},{2,18},{10... | collective-permute-start | bytes 344072 | tf_op jit(solution)/shard_map/ppermute | solution.py:17
  50.9 10.0 %collective-permute-start.19 = (bf16[4,288,128]{2,1,0:T(8,128)(2,1)S(1)}, bf16[4,288,128]{2,1,0:T(8,128)(2,1)S(1)}, u32[]{:S(2)}, u32[]{:S(2)}) collective-permute-start(bf16[4,288,128]{2,1,0:T(8,128)(2,1)S(1)} %get-tuple-element.71), channel_id=1, source_target_pairs={{0,1},{1,0},{2,3},{3,2},{4,5},{5,4},{6,7},{7,6},{8,9},{9,8},{10,11... | collective-permute-start | bytes 884744 | tf_op jit(solution)/shard_map/ppermute | solution.py:17
  58.7 8.5 %collective-permute-start.4 = (bf16[8,112,128]{2,1,0:T(8,128)(2,1)S(1)}, bf16[8,112,128]{2,1,0:T(8,128)(2,1)S(1)}, u32[]{:S(2)}, u32[]{:S(2)}) collective-permute-start(bf16[8,112,128]{2,1,0:T(8,128)(2,1)S(1)} %pad_maximum_fusion.11.refs_0_), channel_id=1, source_target_pairs={{0,1},{1,0},{2,3},{3,2},{4,5},{5,4},{6,7},{7,6},{8,9},{9,8},{10,11... | collective-permute-start | bytes 688136 | tf_op jit(solution)/shard_map/ppermute | solution.py:17
  60.6 28.3 %collective-permute-start.17 = (bf16[8,288,128]{2,1,0:T(8,128)(2,1)S(1)}, bf16[8,288,128]{2,1,0:T(8,128)(2,1)S(1)}, u32[]{:S(2)}, u32[]{:S(2)}) collective-permute-start(bf16[8,288,128]{2,1,0:T(8,128)(2,1)S(1)} %pad_maximum_fusion.3.refs_0_), channel_id=1, source_target_pairs={{0,1},{1,0},{2,3},{3,2},{4,5},{5,4},{6,7},{7,6},{8,9},{9,8},{10,11... | collective-permute-start | bytes 1769480 | tf_op jit(solution)/shard_map/ppermute | solution.py:17
  61.0 28.0 %collective-permute-start.21 = (bf16[8,288,128]{2,1,0:T(8,128)(2,1)S(1)}, bf16[8,288,128]{2,1,0:T(8,128)(2,1)S(1)}, u32[]{:S(2)}, u32[]{:S(2)}) collective-permute-start(bf16[8,288,128]{2,1,0:T(8,128)(2,1)S(1)} %pad_maximum_fusion.4.refs_4_), channel_id=1, source_target_pairs={{0,16},{8,24},{16,0},{24,8},{1,17},{9,25},{17,1},{25,9},{2,18},{10... | collective-permute-start | bytes 1769480 | tf_op jit(solution)/shard_map/ppermute | solution.py:17
  62.8 5.1 %collective-permute-start.3 = (bf16[8,112,128]{2,1,0:T(8,128)(2,1)S(1)}, bf16[8,112,128]{2,1,0:T(8,128)(2,1)S(1)}, u32[]{:S(2)}, u32[]{:S(2)}) collective-permute-start(bf16[8,112,128]{2,1,0:T(8,128)(2,1)S(1)} %pad_maximum_fusion.11.refs_0_), channel_id=1, source_target_pairs={{0,8},{8,0},{16,24},{24,16},{1,9},{9,1},{17,25},{25,17},{2,10},{10... | collective-permute-start | bytes 688136 | tf_op jit(solution)/shard_map/ppermute | solution.py:17
  62.8 5.1 %collective-permute-start.7 = (bf16[8,112,128]{2,1,0:T(8,128)(2,1)S(1)}, bf16[8,112,128]{2,1,0:T(8,128)(2,1)S(1)}, u32[]{:S(2)}, u32[]{:S(2)}) collective-permute-start(bf16[8,112,128]{2,1,0:T(8,128)(2,1)S(1)} %pad_maximum_fusion.12.refs_4_), channel_id=1, source_target_pairs={{0,8},{8,0},{16,24},{24,16},{1,9},{9,1},{17,25},{25,17},{2,10},{10... | collective-permute-start | bytes 688136 | tf_op jit(solution)/shard_map/ppermute | solution.py:17
  67.3 1.6 collective-permute-start.5
  80.2 5.9 %collective-permute-start.10 = (bf16[1,4,2,1024]{3,2,1,0:T(2,128)(2,1)}, bf16[1,4,2,1024]{3,2,1,0:T(2,128)(2,1)S(1)}, u32[]{:S(2)}, u32[]{:S(2)}) collective-permute-start(bf16[1,4,2,1024]{3,2,1,0:T(2,128)(2,1)} %bitcast.61), channel_id=1, source_target_pairs={{0,4},{1,5},{2,6},{3,7},{4,0},{5,1},{6,2},{7,3},{8,12},{9,13},{10,... | collective-permute-start | bytes 49160 | tf_op jit(solution)/shard_map/ppermute | solution.py:17
  86.8 4.0 %collective-permute-start.11 = (bf16[2,4,2,1024]{3,2,1,0:T(2,128)(2,1)S(1)}, bf16[2,4,2,1024]{3,2,1,0:T(2,128)(2,1)S(1)}, u32[]{:S(2)}, u32[]{:S(2)}) collective-permute-start(bf16[2,4,2,1024]{3,2,1,0:T(2,128)(2,1)S(1)} %pad_maximum_fusion.25), channel_id=1, source_target_pairs={{0,2},{1,3},{2,0},{3,1},{4,6},{5,7},{6,4},{7,5},{8,10},{9,11},{10,... | collective-permute-start | bytes 98312 | tf_op jit(solution)/shard_map/ppermute | solution.py:17
  88.4 9.8 %collective-permute-start.16 = (bf16[8,288,128]{2,1,0:T(8,128)(2,1)S(1)}, bf16[8,288,128]{2,1,0:T(8,128)(2,1)S(1)}, u32[]{:S(2)}, u32[]{:S(2)}) collective-permute-start(bf16[8,288,128]{2,1,0:T(8,128)(2,1)S(1)} %pad_maximum_fusion.3.refs_0_), channel_id=1, source_target_pairs={{0,8},{8,0},{16,24},{24,16},{1,9},{9,1},{17,25},{25,17},{2,10},{10... | collective-permute-start | bytes 1769480 | tf_op jit(solution)/shard_map/ppermute | solution.py:17
  88.4 9.8 %collective-permute-start.20 = (bf16[8,288,128]{2,1,0:T(8,128)(2,1)S(1)}, bf16[8,288,128]{2,1,0:T(8,128)(2,1)}, u32[]{:S(2)}, u32[]{:S(2)}) collective-permute-start(bf16[8,288,128]{2,1,0:T(8,128)(2,1)S(1)} %pad_maximum_fusion.4.refs_4_), channel_id=1, source_target_pairs={{0,8},{8,0},{16,24},{24,16},{1,9},{9,1},{17,25},{25,17},{2,10},{10... | collective-permute-start | bytes 1769480 | tf_op jit(solution)/shard_map/ppermute | solution.py:17
  88.9 9.3 %collective-permute-start.18 = (bf16[8,288,128]{2,1,0:T(8,128)(2,1)S(1)}, bf16[8,288,128]{2,1,0:T(8,128)(2,1)}, u32[]{:S(2)}, u32[]{:S(2)}) collective-permute-start(bf16[8,288,128]{2,1,0:T(8,128)(2,1)S(1)} %collective-permute-done.17.refs_2_), channel_id=1, source_target_pairs={{0,8},{8,0},{16,24},{24,16},{1,9},{9,1},{17,25},{25,17},{2,10},{10... | collective-permute-start | bytes 1769480 | tf_op jit(solution)/shard_map/ppermute | solution.py:17
  89.0 9.2 %collective-permute-start.22 = (bf16[8,288,128]{2,1,0:T(8,128)(2,1)S(1)}, bf16[8,288,128]{2,1,0:T(8,128)(2,1)}, u32[]{:S(2)}, u32[]{:S(2)}) collective-permute-start(bf16[8,288,128]{2,1,0:T(8,128)(2,1)S(1)} %collective-permute-done.21.refs_6_), channel_id=1, source_target_pairs={{0,8},{8,0},{16,24},{24,16},{1,9},{9,1},{17,25},{25,17},{2,10},{10... | collective-permute-start | bytes 1769480 | tf_op jit(solution)/shard_map/ppermute | solution.py:17
  91.6 4.8 %collective-permute-start.12 = (bf16[4,4,2,1024]{3,2,1,0:T(2,128)(2,1)S(1)}, bf16[4,4,2,1024]{3,2,1,0:T(2,128)(2,1)S(1)}, u32[]{:S(2)}, u32[]{:S(2)}) collective-permute-start(bf16[4,4,2,1024]{3,2,1,0:T(2,128)(2,1)S(1)} %pad_maximum_fusion.21), channel_id=1, source_target_pairs={{0,1},{1,0},{2,3},{3,2},{4,5},{5,4},{6,7},{7,6},{8,9},{9,8},{10,11... | collective-permute-start | bytes 196616 | tf_op jit(solution)/shard_map/ppermute | solution.py:17
  160.9 4.3 %collective-permute-start.23 = (bf16[4,4,2,1024]{3,2,1,0:T(2,128)(2,1)S(1)}, bf16[4,4,2,1024]{3,2,1,0:T(2,128)(2,1)S(1)}, u32[]{:S(2)}, u32[]{:S(2)}) collective-permute-start(bf16[4,4,2,1024]{3,2,1,0:T(2,128)(2,1)S(1)} %slice.625), channel_id=1, source_target_pairs={{0,1},{1,0},{2,3},{3,2},{4,5},{5,4},{6,7},{7,6},{8,9},{9,8},{10,11... | collective-permute-start | bytes 196616 | tf_op jit(solution)/shard_map/ppermute | solution.py:17
  165.3 4.0 %collective-permute-start.24 = (bf16[2,4,2,1024]{3,2,1,0:T(2,128)(2,1)S(1)}, bf16[2,4,2,1024]{3,2,1,0:T(2,128)(2,1)S(1)}, u32[]{:S(2)}, u32[]{:S(2)}) collective-permute-start(bf16[2,4,2,1024]{3,2,1,0:T(2,128)(2,1)S(1)} %slice.627), channel_id=1, source_target_pairs={{0,2},{1,3},{2,0},{3,1},{4,6},{5,7},{6,4},{7,5},{8,10},{9,11},{10,... | collective-permute-start | bytes 98312 | tf_op jit(solution)/shard_map/ppermute | solution.py:17
  169.4 4.7 %collective-permute-start.25 = (bf16[1,4,2,1024]{3,2,1,0:T(2,128)(2,1)S(1)}, bf16[1,4,2,1024]{3,2,1,0:T(2,128)(2,1)S(1)}, u32[]{:S(2)}, u32[]{:S(2)}) collective-permute-start(bf16[1,4,2,1024]{3,2,1,0:T(2,128)(2,1)S(1)} %slice.629), channel_id=1, source_target_pairs={{0,4},{1,5},{2,6},{3,7},{4,0},{5,1},{6,2},{7,3},{8,12},{9,13},{10,... | collective-permute-start | bytes 49160 | tf_op jit(solution)/shard_map/ppermute | solution.py:17
  186.4 3.6 %collective-permute-start.31 = (bf16[16,112,128]{2,1,0:T(8,128)(2,1)S(1)}, bf16[16,112,128]{2,1,0:T(8,128)(2,1)S(1)}, u32[]{:S(2)}, u32[]{:S(2)}) collective-permute-start(bf16[16,112,128]{2,1,0:T(8,128)(2,1)S(1)} %slice.513), channel_id=1, source_target_pairs={{0,8},{8,0},{16,24},{24,16},{1,9},{9,1},{17,25},{25,17},{2,10},{10... | collective-permute-start | bytes 1376264 | tf_op jit(solution)/shard_map/ppermute | solution.py:17
  188.3 28.9 %collective-permute-start.41 = (bf16[16,304,128]{2,1,0:T(8,128)(2,1)S(1)}, bf16[16,304,128]{2,1,0:T(8,128)(2,1)S(1)}, u32[]{:S(2)}, u32[]{:S(2)}) collective-permute-start(bf16[16,304,128]{2,1,0:T(8,128)(2,1)S(1)} %slice.569), channel_id=1, source_target_pairs={{0,8},{8,0},{16,24},{24,16},{1,9},{9,1},{17,25},{25,17},{2,10},{10... | collective-permute-start | bytes 3735560 | tf_op jit(solution)/shard_map/ppermute | solution.py:17
  188.8 31.1 %collective-permute-start.36 = (bf16[16,304,128]{2,1,0:T(8,128)(2,1)S(1)}, bf16[16,304,128]{2,1,0:T(8,128)(2,1)S(1)}, u32[]{:S(2)}, u32[]{:S(2)}) collective-permute-start(bf16[16,304,128]{2,1,0:T(8,128)(2,1)S(1)} %slice.551), channel_id=1, source_target_pairs={{0,8},{8,0},{16,24},{24,16},{1,9},{9,1},{17,25},{25,17},{2,10},{10... | collective-permute-start | bytes 3735560 | tf_op jit(solution)/shard_map/ppermute | solution.py:17
  189.4 4.4 %collective-permute-start.26 = (bf16[16,112,128]{2,1,0:T(8,128)(2,1)S(1)}, bf16[16,112,128]{2,1,0:T(8,128)(2,1)S(1)}, u32[]{:S(2)}, u32[]{:S(2)}) collective-permute-start(bf16[16,112,128]{2,1,0:T(8,128)(2,1)S(1)} %slice.501), channel_id=1, source_target_pairs={{0,8},{8,0},{16,24},{24,16},{1,9},{9,1},{17,25},{25,17},{2,10},{10... | collective-permute-start | bytes 1376264 | tf_op jit(solution)/shard_map/ppermute | solution.py:17
  190.1 7.7 %collective-permute-start.32 = (bf16[8,112,128]{2,1,0:T(8,128)(2,1)S(1)}, bf16[8,112,128]{2,1,0:T(8,128)(2,1)S(1)}, u32[]{:S(2)}, u32[]{:S(2)}) collective-permute-start(bf16[8,112,128]{2,1,0:T(8,128)(2,1)S(1)} %pad_maximum_fusion.8), channel_id=1, source_target_pairs={{0,1},{1,0},{2,3},{3,2},{4,5},{5,4},{6,7},{7,6},{8,9},{9,8},{10,11... | collective-permute-start | bytes 688136 | tf_op jit(solution)/shard_map/ppermute | solution.py:17
  194.0 8.5 %collective-permute-start.27 = (bf16[8,112,128]{2,1,0:T(8,128)(2,1)S(1)}, bf16[8,112,128]{2,1,0:T(8,128)(2,1)S(1)}, u32[]{:S(2)}, u32[]{:S(2)}) collective-permute-start(bf16[8,112,128]{2,1,0:T(8,128)(2,1)S(1)} %slice.631), channel_id=1, source_target_pairs={{0,16},{8,24},{16,0},{24,8},{1,17},{9,25},{17,1},{25,9},{2,18},{10... | collective-permute-start | bytes 688136 | tf_op jit(solution)/shard_map/ppermute | solution.py:17
  198.0 6.4 %collective-permute-start.33 = (bf16[4,112,128]{2,1,0:T(8,128)(2,1)S(1)}, bf16[4,112,128]{2,1,0:T(8,128)(2,1)S(1)}, u32[]{:S(2)}, u32[]{:S(2)}) collective-permute-start(bf16[4,112,128]{2,1,0:T(8,128)(2,1)S(1)} %pad_maximum_fusion.16), channel_id=1, source_target_pairs={{0,16},{8,24},{16,0},{24,8},{1,17},{9,25},{17,1},{25,9},{2,18},{10... | collective-permute-start | bytes 344072 | tf_op jit(solution)/shard_map/ppermute | solution.py:17
  202.6 4.9 %collective-permute-start.28 = (bf16[4,112,128]{2,1,0:T(8,128)(2,1)S(1)}, bf16[4,112,128]{2,1,0:T(8,128)(2,1)S(1)}, u32[]{:S(2)}, u32[]{:S(2)}) collective-permute-start(bf16[4,112,128]{2,1,0:T(8,128)(2,1)S(1)} %slice.633), channel_id=1, source_target_pairs={{0,1},{1,0},{2,3},{3,2},{4,5},{5,4},{6,7},{7,6},{8,9},{9,8},{10,11... | collective-permute-start | bytes 344072 | tf_op jit(solution)/shard_map/ppermute | solution.py:17
  204.5 4.8 %collective-permute-start.34 = (bf16[2,112,128]{2,1,0:T(8,128)(2,1)S(1)}, bf16[2,112,128]{2,1,0:T(8,128)(2,1)S(1)}, u32[]{:S(2)}, u32[]{:S(2)}) collective-permute-start(bf16[2,112,128]{2,1,0:T(8,128)(2,1)S(1)} %pad_maximum_fusion.22), channel_id=1, source_target_pairs={{0,2},{1,3},{2,0},{3,1},{4,6},{5,7},{6,4},{7,5},{8,10},{9,11},{10,... | collective-permute-start | bytes 172040 | tf_op jit(solution)/shard_map/ppermute | solution.py:17
  207.5 4.8 %collective-permute-start.29 = (bf16[2,112,128]{2,1,0:T(8,128)(2,1)S(1)}, bf16[2,112,128]{2,1,0:T(8,128)(2,1)S(1)}, u32[]{:S(2)}, u32[]{:S(2)}) collective-permute-start(bf16[2,112,128]{2,1,0:T(8,128)(2,1)S(1)} %slice.635), channel_id=1, source_target_pairs={{0,2},{1,3},{2,0},{3,1},{4,6},{5,7},{6,4},{7,5},{8,10},{9,11},{10,... | collective-permute-start | bytes 172040 | tf_op jit(solution)/shard_map/ppermute | solution.py:17
  209.4 5.4 %collective-permute-start.35 = (bf16[1,112,128]{2,1,0:T(8,128)(2,1)S(1)}, bf16[1,112,128]{2,1,0:T(8,128)(2,1)S(1)}, u32[]{:S(2)}, u32[]{:S(2)}) collective-permute-start(bf16[1,112,128]{2,1,0:T(8,128)(2,1)S(1)} %pad_maximum_fusion.26), channel_id=1, source_target_pairs={{0,4},{1,5},{2,6},{3,7},{4,0},{5,1},{6,2},{7,3},{8,12},{9,13},{10,... | collective-permute-start | bytes 86024 | tf_op jit(solution)/shard_map/ppermute | solution.py:17
  212.4 4.8 %collective-permute-start.30 = (bf16[1,112,128]{2,1,0:T(8,128)(2,1)S(1)}, bf16[1,112,128]{2,1,0:T(8,128)(2,1)S(1)}, u32[]{:S(2)}, u32[]{:S(2)}) collective-permute-start(bf16[1,112,128]{2,1,0:T(8,128)(2,1)S(1)} %slice.637), channel_id=1, source_target_pairs={{0,4},{1,5},{2,6},{3,7},{4,0},{5,1},{6,2},{7,3},{8,12},{9,13},{10,... | collective-permute-start | bytes 86024 | tf_op jit(solution)/shard_map/ppermute | solution.py:17
  217.6 13.1 %collective-permute-start.42 = (bf16[8,304,128]{2,1,0:T(8,128)(2,1)S(1)}, bf16[8,304,128]{2,1,0:T(8,128)(2,1)S(1)}, u32[]{:S(2)}, u32[]{:S(2)}) collective-permute-start(bf16[8,304,128]{2,1,0:T(8,128)(2,1)S(1)} %pad_maximum_fusion), channel_id=1, source_target_pairs={{0,1},{1,0},{2,3},{3,2},{4,5},{5,4},{6,7},{7,6},{8,9},{9,8},{10,11... | collective-permute-start | bytes 1867784 | tf_op jit(solution)/shard_map/ppermute | solution.py:17
  220.3 16.1 %collective-permute-start.37 = (bf16[8,304,128]{2,1,0:T(8,128)(2,1)S(1)}, bf16[8,304,128]{2,1,0:T(8,128)(2,1)S(1)}, u32[]{:S(2)}, u32[]{:S(2)}) collective-permute-start(bf16[8,304,128]{2,1,0:T(8,128)(2,1)S(1)} %slice.668), channel_id=1, source_target_pairs={{0,16},{8,24},{16,0},{24,8},{1,17},{9,25},{17,1},{25,9},{2,18},{10... | collective-permute-start | bytes 1867784 | tf_op jit(solution)/shard_map/ppermute | solution.py:17
  230.9 8.9 %collective-permute-start.43 = (bf16[4,304,128]{2,1,0:T(8,128)(2,1)S(1)}, bf16[4,304,128]{2,1,0:T(8,128)(2,1)S(1)}, u32[]{:S(2)}, u32[]{:S(2)}) collective-permute-start(bf16[4,304,128]{2,1,0:T(8,128)(2,1)S(1)} %pad_maximum_fusion.5), channel_id=1, source_target_pairs={{0,16},{8,24},{16,0},{24,8},{1,17},{9,25},{17,1},{25,9},{2,18},{10... | collective-permute-start | bytes 933896 | tf_op jit(solution)/shard_map/ppermute | solution.py:17
  236.7 7.0 %collective-permute-start.38 = (bf16[4,304,128]{2,1,0:T(8,128)(2,1)S(1)}, bf16[4,304,128]{2,1,0:T(8,128)(2,1)S(1)}, u32[]{:S(2)}, u32[]{:S(2)}) collective-permute-start(bf16[4,304,128]{2,1,0:T(8,128)(2,1)S(1)} %slice.670), channel_id=1, source_target_pairs={{0,1},{1,0},{2,3},{3,2},{4,5},{5,4},{6,7},{7,6},{8,9},{9,8},{10,11... | collective-permute-start | bytes 933896 | tf_op jit(solution)/shard_map/ppermute | solution.py:17
  239.9 6.2 %collective-permute-start.44 = (bf16[2,304,128]{2,1,0:T(8,128)(2,1)S(1)}, bf16[2,304,128]{2,1,0:T(8,128)(2,1)S(1)}, u32[]{:S(2)}, u32[]{:S(2)}) collective-permute-start(bf16[2,304,128]{2,1,0:T(8,128)(2,1)S(1)} %pad_maximum_fusion.13), channel_id=1, source_target_pairs={{0,2},{1,3},{2,0},{3,1},{4,6},{5,7},{6,4},{7,5},{8,10},{9,11},{10,... | collective-permute-start | bytes 466952 | tf_op jit(solution)/shard_map/ppermute | solution.py:17
  243.7 6.0 %collective-permute-start.39 = (bf16[2,304,128]{2,1,0:T(8,128)(2,1)S(1)}, bf16[2,304,128]{2,1,0:T(8,128)(2,1)S(1)}, u32[]{:S(2)}, u32[]{:S(2)}) collective-permute-start(bf16[2,304,128]{2,1,0:T(8,128)(2,1)S(1)} %slice.672), channel_id=1, source_target_pairs={{0,2},{1,3},{2,0},{3,1},{4,6},{5,7},{6,4},{7,5},{8,10},{9,11},{10,... | collective-permute-start | bytes 466952 | tf_op jit(solution)/shard_map/ppermute | solution.py:17
  246.2 5.4 %collective-permute-start.45 = (bf16[1,304,128]{2,1,0:T(8,128)(2,1)S(1)}, bf16[1,304,128]{2,1,0:T(8,128)(2,1)S(1)}, u32[]{:S(2)}, u32[]{:S(2)}) collective-permute-start(bf16[1,304,128]{2,1,0:T(8,128)(2,1)S(1)} %pad_maximum_fusion.19), channel_id=1, source_target_pairs={{0,4},{1,5},{2,6},{3,7},{4,0},{5,1},{6,2},{7,3},{8,12},{9,13},{10,... | collective-permute-start | bytes 233480 | tf_op jit(solution)/shard_map/ppermute | solution.py:17
  249.8 6.2 %collective-permute-start.40 = (bf16[1,304,128]{2,1,0:T(8,128)(2,1)S(1)}, bf16[1,304,128]{2,1,0:T(8,128)(2,1)S(1)}, u32[]{:S(2)}, u32[]{:S(2)}) collective-permute-start(bf16[1,304,128]{2,1,0:T(8,128)(2,1)S(1)} %slice.674), channel_id=1, source_target_pairs={{0,4},{1,5},{2,6},{3,7},{4,0},{5,1},{6,2},{7,3},{8,12},{9,13},{10,... | collective-permute-start | bytes 233480 | tf_op jit(solution)/shard_map/ppermute | solution.py:17
  (17 other events, 177.4 us)
where the time goes:
time: 259 us; the launch traced here: 258 us
  waiting for transfers between devices  85.1 us (33%)
  Pallas kernels  79.6 us (31%)
  starting transfers between devices  61.1 us (24%)
  local copies, waits for them, and re-layouts  23 us (9%)
  other arithmetic  8.32 us (3%)
    ppermute x46, waiting for transfers between devices, swap(): return lax.ppermute(array, axis, [(i, i ^ bit) for i in range(count)])  85.1 us
    ppermute x46, starting transfers between devices, swap(): return lax.ppermute(array, axis, [(i, i ^ bit) for i in range(count)])  61.1 us
    pallas_call x1, Pallas kernels, feed(): pl.pallas_call(kernel, grid=(count,), in_specs=[pl.BlockSpec(memory_space...  33.6 us
    pallas_call x1, Pallas kernels, attend_back(): pl.pallas_call(kernel, grid=(count,), in_specs=[each(qkv.shape), each(sum...  12 us
    pallas_call x1, Pallas kernels, project_back(): pl.pallas_call(kernel, grid=(count,), in_specs=[pl.BlockSpec(memory_space...  10.6 us
    pallas_call x1, Pallas kernels, attend(): pl.pallas_call(kernel, grid=(count,), in_specs=[each(qkv.shape), each(sum...  8.86 us
    pallas_call x2, Pallas kernels, unpack(): pl.pallas_call(kernel, out_shape=[jax.ShapeDtypeStruct(shape, BF16) for s...  8.61 us
    pallas_call x1, Pallas kernels, project(): pl.pallas_call(kernel, grid=(count,), in_specs=[each(inputs.shape)] + [fu...  5.96 us
  transfers between devices with their start and end apart: 46, of which 30 were waited for; matrix products, arithmetic and copies ran while one was open for 6% of the time, Pallas kernels for 4%

commit v1 on v0

--- a/solution.py
+++ b/solution.py
@@ -40,13 +40,15 @@
 CORE = ("batch", 1)
 
 
-def gather_all(pack):
-    rows = pack.shape[0]
-    half = rows // 2
-    state = pack[None]
+def gather_outer(state):
+    for stage in outer_stages():
+        state = jnp.concatenate([state, swap(state, *stage)], 0)
+    return state
+
+
+def gather_inner(state):
+    half = state.shape[1] // 2
     outer = outer_stages()
-    for stage in outer:
-        state = jnp.concatenate([state, swap(state, *stage)], 0)
     pieces = []
     for first, order in ((0, (X_STAGE, Y_STAGE)), (half, (Y_STAGE, X_STAGE))):
         part = state[:, first : first + half]
@@ -76,29 +78,19 @@
     return found
 
 
-def unpack(pieces, segments, targets, shapes):
-    arrays = [piece for piece, _, _ in pieces]
-
-    def kernel(spot, *refs):
-        ins, outs = refs[: len(arrays)], refs[len(arrays) :]
-        for ref, (piece, names, first) in zip(ins, pieces):
-            for p, (sr, br) in enumerate(names):
-                s, b = spot[0] ^ sr, spot[1] ^ br
-                for name, row, here, size in cuts(segments, first, piece.shape[1]):
-                    if name == "vec" and br != 0:
-                        continue
+def assemble(spot, refs, pieces, segments, targets, outs, vec):
+    for ref, (piece, names, first) in zip(refs, pieces):
+        for p, (sr, br) in enumerate(names):
+            s, b = spot[0] ^ sr, spot[1] ^ br
+            for name, row, here, size in cuts(segments, first, piece.shape[1]):
+                if name == "vec":
+                    if br == 0:
+                        vec(ref[p, here : here + size, :], s)
+                else:
                     number, top, left = targets(name, row, s, b)
                     outs[number][
                         pl.ds(pl.multiple_of(top, 16), size), pl.ds(pl.multiple_of(left, 128), 128)
                     ] = ref[p, here : here + size, :]
-
-    return pl.pallas_call(
-        kernel,
-        out_shape=[jax.ShapeDtypeStruct(shape, BF16) for shape in shapes],
-        in_specs=[pl.BlockSpec(memory_space=pltpu.SMEM)]
-        + [pl.BlockSpec(memory_space=pltpu.VMEM) for _ in arrays],
-        out_specs=[pl.BlockSpec(memory_space=pltpu.VMEM) for _ in shapes],
-    )(place(), *arrays)
 
 
 def pack_order():
@@ -111,9 +103,11 @@
 
 def write_packed(spot, ins, vec_block, outs, segments, targets, orders):
     half = sum(size for _, size in segments) // 2
-    for out, names, first in zip(outs, orders, (0, half)):
+    for k, (names, first) in enumerate(zip(orders, (0, half))):
         for p, (sr, br) in enumerate(names):
             s, b = spot[0] ^ sr, spot[1] ^ br
+            out = outs[2 * k + p // (len(names) // 2)]
+            p = p % (len(names) // 2)
             for name, row, here, size in cuts(segments, first, half):
                 if name == "vec":
                     out[p, here : here + size, :] = vec_block(s)
@@ -144,29 +138,123 @@
     return jnp.concatenate([low] + split_pair(total), -2)
 
 
-def reduce_all(halves, pairs):
-    outer = outer_stages()[::-1]
+ORDERS = ((CORE, X_STAGE, Y_STAGE), (CORE, Y_STAGE, X_STAGE))
+
+
+def reduce_step(halves, step, last=False):
     done = []
-    for k, (state, order) in enumerate(
-        zip(halves, ((CORE, X_STAGE, Y_STAGE), (CORE, Y_STAGE, X_STAGE)))
-    ):
-        add = add_pairs if pairs and k == 1 else add_low
-        stages = list(order) + outer
-        for stage in stages:
-            count = state.shape[0] // 2
-            theirs = swap(state[count:], *stage)
-            mine = state[:count]
-            if stage is stages[-1]:
-                if add is add_pairs:
-                    total = join_pair(mine) + join_pair(theirs)
-                    body = mine[:, :-VEC_ROWS].astype(F32) + theirs[:, :-VEC_ROWS].astype(F32)
-                    state = jnp.concatenate([body, total], 1)
+    for k, (kept, sent) in enumerate(halves):
+        theirs = swap(sent, *ORDERS[k][step])
+        if last:
+            done.append((kept, theirs))
+            continue
+        state = (add_pairs if k == 1 else add_low)(kept, theirs)
+        count = state.shape[0] // 2
+        done.append((state[:count], state[count:]))
+    return done
+
+
+def sum_rows(mine, theirs, spans):
+    total = mine.astype(F32) + theirs.astype(F32)
+    count = VEC_ROWS // 2
+    return total, [total[at : at + count] + total[at + count : at + VEC_ROWS] for at in spans]
+
+
+def joined_sum(couples):
+    count = couples[0][0].shape[0]
+    rows = sum(kept.shape[1] for kept, _, _ in couples)
+
+    def kernel(*refs):
+        ins, outs = refs[:-2], refs[-2:]
+        for p in range(count):
+            out = outs[p // (count // 2)]
+            at = 0
+            for k, (kept, _, vectors) in enumerate(couples):
+                size = kept.shape[1]
+                total, pairs = sum_rows(
+                    ins[2 * k][p], ins[2 * k + 1][p], [size - VEC_ROWS] if vectors else []
+                )
+                out[p % (count // 2), at : at + size, :] = total.astype(BF16)
+                for pair in pairs:
+                    high = pair.astype(BF16)
+                    low = (pair - high.astype(F32)).astype(BF16)
+                    end = at + size
+                    out[p % (count // 2), end - VEC_ROWS : end - VEC_ROWS // 2, :] = high
+                    out[p % (count // 2), end - VEC_ROWS // 2 : end, :] = low
+                at += size
+
+    arrays = [array for kept, theirs, _ in couples for array in (kept, theirs)]
+    return pl.pallas_call(
+        kernel,
+        out_shape=[jax.ShapeDtypeStruct((count // 2, rows, 128), BF16)] * 2,
+        in_specs=[pl.BlockSpec(memory_space=pltpu.VMEM)] * len(arrays),
+        out_specs=[pl.BlockSpec(memory_space=pltpu.VMEM)] * 2,
+    )(*arrays)
+
+
+def again(kept, theirs, spans):
+    count, rows = kept.shape[:2]
+
+    def kernel(mine_ref, theirs_ref, *outs):
+        for p in range(count):
+            out = outs[p // (count // 2)]
+            q = p % (count // 2)
+            total, pairs = sum_rows(mine_ref[p], theirs_ref[p], spans)
+            out[q] = total.astype(BF16)
+            for pair, at in zip(pairs, spans):
+                high = pair.astype(BF16)
+                out[q, at : at + VEC_ROWS // 2, :] = high
+                low = (pair - high.astype(F32)).astype(BF16)
+                out[q, at + VEC_ROWS // 2 : at + VEC_ROWS, :] = low
+
+    return pl.pallas_call(
+        kernel,
+        out_shape=[jax.ShapeDtypeStruct((count // 2, rows, 128), BF16)] * 2,
+        in_specs=[pl.BlockSpec(memory_space=pltpu.VMEM)] * 2,
+        out_specs=[pl.BlockSpec(memory_space=pltpu.VMEM)] * 2,
+    )(kept, theirs)
+
+
+def finish(kept, theirs, parts, spans, shapes):
+    def kernel(mine_ref, theirs_ref, *outs):
+        total, pairs = sum_rows(mine_ref[0], theirs_ref[0], spans)
+        for number, row, left, at, size in parts:
+            outs[number][row : row + size, left : left + 128] = total[at : at + size]
+        for k, pair in enumerate(pairs):
+            outs[len(shapes) + k][...] = pair
+
+    return pl.pallas_call(
+        kernel,
+        out_shape=[jax.ShapeDtypeStruct(shape, F32) for shape in shapes]
+        + [jax.ShapeDtypeStruct((VEC_ROWS // 2, 128), F32)] * len(spans),
+        in_specs=[pl.BlockSpec(memory_space=pltpu.VMEM)] * 2,
+        out_specs=[pl.BlockSpec(memory_space=pltpu.VMEM)] * (len(shapes) + len(spans)),
+    )(kept, theirs)
+
+
+def reduce_end(groups, weights):
+    couples = []
+    parts = []
+    spans = []
+    at = 0
+    for numbers, halves in groups:
+        segments = columns([weights[n] for n in numbers]) + [("vec", VEC_ROWS)]
+        for k, (kept, theirs) in enumerate(halves):
+            couples.append((kept, theirs, k == 1))
+            half = kept.shape[1]
+            for name, row, here, size in cuts(segments, k * half, half):
+                if name == "vec":
+                    spans.append(at + here)
                 else:
-                    state = mine.astype(F32) + theirs.astype(F32)
-            else:
-                state = add(mine, theirs)
-        done.append(state[0])
-    return jnp.concatenate(done, 0)
+                    parts.append((numbers[name[0]], row, name[1] * 128, at + here, size))
+            at += half
+    kept, sent = joined_sum(couples)
+    stages = outer_stages()[::-1]
+    for k, stage in enumerate(stages):
+        theirs = swap(sent, *stage)
+        if k < len(stages) - 1:
+            kept, sent = again(kept, theirs, spans)
+    return finish(kept, theirs, parts, spans, [w.shape for w in weights])
 
 
 def seq_stages():
@@ -228,50 +316,54 @@
     ]
 
 
-def gather_group(weights, vectors, after=None):
-    blocks = packed(weights)
-    segments = columns(weights)
-    shapes = whole(weights)
-    if vectors:
-        flat = jnp.concatenate(vectors).reshape(-1, 128)
-        blocks = blocks + [jnp.pad(flat, ((0, VEC_ROWS - flat.shape[0]), (0, 0)))]
-        segments = segments + [("vec", VEC_ROWS)]
-        shapes = shapes + [(lax.axis_size("seq") * VEC_ROWS, 128)]
-    block = jnp.concatenate(blocks, 0)
-    if after is not None:
-        block = lax.optimization_barrier((block, after))[0]
-    pieces = gather_all(block)
-    return unpack(pieces, segments, spots(weights), shapes), pieces[-1][0]
-
-
-def gather_weights(weights, vectors):
-    if not whole_tiles(weights, vectors):
-        wide = [lax.all_gather(w, "batch", axis=1, tiled=True) for w in weights]
-        wide = [lax.all_gather(w, "seq", axis=0, tiled=True) for w in wide]
-        return wide, [lax.all_gather(v, "seq", axis=0, tiled=True) for v in vectors]
-    first, last = gather_group(weights[:3], vectors)
-    second, _ = gather_group(weights[3:], [], last)
-    sizes = [v.shape[0] for v in vectors]
-    flat = first[3].reshape(lax.axis_size("seq"), VEC_ROWS * 128)
-    wide = []
-    at = 0
-    for size in sizes:
-        wide.append(flat[:, at : at + size].reshape(-1))
-        at += size
-    return first[:3] + second, wide
-
-
-def reduce_group(weights, halves, sizes):
-    rows = reduce_all(halves, True)
+def pack_shards(weights, vectors, after=None):
+    segments = columns(weights) + ([("vec", VEC_ROWS)] if vectors else [])
+    rows = sum(size for _, size in segments)
+    extra = [] if after is None else [after]
+
+    def kernel(spot, *refs):
+        out = refs[-1]
+        at = 0
+        for ref, weight in zip(refs, weights):
+            for left in range(0, weight.shape[1], 128):
+                out[0, at : at + weight.shape[0], :] = ref[:, left : left + 128]
+                at += weight.shape[0]
+        if not vectors:
+            return
+        found = []
+        for ref in refs[len(weights) : len(weights) + len(vectors)]:
+            size = ref.shape[0]
+            line = ref[...].astype(F32)
+            if size < 128:
+                line = jnp.concatenate([line[None]] * (128 // size), 1)
+                lane = lax.broadcasted_iota(jnp.int32, line.shape, 1)
+                found.append(jnp.where(lane // size == spot[0] % (128 // size), line, 0.0))
+            else:
+                found += [line[None, k : k + 128] for k in range(0, size, 128)]
+        row = lax.broadcasted_iota(jnp.int32, (VEC_ROWS, 128), 0)
+        block = jnp.zeros((VEC_ROWS, 128), F32)
+        for k, line in enumerate(found):
+            block = jnp.where(row == k, line, block)
+        out[0, at:, :] = block.astype(BF16)
+
+    return pl.pallas_call(
+        kernel,
+        out_shape=jax.ShapeDtypeStruct((1, rows, 128), BF16),
+        in_specs=[pl.BlockSpec(memory_space=pltpu.SMEM)]
+        + [pl.BlockSpec(memory_space=pltpu.VMEM)] * (len(weights) + len(vectors))
+        + [pl.BlockSpec(memory_space=pl.ANY)] * len(extra),
+        out_specs=pl.BlockSpec(memory_space=pltpu.VMEM),
+    )(place(), *weights, *vectors, *extra)
+
+
+def gather_plain(weights, vectors):
+    wide = [lax.all_gather(w, "batch", axis=1, tiled=True) for w in weights]
+    wide = [lax.all_gather(w, "seq", axis=0, tiled=True) for w in wide]
+    return wide, [lax.all_gather(v, "seq", axis=0, tiled=True).astype(F32) for v in vectors]
+
+
+def own_parts(lanes, sizes):
     outs = []
-    at = 0
-    for weight in weights:
-        parts = []
-        for _ in range(weight.shape[1] // 128):
-            parts.append(rows[at : at + weight.shape[0]])
-            at += weight.shape[0]
-        outs.append(parts[0] if len(parts) == 1 else jnp.concatenate(parts, 1))
-    lanes = rows[at:]
     row = 0
     for size in sizes:
         if size < 128:
@@ -329,13 +421,51 @@
     return pl.BlockSpec((1,) + tuple(shape[1:]), lambda i: (i,) + (0,) * (len(shape) - 1))
 
 
-def project(inputs, w_query, w_key, w_value, gain, shift):
+NARROW = 8
+
+
+def project(inputs, shards, slices, pieces, wide, lines, tiles):
     count, rows, width = inputs.shape
     half = rows // 2
-
-    def kernel(x_ref, q_ref, k_ref, v_ref, gain_ref, shift_ref, out_ref, pooled_ref):
+    hidden = slices[5].shape[0] * lax.axis_size("seq")
+    segments = columns(shards) + [("vec", VEC_ROWS)]
+    targets = spots(shards)
+    order = (0, 1, 2, 3, 4, 6)
+    arrays = [piece for piece, _, _ in pieces] if tiles else list(wide) + list(lines)
+
+    def kernel(spot, x_ref, *refs):
+        ins = refs[: len(arrays)]
+        out_ref, pooled_ref, q_ref, k_ref, v_ref, narrow_ref, wide_ref = refs[len(arrays) :]
+
+        @pl.when(pl.program_id(0) == 0)
+        def _():
+            if tiles:
+                narrow_ref[...] = jnp.zeros_like(narrow_ref)
+                wide_ref[...] = jnp.zeros_like(wide_ref)
+
+                def vec(block, s):
+                    block = block.astype(F32)
+                    row = 0
+                    for k, member in enumerate(slices):
+                        size = member.shape[0]
+                        start = s * size
+                        for at in range(0, size, 128):
+                            left = pl.multiple_of((start + at) // 128 * 128, 128)
+                            line = block[row : row + 1]
+                            if k == 5:
+                                wide_ref[0:1, pl.ds(left, 128)] += line
+                            else:
+                                to = order.index(k)
+                                narrow_ref[to : to + 1, pl.ds(left, 128)] += line
+                            row += 1
+
+                assemble(spot, ins, pieces, segments, targets, (q_ref, k_ref, v_ref), vec)
+            else:
+                for ref, source in zip((q_ref, k_ref, v_ref, narrow_ref, wide_ref), ins):
+                    ref[...] = source[...]
+
         unit, _ = norm_parts(x_ref[0].astype(F32))
-        normed = (unit * gain_ref[...] + shift_ref[...]).astype(BF16)
+        normed = (unit * narrow_ref[0:1, :] + narrow_ref[1:2, :]).astype(BF16)
         out_ref[0, :, :width] = dot(normed, q_ref[...]).astype(BF16)
         for k, ref in enumerate((k_ref, v_ref)):
             product = dot(normed, ref[...])
@@ -345,13 +475,18 @@
                 pooled_ref[0, j : j + 1, k * width : (k + 1) * width] = mean.astype(BF16)
 
     shapes = [(count, rows, 3 * width), (count, 2, 2 * width)]
+    square = (width, width)
     return pl.pallas_call(
         kernel,
         grid=(count,),
-        in_specs=[each(inputs.shape)] + [full((width, width))] * 3 + [full((1, width))] * 2,
-        out_specs=[each(shape) for shape in shapes],
-        out_shape=[jax.ShapeDtypeStruct(shape, BF16) for shape in shapes],
-    )(inputs, w_query, w_key, w_value, gain, shift)
+        in_specs=[pl.BlockSpec(memory_space=pltpu.SMEM), each(inputs.shape)]
+        + [pl.BlockSpec(memory_space=pltpu.VMEM)] * len(arrays),
+        out_specs=[each(shape) for shape in shapes]
+        + [full(square)] * 3
+        + [full((NARROW, width)), full((1, hidden))],
+        out_shape=[jax.ShapeDtypeStruct(shape, BF16) for shape in shapes + [square] * 3]
+        + [jax.ShapeDtypeStruct((NARROW, width), F32), jax.ShapeDtypeStruct((1, hidden), F32)],
+    )(place(), inputs, *arrays)
 
 
 def head_mask(rows, lane_half):
@@ -369,11 +504,11 @@
     return jnp.concatenate([scores[:rows], far], 0)
 
 
-def attend(qkv, summaries, visible, inputs, w_out, bias_out):
-    count, rows, width = inputs.shape
+def attend(qkv, summaries, visible):
+    count, rows, width = qkv.shape[0], qkv.shape[1], qkv.shape[2] // 3
     far = summaries.shape[1]
 
-    def kernel(qkv_ref, sum_ref, vis_ref, x_ref, w_ref, bias_ref, mixed_ref, lse_ref, middle_ref):
+    def kernel(qkv_ref, sum_ref, vis_ref, mixed_ref, lse_ref):
         seen = vis_ref[...]
         for pair in range(HEADS // 2):
             at = pair * 2 * HEAD
@@ -404,9 +539,8 @@
                 part = dot(only(values, side), probs, 0, 0)
                 total = part if total is None else total + part
             mixed_ref[0, :, at : at + 2 * HEAD] = total.T.astype(BF16)
-        branch = dot(mixed_ref[0], w_ref[...]) + bias_ref[...]
-        middle_ref[0] = x_ref[0].astype(F32) + branch
-
+
+    block = (count, rows, width)
     return pl.pallas_call(
         kernel,
         grid=(count,),
@@ -414,17 +548,13 @@
             each(qkv.shape),
             each(summaries.shape),
             full((far, rows)),
-            each(inputs.shape),
-            full((width, width)),
-            full((1, width)),
         ],
-        out_specs=[each(inputs.shape), each((count, HEADS, rows)), each(inputs.shape)],
+        out_specs=[each(block), each((count, HEADS, rows))],
         out_shape=[
-            jax.ShapeDtypeStruct(inputs.shape, BF16),
+            jax.ShapeDtypeStruct(block, BF16),
             jax.ShapeDtypeStruct((count, HEADS, rows), F32),
-            jax.ShapeDtypeStruct(inputs.shape, F32),
         ],
-    )(qkv, summaries, visible, inputs, w_out, bias_out)
+    )(qkv, summaries, visible)
 
 
 def split_rows(total):
@@ -448,11 +578,10 @@
     return block
 
 
-def feed(
-    middle, cotangent, mixed, w_out, w_up, w_down, gain, shift, bias_up, bias_down, shards, tiles
-):
-    count, rows, width = middle.shape
-    hidden_width = w_up.shape[1]
+def feed(inputs, cotangent, mixed, narrow, long_bias, pieces, wide, shards, tiles):
+    count, rows, width = inputs.shape
+    hidden_width = long_bias.shape[1]
+    arrays = [piece for piece, _, _ in pieces] if tiles else list(wide)
     step = 512
     grads = [(width, width), (width, hidden_width), (hidden_width, width)]
     segments = columns(shards) + [("vec", VEC_ROWS)]
@@ -461,26 +590,33 @@
     half = sum(size for _, size in segments) // 2
     per = width // lax.axis_size("seq")
 
-    def kernel(spot, middle_ref, cot_ref, mixed_ref, wo_ref, wu_ref, wd_ref, gain_ref, shift_ref,
-               bu_ref, bd_ref, out_ref, mgrad_ref, xgrad_ref, narrow_ref, wide_ref, *rest):
+    def kernel(spot, x_ref, cot_ref, mixed_ref, lines_ref, bu_ref, *rest):
+        ins, rest = rest[: len(arrays)], rest[len(arrays) :]
+        out_ref, mgrad_ref, xgrad_ref, narrow_ref, wide_ref, *rest = rest
         if tiles:
-            packs, (go_ref, gu_ref, gd_ref, high_ref, long_ref) = rest[:2], rest[2:]
+            packs, rest = rest[:4], rest[4:]
+            go_ref, gu_ref, gd_ref, high_ref, long_ref, wo_ref, wu_ref, wd_ref = rest
         else:
             go_ref, gu_ref, gd_ref = rest
+            wo_ref, wu_ref, wd_ref = ins
         step_id = pl.program_id(0)
+        bias, gain, shift, last = (lines_ref[k : k + 1, :] for k in (4, 2, 3, 5))
 
         @pl.when(step_id == 0)
         def _():
             for ref in (go_ref, gu_ref, gd_ref, narrow_ref, wide_ref):
                 ref[...] = jnp.zeros_like(ref)
-
-        middle = middle_ref[0]
+            if tiles:
+                weights = (wo_ref, wu_ref, wd_ref)
+                assemble(spot, ins, pieces, segments[:-1], targets, weights, None)
+
+        middle = x_ref[0].astype(F32) + (dot(mixed_ref[0], wo_ref[...]) + bias)
         cot = cot_ref[0]
         tangent = cot.astype(BF16)
         unit, scale = norm_parts(middle)
-        normed = (unit * gain_ref[...] + shift_ref[...]).astype(BF16)
+        normed = (unit * gain + shift).astype(BF16)
         flipped = normed.T
-        final = middle + bd_ref[...]
+        final = middle + last
         back = None
         for at in range(0, hidden_width, step):
             here = slice(at, at + step)
@@ -497,7 +633,7 @@
         out_ref[0] = final.astype(BF16)
         narrow_ref[0:1, :] += jnp.sum(back * unit, 0, keepdims=True)
         narrow_ref[1:2, :] += jnp.sum(back, 0, keepdims=True)
-        middle_grad = cot + norm_back(back, unit, scale, gain_ref[...])
+        middle_grad = cot + norm_back(back, unit, scale, gain)
         mgrad_ref[0] = middle_grad
         branch = middle_grad.astype(BF16)
         narrow_ref[2:3, :] += jnp.sum(branch.astype(F32), 0, keepdims=True)
@@ -526,7 +662,7 @@
                     orders,
                 )
 
-    block = middle.shape
+    block = inputs.shape
     out_shape = [
         jax.ShapeDtypeStruct(block, BF16),
         jax.ShapeDtypeStruct(block, F32),
@@ -537,10 +673,12 @@
     out_specs = [each(block)] * 3 + [full((8, width)), full((8, hidden_width))]
     scratch = []
     if tiles:
-        out_shape += [jax.ShapeDtypeStruct((len(names), half, 128), BF16) for names in orders]
-        out_specs += [full((len(names), half, 128)) for names in orders]
+        packed_shapes = [(len(names) // 2, half, 128) for names in orders for _ in range(2)]
+        out_shape += [jax.ShapeDtypeStruct(shape, BF16) for shape in packed_shapes]
+        out_specs += [pl.BlockSpec(memory_space=pltpu.VMEM)] * 4
         scratch = [pltpu.VMEM(shape, F32) for shape in grads]
         scratch += [pltpu.VMEM((VEC_ROWS, width), F32), pltpu.VMEM((VEC_ROWS, hidden_width), F32)]
+        scratch += [pltpu.VMEM(shape, BF16) for shape in grads]
     else:
         out_shape += [jax.ShapeDtypeStruct(shape, F32) for shape in grads]
         out_specs += [full(shape) for shape in grads]
@@ -549,21 +687,26 @@
         grid=(count,),
         in_specs=[pl.BlockSpec(memory_space=pltpu.SMEM)]
         + [each(block)] * 3
-        + [full(shape) for shape in ((width, width), (width, hidden_width), (hidden_width, width))]
-        + [full((1, width)), full((1, width)), full((1, hidden_width)), full((1, width))],
+        + [full(narrow.shape), full(long_bias.shape)]
+        + [pl.BlockSpec(memory_space=pltpu.VMEM)] * len(arrays),
         out_specs=out_specs,
         out_shape=out_shape,
         scratch_shapes=scratch,
-    )(
-        place(), middle, cotangent, mixed, w_out, w_up, w_down, gain, shift, bias_up, bias_down
-    )
-
-
-def attend_back(qkv, summaries, visible, lse, mixed_grad):
+    )(place(), inputs, cotangent, mixed, narrow, long_bias, *arrays)
+
+
+def attend_back(qkv, summaries, visible, lse, mixed_grad, first, number, before=(), after=()):
     count, rows, width = mixed_grad.shape
     far = summaries.shape[1]
-
-    def kernel(qkv_ref, sum_ref, vis_ref, lse_ref, grad_ref, dq_ref, dk_ref, dv_ref, far_ref):
+    extra = list(before) + list(after)
+
+    def each(shape):
+        return pl.BlockSpec(
+            (1,) + tuple(shape[1:]), lambda i: (i + first,) + (0,) * (len(shape) - 1)
+        )
+
+    def kernel(qkv_ref, sum_ref, vis_ref, lse_ref, grad_ref, *rest):
+        dq_ref, dk_ref, dv_ref, far_ref = rest[len(extra) :]
         seen = vis_ref[...]
         for pair in range(HEADS // 2):
             at = pair * 2 * HEAD
@@ -603,14 +746,15 @@
     block = mixed_grad.shape
     return pl.pallas_call(
         kernel,
-        grid=(count,),
+        grid=(number,),
         in_specs=[
             each(qkv.shape),
             each(summaries.shape),
             full((far, rows)),
             each(lse.shape),
             each(block),
-        ],
+        ]
+        + [pl.BlockSpec(memory_space=pl.ANY)] * len(extra),
         out_specs=[each(block)] * 3 + [each(summaries.shape)],
         out_shape=[
             jax.ShapeDtypeStruct(block, BF16),
@@ -618,11 +762,12 @@
             jax.ShapeDtypeStruct(block, F32),
             jax.ShapeDtypeStruct(summaries.shape, BF16),
         ],
-    )(qkv, summaries, visible, lse, mixed_grad)
+        input_output_aliases={5 + k: k for k in range(len(before))},
+    )(qkv, summaries, visible, lse, mixed_grad, *extra)
 
 
 def project_back(
-    inputs, d_query, d_keys, d_values, owned, weights, gain, shift, middle_grad, shards, tiles
+    inputs, d_query, d_keys, d_values, owned, weights, narrow, middle_grad, shards, tiles, after
 ):
     count, rows, width = inputs.shape
     half_span = rows // 2
@@ -632,10 +777,12 @@
     half = sum(size for _, size in segments) // 2
     per = width // lax.axis_size("seq")
 
-    def kernel(spot, x_ref, dq_ref, dk_ref, dv_ref, own_ref, wq_ref, wk_ref, wv_ref, gain_ref,
-               shift_ref, mgrad_ref, igrad_ref, narrow_ref, *rest):
+    def kernel(spot, x_ref, dq_ref, dk_ref, dv_ref, own_ref, wq_ref, wk_ref, wv_ref,
+               lines_ref, mgrad_ref, *rest):
+        igrad_ref, narrow_ref, *rest = rest[len(after) :]
+        gain, shift = lines_ref[0:1, :], lines_ref[1:2, :]
         if tiles:
-            packs, (gq_ref, gk_ref, gv_ref, high_ref) = rest[:2], rest[2:]
+            packs, (gq_ref, gk_ref, gv_ref, high_ref) = rest[:4], rest[4:]
         else:
             gq_ref, gk_ref, gv_ref = rest
         step_id = pl.program_id(0)
@@ -646,7 +793,7 @@
                 ref[...] = jnp.zeros_like(ref)
 
         unit, scale = norm_parts(x_ref[0].astype(F32))
-        flipped = (unit * gain_ref[...] + shift_ref[...]).astype(BF16).T
+        flipped = (unit * gain + shift).astype(BF16).T
         back = dot(dq_ref[0], wq_ref[...], 1, 1)
         gq_ref[...] += dot(flipped, dq_ref[0])
         for k, (direct, w_ref, g_ref) in enumerate(
@@ -664,7 +811,7 @@
             back = back + dot(act, w_ref[...], 1, 1)
         narrow_ref[0:1, :] += jnp.sum(back * unit, 0, keepdims=True)
         narrow_ref[1:2, :] += jnp.sum(back, 0, keepdims=True)
-        igrad_ref[0] = mgrad_ref[0] + norm_back(back, unit, scale, gain_ref[...])
+        igrad_ref[0] = mgrad_ref[0] + norm_back(back, unit, scale, gain)
 
         if tiles:
 
@@ -689,8 +836,9 @@
     out_specs = [each(block), full((8, width))]
     scratch = []
     if tiles:
-        out_shape += [jax.ShapeDtypeStruct((len(names), half, 128), BF16) for names in orders]
-        out_specs += [full((len(names), half, 128)) for names in orders]
+        packed_shapes = [(len(names) // 2, half, 128) for names in orders for _ in range(2)]
+        out_shape += [jax.ShapeDtypeStruct(shape, BF16) for shape in packed_shapes]
+        out_specs += [pl.BlockSpec(memory_space=pltpu.VMEM)] * 4
         scratch = [pltpu.VMEM(square, F32)] * 3 + [pltpu.VMEM((VEC_ROWS, width), F32)]
     else:
         out_shape += [jax.ShapeDtypeStruct(square, F32)] * 3
@@ -702,12 +850,12 @@
         + [each(block)] * 4
         + [each(owned.shape)]
         + [full(square)] * 3
-        + [full((1, width))] * 2
-        + [each(block)],
+        + [full(narrow.shape), each(block)]
+        + [pl.BlockSpec(memory_space=pl.ANY)] * len(after),
         out_specs=out_specs,
         out_shape=out_shape,
         scratch_shapes=scratch,
-    )(place(), inputs, d_query, d_keys, d_values, owned, *weights, gain, shift, middle_grad)
+    )(place(), inputs, d_query, d_keys, d_values, owned, *weights, narrow, middle_grad, *after)
 
 
 def local(
@@ -730,34 +878,43 @@
     shards = [query_weight, key_weight, value_weight, out_weight, up_weight, down_weight]
     slices = [norm1_gain, norm1_bias, norm2_gain, norm2_bias, out_bias, up_bias, down_bias]
     tiles = whole_tiles(shards, slices)
-    wide, gathered = gather_weights(shards, slices)
-    w_query, w_key, w_value, w_out, w_up, w_down = wide
-    gain_one, bias_one, gain_two, bias_two, bias_out, bias_up, bias_down = [
-        member.astype(F32)[None] for member in gathered
-    ]
     count, rows, width = inputs.shape
-    qkv, pooled = project(inputs, w_query, w_key, w_value, gain_one, bias_one)
+    wide, lines, early, late = [None] * 6, (), (), ()
+    if tiles:
+        state = gather_outer(pack_shards(shards[:3], slices))
+        other = gather_outer(pack_shards(shards[3:], [], state))
+        early = gather_inner(state)
+        late = gather_inner(other)
+    else:
+        wide, members = gather_plain(shards, slices)
+        blank = jnp.zeros((NARROW - 6, width), F32)
+        lines = (
+            jnp.concatenate([jnp.stack([members[k] for k in (0, 1, 2, 3, 4, 6)]), blank]),
+            members[5][None],
+        )
+    qkv, pooled, w_query, w_key, w_value, narrow, long_bias = project(
+        inputs, shards[:3], slices, early, wide[:3], lines, tiles
+    )
     summaries = jnp.transpose(gather_seq(pooled), (1, 0, 2, 3)).reshape(count, -1, 2 * width)
     here = lax.axis_index("seq")
     marks = jnp.array([s for s, _ in relative_ids(seq_stages())], jnp.int32)
     visible = jnp.repeat((marks ^ here) < here, 2).astype(F32)
     visible = jnp.broadcast_to(visible[:, None], (visible.shape[0], rows))
-    mixed, lse, middle = attend(qkv, summaries, visible, inputs, w_out, bias_out)
+    mixed, lse = attend(qkv, summaries, visible)
     outputs, middle_grad, mixed_grad, narrow_two, wide_two, *second = feed(
-        middle,
-        cotangent,
-        mixed,
-        w_out,
-        w_up,
-        w_down,
-        gain_two,
-        bias_two,
-        bias_up,
-        bias_down,
-        shards[3:],
-        tiles,
+        inputs, cotangent, mixed, narrow, long_bias, late, wide[3:], shards[3:], tiles
     )
-    d_query, d_keys, d_values, terms = attend_back(qkv, summaries, visible, lse, mixed_grad)
+    ties = []
+    if tiles:
+        second = reduce_step([tuple(second[:2]), tuple(second[2:])], 0)
+        ties = [member for couple in second for member in couple]
+    begun = attend_back(qkv, summaries, visible, lse, mixed_grad, 0, count // 2)
+    d_query, d_keys, d_values, terms = attend_back(
+        qkv, summaries, visible, lse, mixed_grad, count // 2, count - count // 2, begun, ties
+    )
+    if tiles:
+        second = reduce_step(second, 1)
+        ties = [member for couple in second for member in couple]
     terms = jnp.transpose(terms.reshape(count, -1, 2, 2 * width), (1, 0, 2, 3))
     owned = reduce_seq(terms)
     input_grad, narrow_one, *first = project_back(
@@ -767,18 +924,21 @@
         d_values,
         owned,
         (w_query, w_key, w_value),
-        gain_one,
-        bias_one,
+        narrow,
         middle_grad,
         shards[:3],
         tiles,
+        ties,
     )
     if tiles:
+        second = reduce_step(second, 2, True)
+        first = reduce_step([tuple(first[:2]), tuple(first[2:])], 0)
+        first = reduce_step(reduce_step(first, 1), 2, True)
+        *matrices, lines_two, lines_one = reduce_end([((3, 4, 5), second), ((0, 1, 2), first)], shards)
         size = norm1_gain.shape[0]
-        tail = reduce_group(shards[3:], second, [size] * 4 + [up_bias.shape[0]])
-        front = reduce_group(shards[:3], first, [size] * 2)
-        matrices = front[:3] + tail[:3]
-        vectors = front[3:] + tail[3:6] + [tail[7], tail[6]]
+        tail = own_parts(lines_two, [size] * 4 + [up_bias.shape[0]])
+        front = own_parts(lines_one, [size] * 2)
+        vectors = front + tail[:3] + [tail[4], tail[3]]
     else:
         vectors = [
             narrow_one[0],

time: 259 us -> 249 us (0.961)
  starting transfers between devices: 61.1 us -> 40.4 us
  other arithmetic: 8.32 us -> 14.2 us
  Pallas kernels: 79.6 us -> 83.5 us
  waiting for transfers between devices: 85.1 us -> 88.5 us
  local copies, waits for them, and re-layouts: 23 us -> 19.8 us
    ppermute x46 -> x40, starting transfers between devices: 61.1 us -> 40.4 us  [swap(): return lax.ppermute(array, axis, [(i, i ^ bit) for i in range(count)])]
    concatenate x2 -> x0, local copies, waits for them, and re-layouts: 4.8 us -> none  [the longest x1 4.79 us: gather_group(): flat = jnp.concatenate(vectors).reshape(-1, 128)]
    convert_element_type x6 -> x0, local copies, waits for them, and re-layouts: 3.84 us -> none  [local(): member.astype(F32)[None]]
    pallas_call x4 -> x8, Pallas kernels: 26.6 us -> 30 us  [the longest x2 14.2 us: attend_back(): pl.pallas_call(kernel, grid=(number,), in_specs=[each(qkv.shape), each(su...]
    ppermute x46 -> x40, waiting for transfers between devices: 85.1 us -> 88.5 us  [swap(): return lax.ppermute(array, axis, [(i, i ^ bit) for i in range(count)])]
    convert_element_type x16 -> x8, other arithmetic: 1.6 us -> 4.79 us  [add_low(): return (mine.astype(F32) + theirs.astype(F32)).astype(BF16)]
    concatenate x10 -> x8, other arithmetic: 1.56 us -> 4.42 us  [the longest x4 4.27 us: gather_outer(): state = jnp.concatenate([state, swap(state, *stage)], 0)]
    slice x20 -> x10, local copies, waits for them, and re-layouts: 3.96 us -> 6.3 us  [the longest x7 5.38 us: reduce_step(): done.append((state[:count], state[count:]))]
  transfers between devices with their start and end apart: 46 -> 40, of which waited for: 30 -> 23; matrix products, arithmetic and copies ran while one was open for 6% -> 5% of each run, Pallas kernels for 4% -> 9%
where the time goes in v1:
time: 249 us; the launch traced here: 248 us
  waiting for transfers between devices  88.5 us (36%)
  Pallas kernels  83.5 us (34%)
  starting transfers between devices  40.4 us (16%)
  local copies, waits for them, and re-layouts  19.8 us (8%)
  other arithmetic  14.2 us (6%)
    ppermute x40, waiting for transfers between devices, swap(): return lax.ppermute(array, axis, [(i, i ^ bit) for i in range(count)])  88.5 us
    ppermute x40, starting transfers between devices, swap(): return lax.ppermute(array, axis, [(i, i ^ bit) for i in range(count)])  40.4 us
    pallas_call x1, Pallas kernels, feed(): pl.pallas_call(kernel, grid=(count,), in_specs=[pl.BlockSpec(memory_space...  35.3 us
    pallas_call x2, Pallas kernels, attend_back(): pl.pallas_call(kernel, grid=(number,), in_specs=[each(qkv.shape), each(su...  14.2 us
    pallas_call x1, Pallas kernels, project_back(): pl.pallas_call(kernel, grid=(count,), in_specs=[pl.BlockSpec(memory_space...  10.5 us
    pallas_call x1, Pallas kernels, attend(): pl.pallas_call(kernel, grid=(count,), in_specs=[each(qkv.shape), each(sum...  7.61 us
    pallas_call x1, Pallas kernels, project(): pl.pallas_call(kernel, grid=(count,), in_specs=[pl.BlockSpec(memory_space...  6.6 us
    unnamed x56, local copies, waits for them, and re-layouts  5.96 us
  transfers between devices with their start and end apart: 40, of which 23 were waited for; matrix products, arithmetic and copies ran while one was open for 5% of the time, Pallas kernels for 9%

profile of v1, /device:TPU:0, one launch (start us, length us, event | category | flops | bytes accessed | tf_op | source)
XLA Modules:
  0.0 247.6 jit_solution(3896534977850698407)
XLA Ops:
  1.2 1.5 shard_map.271
  2.8 4.1 %collective-permute-start = (bf16[1,224,128]{2,1,0:T(8,128)(2,1)}, bf16[1,224,128]{2,1,0:T(8,128)(2,1)S(1)}, u32[]{:S(2)}, u32[]{:S(2)}) collective-permute-start(bf16[1,224,128]{2,1,0:T(8,128)(2,1)} %shard_map.271), channel_id=1, source_target_pairs={{0,4},{1,5},{2,6},{3,7},{4,0},{5,1},{6,2},{7,3},{8,12},{9,13},{10,... | collective-permute-start | bytes 172040 | tf_op jit(solution)/shard_map/ppermute | solution.py:17
  6.8 3.0 %collective-permute-done = bf16[1,224,128]{2,1,0:T(8,128)(2,1)S(1)} collective-permute-done((bf16[1,224,128]{2,1,0:T(8,128)(2,1)}, bf16[1,224,128]{2,1,0:T(8,128)(2,1)S(1)}, u32[]{:S(2)}, u32[]{:S(2)}) %collective-permute-start) | collective-permute-done | bytes 57376 | tf_op jit(solution)/shard_map/ppermute | solution.py:17
  12.0 3.5 %collective-permute-done.1 = bf16[2,224,128]{2,1,0:T(8,128)(2,1)S(1)} collective-permute-done((bf16[2,224,128]{2,1,0:T(8,128)(2,1)S(1)}, bf16[2,224,128]{2,1,0:T(8,128)(2,1)S(1)}, u32[]{:S(2)}, u32[]{:S(2)}) %collective-permute-start.1) | collective-permute-done | bytes 114720 | tf_op jit(solution)/shard_map/ppermute | solution.py:17
  15.5 1.5 pad_maximum_fusion.8.refs_3_
  17.0 1.6 shard_map.274
  18.6 2.5 collective-permute-start.13
  21.1 5.4 %collective-permute-done.13 = bf16[1,576,128]{2,1,0:T(8,128)(2,1)S(1)} collective-permute-done((bf16[1,576,128]{2,1,0:T(8,128)(2,1)}, bf16[1,576,128]{2,1,0:T(8,128)(2,1)S(1)}, u32[]{:S(2)}, u32[]{:S(2)}) %collective-permute-start.13) | collective-permute-done | bytes 147488 | tf_op jit(solution)/shard_map/ppermute | solution.py:17
  28.1 6.1 %collective-permute-done.14 = bf16[2,576,128]{2,1,0:T(8,128)(2,1)S(1)} collective-permute-done((bf16[2,576,128]{2,1,0:T(8,128)(2,1)S(1)}, bf16[2,576,128]{2,1,0:T(8,128)(2,1)S(1)}, u32[]{:S(2)}, u32[]{:S(2)}) %collective-permute-start.14) | collective-permute-done | bytes 294944 | tf_op jit(solution)/shard_map/ppermute | solution.py:17
  35.2 1.8 collective-permute-start.15
  37.0 1.6 collective-permute-start.6
  39.4 3.7 %collective-permute-done.6 = bf16[4,112,128]{2,1,0:T(8,128)(2,1)S(1)} collective-permute-done((bf16[4,112,128]{2,1,0:T(8,128)(2,1)S(1)}, bf16[4,112,128]{2,1,0:T(8,128)(2,1)S(1)}, u32[]{:S(2)}, u32[]{:S(2)}) %collective-permute-start.6) | collective-permute-done | bytes 114720 | tf_op jit(solution)/shard_map/ppermute | solution.py:17
  43.5 1.6 collective-permute-done.15
  45.2 1.8 collective-permute-start.17
  47.0 2.4 collective-permute-done.19
  49.9 1.8 collective-permute-start.4
  52.5 8.4 %collective-permute-done.4.refs_2_ = bf16[8,112,128]{2,1,0:T(8,128)(2,1)S(1)} collective-permute-done((bf16[8,112,128]{2,1,0:T(8,128)(2,1)S(1)}, bf16[8,112,128]{2,1,0:T(8,128)(2,1)S(1)}, u32[]{:S(2)}, u32[]{:S(2)}) %collective-permute-start.4) | collective-permute-done | bytes 229408 | tf_op jit(solution)/shard_map/ppermute | solution.py:17
  63.9 6.6 %shard_map.272 = (bf16[4,256,1536]{2,1,0:T(8,128)(2,1)}, bf16[4,2,1024]{2,1,0:T(2,128)(2,1)}, bf16[512,512]{1,0:T(8,128)(2,1)}, bf16[512,512]{1,0:T(8,128)(2,1)}...) custom-call(s32[2]{0:T(128)} %pad_add_fusion.spot, bf16[4,256,512]{2,1,0:T(8,128)(2,1)} %x_ref.5, ...), custom_call_target="tpu_custom_call" | custom-call | tf_op jit(solution)/shard_map/pallas_call | solution.py:479
  70.5 2.2 collective-permute-start.10
  73.8 1.7 collective-permute-done.10
  77.2 3.0 %collective-permute-done.11 = bf16[2,4,2,1024]{3,2,1,0:T(2,128)(2,1)S(1)} collective-permute-done((bf16[2,4,2,1024]{3,2,1,0:T(2,128)(2,1)S(1)}, bf16[2,4,2,1024]{3,2,1,0:T(2,128)(2,1)S(1)}, u32[]{:S(2)}, u32[]{:S(2)}) %collective-permute-start.11) | collective-permute-done | bytes 32800 | tf_op jit(solution)/shard_map/ppermute | solution.py:17
  81.0 1.6 collective-permute-start.12
  82.7 2.6 %collective-permute-done.12 = bf16[4,4,2,1024]{3,2,1,0:T(2,128)(2,1)S(1)} collective-permute-done((bf16[4,4,2,1024]{3,2,1,0:T(2,128)(2,1)S(1)}, bf16[4,4,2,1024]{3,2,1,0:T(2,128)(2,1)S(1)}, u32[]{:S(2)}, u32[]{:S(2)}) %collective-permute-start.12) | collective-permute-done | bytes 65568 | tf_op jit(solution)/shard_map/ppermute | solution.py:17
  87.7 7.6 %shard_map.273 = (bf16[4,256,512]{2,1,0:T(8,128)(2,1)}, f32[4,8,256]{2,1,0:T(8,128)}) custom-call(bf16[4,256,1536]{2,1,0:T(8,128)(2,1)} %get-tuple-element.56.qkv_ref, bf16[4,16,1024]{2,1,0:T(8,128)(2,1)} %reshape.52.sum_ref, f32[16,256]{1,0:T(8,128)} %broadcast_in_dim.14.vis_ref), custom_call_target="tpu_custom_call" | custom-call | tf_op jit(solution)/shard_map/pallas_call | solution.py:544
  96.2 35.3 %shard_map.275 = (bf16[4,256,512]{2,1,0:T(8,128)(2,1)}, f32[4,256,512]{2,1,0:T(8,128)}, bf16[4,256,512]{2,1,0:T(8,128)(2,1)}, f32[8,512]{1,0:T(8,128)}, f32[8,20...) custom-call(s32[2]{0:T(128)} %pad_add_fusion.spot, ...), custom_call_target="tpu_custom_call" | custom-call | tf_op jit(solution)/shard_map/pallas_call | solution.py:685
  132.1 7.0 %shard_map.276 = (bf16[4,256,512]{2,1,0:T(8,128)(2,1)}, f32[4,256,512]{2,1,0:T(8,128)}, f32[4,256,512]{2,1,0:T(8,128)}, bf16[4,16,1024]{2,1,0:T(8,128)(2,1)}) custom-call(bf16[4,256,1536]{2,1,0:T(8,128)(2,1)} %get-tuple-element.56.qkv_ref, bf16[4,16,1024]{2,1,0:T(8,128)(2,1)} %reshape.52.sum_ref, f32[16,256]{1,0:T(8,128)} %broadcast_in_dim.14.vis_ref, ...), custom_call_target="tpu_custom_call" | custom-call | tf_op jit(solution)/shard_map/pallas_call | solution.py:747
  140.3 1.5 add_convert_fusion.1
  143.6 1.6 add_convert_fusion
  146.4 7.2 %shard_map.277 = (bf16[4,256,512]{2,1,0:T(8,128)(2,1)}, f32[4,256,512]{2,1,0:T(8,128)}, f32[4,256,512]{2,1,0:T(8,128)}, bf16[4,16,1024]{2,1,0:T(8,128)(2,1)}) custom-call(bf16[4,256,1536]{2,1,0:T(8,128)(2,1)} %get-tuple-element.56.qkv_ref, ...), custom_call_target="tpu_custom_call", output_to_operand_aliasing={{0}: (5, {}), {1}: (6, {}), {2}: (7, {}), {3}: (8, {})} | custom-call | tf_op jit(solution)/shard_map/pallas_call | solution.py:747
  154.8 1.6 collective-permute-start.25
  156.9 2.4 collective-permute-done.25
  160.3 3.0 %collective-permute-done.26 = bf16[2,4,2,1024]{3,2,1,0:T(2,128)(2,1)S(1)} collective-permute-done((bf16[2,4,2,1024]{3,2,1,0:T(2,128)(2,1)S(1)}, bf16[2,4,2,1024]{3,2,1,0:T(2,128)(2,1)S(1)}, u32[]{:S(2)}, u32[]{:S(2)}) %collective-permute-start.26) | collective-permute-done | bytes 32800 | tf_op jit(solution)/shard_map/ppermute | solution.py:17
  163.4 2.2 collective-permute-start.27
  168.8 3.7 %collective-permute-done.29 = bf16[8,304,128]{2,1,0:T(8,128)(2,1)S(1)} collective-permute-done((bf16[8,304,128]{2,1,0:T(8,128)(2,1)}, bf16[8,304,128]{2,1,0:T(8,128)(2,1)S(1)}, u32[]{:S(2)}, u32[]{:S(2)}) %collective-permute-start.29) | collective-permute-done | bytes 622624 | tf_op jit(solution)/shard_map/ppermute | solution.py:17
  173.6 5.6 %collective-permute-done.28 = bf16[8,304,128]{2,1,0:T(8,128)(2,1)S(1)} collective-permute-done((bf16[8,304,128]{2,1,0:T(8,128)(2,1)S(1)}, bf16[8,304,128]{2,1,0:T(8,128)(2,1)S(1)}, u32[]{:S(2)}, u32[]{:S(2)}) %collective-permute-start.28) | collective-permute-done | bytes 622624 | tf_op jit(solution)/shard_map/ppermute | solution.py:17
  180.2 10.5 %shard_map.278 = (f32[4,256,512]{2,1,0:T(8,128)}, f32[8,512]{1,0:T(8,128)}, bf16[16,112,128]{2,1,0:T(8,128)(2,1)}, bf16[16,112,128]{2,1,0:T(8,128)(2,1)}, bf16[1...) custom-call(s32[2]{0:T(128)} %pad_add_fusion.spot, bf16[4,256,512]{2,1,0:T(8,128)(2,1)} %x_ref.5, ...), custom_call_target="tpu_custom_call" | custom-call | tf_op jit(solution)/shard_map/pallas_call | solution.py:846
  190.8 1.6 collective-permute-start.31
  192.4 1.5 collective-permute-start.30
  196.7 1.5 collective-permute-start.33
  198.2 8.6 %collective-permute-done.36 = bf16[8,112,128]{2,1,0:T(8,128)(2,1)S(1)} collective-permute-done((bf16[8,112,128]{2,1,0:T(8,128)(2,1)S(1)}, bf16[8,112,128]{2,1,0:T(8,128)(2,1)S(1)}, u32[]{:S(2)}, u32[]{:S(2)}) %collective-permute-start.36) | collective-permute-done | bytes 229408 | tf_op jit(solution)/shard_map/ppermute | solution.py:17
  208.8 1.5 collective-permute-start.34
  210.3 2.0 collective-permute-done.37.refs_7_
  214.2 2.4 shard_map.279
  216.6 1.7 collective-permute-start.38
  218.3 8.4 %collective-permute-done.38.theirs_ref = bf16[2,832,128]{2,1,0:T(8,128)(2,1)S(1)} collective-permute-done((bf16[2,832,128]{2,1,0:T(8,128)(2,1)}, bf16[2,832,128]{2,1,0:T(8,128)(2,1)S(1)}, u32[]{:S(2)}, u32[]{:S(2)}) %collective-permute-start.38) | collective-permute-done | bytes 426016 | tf_op jit(solution)/shard_map/ppermute | solution.py:17
  227.5 1.9 shard_map.280
  230.2 9.3 %collective-permute-done.39.theirs_ref = bf16[1,832,128]{2,1,0:T(8,128)(2,1)S(1)} collective-permute-done((bf16[1,832,128]{2,1,0:T(8,128)(2,1)}, bf16[1,832,128]{2,1,0:T(8,128)(2,1)S(1)}, u32[]{:S(2)}, u32[]{:S(2)}) %collective-permute-start.39) | collective-permute-done | bytes 213024 | tf_op jit(solution)/shard_map/ppermute | solution.py:17
  240.2 1.8 shard_map.281
  (158 shorter events, 45.0 us)
Async XLA Ops:
  2.8 7.0 %collective-permute-start = (bf16[1,224,128]{2,1,0:T(8,128)(2,1)}, bf16[1,224,128]{2,1,0:T(8,128)(2,1)S(1)}, u32[]{:S(2)}, u32[]{:S(2)}) collective-permute-start(bf16[1,224,128]{2,1,0:T(8,128)(2,1)} %shard_map.271), channel_id=1, source_target_pairs={{0,4},{1,5},{2,6},{3,7},{4,0},{5,1},{6,2},{7,3},{8,12},{9,13},{10,... | collective-permute-start | bytes 172040 | tf_op jit(solution)/shard_map/ppermute | solution.py:17
  10.6 4.9 %collective-permute-start.1 = (bf16[2,224,128]{2,1,0:T(8,128)(2,1)S(1)}, bf16[2,224,128]{2,1,0:T(8,128)(2,1)S(1)}, u32[]{:S(2)}, u32[]{:S(2)}) collective-permute-start(bf16[2,224,128]{2,1,0:T(8,128)(2,1)S(1)} %pad_maximum_fusion.12), channel_id=1, source_target_pairs={{0,2},{1,3},{2,0},{3,1},{4,6},{5,7},{6,4},{7,5},{8,10},{9,11},{10,... | collective-permute-start | bytes 344072 | tf_op jit(solution)/shard_map/ppermute | solution.py:17
  18.6 7.8 %collective-permute-start.13 = (bf16[1,576,128]{2,1,0:T(8,128)(2,1)}, bf16[1,576,128]{2,1,0:T(8,128)(2,1)S(1)}, u32[]{:S(2)}, u32[]{:S(2)}) collective-permute-start(bf16[1,576,128]{2,1,0:T(8,128)(2,1)} %shard_map.274), channel_id=1, source_target_pairs={{0,4},{1,5},{2,6},{3,7},{4,0},{5,1},{6,2},{7,3},{8,12},{9,13},{10,... | collective-permute-start | bytes 442376 | tf_op jit(solution)/shard_map/ppermute | solution.py:17
  27.4 6.8 %collective-permute-start.14 = (bf16[2,576,128]{2,1,0:T(8,128)(2,1)S(1)}, bf16[2,576,128]{2,1,0:T(8,128)(2,1)S(1)}, u32[]{:S(2)}, u32[]{:S(2)}) collective-permute-start(bf16[2,576,128]{2,1,0:T(8,128)(2,1)S(1)} %pad_maximum_fusion.5), channel_id=1, source_target_pairs={{0,2},{1,3},{2,0},{3,1},{4,6},{5,7},{6,4},{7,5},{8,10},{9,11},{10,... | collective-permute-start | bytes 884744 | tf_op jit(solution)/shard_map/ppermute | solution.py:17
  35.2 9.9 %collective-permute-start.15 = (bf16[4,288,128]{2,1,0:T(8,128)(2,1)S(1)}, bf16[4,288,128]{2,1,0:T(8,128)(2,1)S(1)}, u32[]{:S(2)}, u32[]{:S(2)}) collective-permute-start(bf16[4,288,128]{2,1,0:T(8,128)(2,1)S(1)} %get-tuple-element.112), channel_id=1, source_target_pairs={{0,16},{8,24},{16,0},{24,8},{1,17},{9,25},{17,1},{25,9},{2,18},{10... | collective-permute-start | bytes 884744 | tf_op jit(solution)/shard_map/ppermute | solution.py:17
  37.0 6.1 %collective-permute-start.6 = (bf16[4,112,128]{2,1,0:T(8,128)(2,1)S(1)}, bf16[4,112,128]{2,1,0:T(8,128)(2,1)S(1)}, u32[]{:S(2)}, u32[]{:S(2)}) collective-permute-start(bf16[4,112,128]{2,1,0:T(8,128)(2,1)S(1)} %get-tuple-element.119), channel_id=1, source_target_pairs={{0,1},{1,0},{2,3},{3,2},{4,5},{5,4},{6,7},{7,6},{8,9},{9,8},{10,11... | collective-permute-start | bytes 344072 | tf_op jit(solution)/shard_map/ppermute | solution.py:17
  38.6 10.8 %collective-permute-start.19 = (bf16[4,288,128]{2,1,0:T(8,128)(2,1)S(1)}, bf16[4,288,128]{2,1,0:T(8,128)(2,1)S(1)}, u32[]{:S(2)}, u32[]{:S(2)}) collective-permute-start(bf16[4,288,128]{2,1,0:T(8,128)(2,1)S(1)} %get-tuple-element.111), channel_id=1, source_target_pairs={{0,1},{1,0},{2,3},{3,2},{4,5},{5,4},{6,7},{7,6},{8,9},{9,8},{10,11... | collective-permute-start | bytes 884744 | tf_op jit(solution)/shard_map/ppermute | solution.py:17
  39.1 10.7 %collective-permute-start.2 = (bf16[4,112,128]{2,1,0:T(8,128)(2,1)S(1)}, bf16[4,112,128]{2,1,0:T(8,128)(2,1)S(1)}, u32[]{:S(2)}, u32[]{:S(2)}) collective-permute-start(bf16[4,112,128]{2,1,0:T(8,128)(2,1)S(1)} %get-tuple-element.120), channel_id=1, source_target_pairs={{0,16},{8,24},{16,0},{24,8},{1,17},{9,25},{17,1},{25,9},{2,18},{10... | collective-permute-start | bytes 344072 | tf_op jit(solution)/shard_map/ppermute | solution.py:17
  43.1 9.4 %collective-permute-start.8 = (bf16[8,112,128]{2,1,0:T(8,128)(2,1)S(1)}, bf16[8,112,128]{2,1,0:T(8,128)(2,1)S(1)}, u32[]{:S(2)}, u32[]{:S(2)}) collective-permute-start(bf16[8,112,128]{2,1,0:T(8,128)(2,1)S(1)} %pad_maximum_fusion.10.refs_4_), channel_id=1, source_target_pairs={{0,16},{8,24},{16,0},{24,8},{1,17},{9,25},{17,1},{25,9},{2,18},{10... | collective-permute-start | bytes 688136 | tf_op jit(solution)/shard_map/ppermute | solution.py:17
  45.2 27.5 %copy-start.1 = (bf16[8,288,128]{2,1,0:T(8,128)(2,1)}, bf16[8,288,128]{2,1,0:T(8,128)(2,1)S(1)}, u32[]{:S(2)}) copy-start(bf16[8,288,128]{2,1,0:T(8,128)(2,1)S(1)} %pad_maximum_fusion.3.rest_0_) | copy-start | bytes 1769476
  45.2 28.0 %collective-permute-start.17 = (bf16[8,288,128]{2,1,0:T(8,128)(2,1)S(1)}, bf16[8,288,128]{2,1,0:T(8,128)(2,1)S(1)}, u32[]{:S(2)}, u32[]{:S(2)}) collective-permute-start(bf16[8,288,128]{2,1,0:T(8,128)(2,1)S(1)} %pad_maximum_fusion.3.rest_0_), channel_id=1, source_target_pairs={{0,1},{1,0},{2,3},{3,2},{4,5},{5,4},{6,7},{7,6},{8,9},{9,8},{10,11... | collective-permute-start | bytes 1769480 | tf_op jit(solution)/shard_map/ppermute | solution.py:17
  49.5 23.3 %copy-start.2 = (bf16[8,288,128]{2,1,0:T(8,128)(2,1)}, bf16[8,288,128]{2,1,0:T(8,128)(2,1)S(1)}, u32[]{:S(2)}) copy-start(bf16[8,288,128]{2,1,0:T(8,128)(2,1)S(1)} %pad_maximum_fusion.4.rest_4_) | copy-start | bytes 1769476
  49.5 23.8 %collective-permute-start.21 = (bf16[8,288,128]{2,1,0:T(8,128)(2,1)S(1)}, bf16[8,288,128]{2,1,0:T(8,128)(2,1)S(1)}, u32[]{:S(2)}, u32[]{:S(2)}) collective-permute-start(bf16[8,288,128]{2,1,0:T(8,128)(2,1)S(1)} %pad_maximum_fusion.4.rest_4_), channel_id=1, source_target_pairs={{0,16},{8,24},{16,0},{24,8},{1,17},{9,25},{17,1},{25,9},{2,18},{10... | collective-permute-start | bytes 1769480 | tf_op jit(solution)/shard_map/ppermute | solution.py:17
  49.9 13.3 %copy-start.10 = (bf16[8,112,128]{2,1,0:T(8,128)(2,1)}, bf16[8,112,128]{2,1,0:T(8,128)(2,1)S(1)}, u32[]{:S(2)}) copy-start(bf16[8,112,128]{2,1,0:T(8,128)(2,1)S(1)} %pad_maximum_fusion.9.refs_0_) | copy-start | bytes 688132
  49.9 32.7 %copy-start.27 = (s32[8]{0:T(128)S(1)}, s32[8]{0:T(128)}, u32[]{:S(2)}) copy-start(s32[8]{0:T(128)} %constant.44.clone) | copy-start | bytes 100
  49.9 11.1 %collective-permute-start.4 = (bf16[8,112,128]{2,1,0:T(8,128)(2,1)S(1)}, bf16[8,112,128]{2,1,0:T(8,128)(2,1)S(1)}, u32[]{:S(2)}, u32[]{:S(2)}) collective-permute-start(bf16[8,112,128]{2,1,0:T(8,128)(2,1)S(1)} %pad_maximum_fusion.9.refs_0_), channel_id=1, source_target_pairs={{0,1},{1,0},{2,3},{3,2},{4,5},{5,4},{6,7},{7,6},{8,9},{9,8},{10,11... | collective-permute-start | bytes 688136 | tf_op jit(solution)/shard_map/ppermute | solution.py:17
  51.7 9.2 %collective-permute-start.7 = (bf16[8,112,128]{2,1,0:T(8,128)(2,1)S(1)}, bf16[8,112,128]{2,1,0:T(8,128)(2,1)S(1)}, u32[]{:S(2)}, u32[]{:S(2)}) collective-permute-start(bf16[8,112,128]{2,1,0:T(8,128)(2,1)S(1)} %pad_maximum_fusion.10.refs_4_), channel_id=1, source_target_pairs={{0,8},{8,0},{16,24},{24,16},{1,9},{9,1},{17,25},{25,17},{2,10},{10... | collective-permute-start | bytes 688136 | tf_op jit(solution)/shard_map/ppermute | solution.py:17
  52.5 9.0 %collective-permute-start.3 = (bf16[8,112,128]{2,1,0:T(8,128)(2,1)S(1)}, bf16[8,112,128]{2,1,0:T(8,128)(2,1)S(1)}, u32[]{:S(2)}, u32[]{:S(2)}) collective-permute-start(bf16[8,112,128]{2,1,0:T(8,128)(2,1)S(1)} %pad_maximum_fusion.9.refs_0_), channel_id=1, source_target_pairs={{0,8},{8,0},{16,24},{24,16},{1,9},{9,1},{17,25},{25,17},{2,10},{10... | collective-permute-start | bytes 688136 | tf_op jit(solution)/shard_map/ppermute | solution.py:17
  61.0 1.5 collective-permute-start.9
  61.0 2.2 collective-permute-start.5
  70.5 5.0 %collective-permute-start.10 = (bf16[1,4,2,1024]{3,2,1,0:T(2,128)(2,1)}, bf16[1,4,2,1024]{3,2,1,0:T(2,128)(2,1)S(1)}, u32[]{:S(2)}, u32[]{:S(2)}) collective-permute-start(bf16[1,4,2,1024]{3,2,1,0:T(2,128)(2,1)} %bitcast.28), channel_id=1, source_target_pairs={{0,4},{1,5},{2,6},{3,7},{4,0},{5,1},{6,2},{7,3},{8,12},{9,13},{10,... | collective-permute-start | bytes 49160 | tf_op jit(solution)/shard_map/ppermute | solution.py:17
  72.7 22.6 %collective-permute-start.16 = (bf16[8,288,128]{2,1,0:T(8,128)(2,1)S(1)}, bf16[8,288,128]{2,1,0:T(8,128)(2,1)S(1)}, u32[]{:S(2)}, u32[]{:S(2)}) collective-permute-start(bf16[8,288,128]{2,1,0:T(8,128)(2,1)S(1)} %pad_maximum_fusion.3.rest_0_), channel_id=1, source_target_pairs={{0,8},{8,0},{16,24},{24,16},{1,9},{9,1},{17,25},{25,17},{2,10},{10... | collective-permute-start | bytes 1769480 | tf_op jit(solution)/shard_map/ppermute | solution.py:17
  72.7 22.6 %collective-permute-start.20 = (bf16[8,288,128]{2,1,0:T(8,128)(2,1)S(1)}, bf16[8,288,128]{2,1,0:T(8,128)(2,1)}, u32[]{:S(2)}, u32[]{:S(2)}) collective-permute-start(bf16[8,288,128]{2,1,0:T(8,128)(2,1)S(1)} %pad_maximum_fusion.4.rest_4_), channel_id=1, source_target_pairs={{0,8},{8,0},{16,24},{24,16},{1,9},{9,1},{17,25},{25,17},{2,10},{10... | collective-permute-start | bytes 1769480 | tf_op jit(solution)/shard_map/ppermute | solution.py:17
  73.2 22.1 %copy-start.11 = (bf16[8,288,128]{2,1,0:T(8,128)(2,1)}, bf16[8,288,128]{2,1,0:T(8,128)(2,1)S(1)}, u32[]{:S(2)}) copy-start(bf16[8,288,128]{2,1,0:T(8,128)(2,1)S(1)} %collective-permute-done.17.rest_2_) | copy-start | bytes 1769476
  73.2 22.1 %collective-permute-start.18 = (bf16[8,288,128]{2,1,0:T(8,128)(2,1)S(1)}, bf16[8,288,128]{2,1,0:T(8,128)(2,1)}, u32[]{:S(2)}, u32[]{:S(2)}) collective-permute-start(bf16[8,288,128]{2,1,0:T(8,128)(2,1)S(1)} %collective-permute-done.17.rest_2_), channel_id=1, source_target_pairs={{0,8},{8,0},{16,24},{24,16},{1,9},{9,1},{17,25},{25,17},{2,10},{10... | collective-permute-start | bytes 1769480 | tf_op jit(solution)/shard_map/ppermute | solution.py:17
  73.3 22.0 %copy-start.12 = (bf16[8,288,128]{2,1,0:T(8,128)(2,1)}, bf16[8,288,128]{2,1,0:T(8,128)(2,1)S(1)}, u32[]{:S(2)}) copy-start(bf16[8,288,128]{2,1,0:T(8,128)(2,1)S(1)} %collective-permute-done.21.rest_6_) | copy-start | bytes 1769476
  73.3 22.1 %collective-permute-start.22 = (bf16[8,288,128]{2,1,0:T(8,128)(2,1)S(1)}, bf16[8,288,128]{2,1,0:T(8,128)(2,1)}, u32[]{:S(2)}, u32[]{:S(2)}) collective-permute-start(bf16[8,288,128]{2,1,0:T(8,128)(2,1)S(1)} %collective-permute-done.21.rest_6_), channel_id=1, source_target_pairs={{0,8},{8,0},{16,24},{24,16},{1,9},{9,1},{17,25},{25,17},{2,10},{10... | collective-permute-start | bytes 1769480 | tf_op jit(solution)/shard_map/ppermute | solution.py:17
  76.2 4.0 %collective-permute-start.11 = (bf16[2,4,2,1024]{3,2,1,0:T(2,128)(2,1)S(1)}, bf16[2,4,2,1024]{3,2,1,0:T(2,128)(2,1)S(1)}, u32[]{:S(2)}, u32[]{:S(2)}) collective-permute-start(bf16[2,4,2,1024]{3,2,1,0:T(2,128)(2,1)S(1)} %pad_maximum_fusion.14), channel_id=1, source_target_pairs={{0,2},{1,3},{2,0},{3,1},{4,6},{5,7},{6,4},{7,5},{8,10},{9,11},{10,... | collective-permute-start | bytes 98312 | tf_op jit(solution)/shard_map/ppermute | solution.py:17
  81.0 4.3 %collective-permute-start.12 = (bf16[4,4,2,1024]{3,2,1,0:T(2,128)(2,1)S(1)}, bf16[4,4,2,1024]{3,2,1,0:T(2,128)(2,1)S(1)}, u32[]{:S(2)}, u32[]{:S(2)}) collective-permute-start(bf16[4,4,2,1024]{3,2,1,0:T(2,128)(2,1)S(1)} %pad_maximum_fusion.13), channel_id=1, source_target_pairs={{0,1},{1,0},{2,3},{3,2},{4,5},{5,4},{6,7},{7,6},{8,9},{9,8},{10,11... | collective-permute-start | bytes 196616 | tf_op jit(solution)/shard_map/ppermute | solution.py:17
  131.6 7.6 %collective-permute-start.24 = (bf16[16,304,128]{2,1,0:T(8,128)(2,1)}, bf16[16,304,128]{2,1,0:T(8,128)(2,1)S(1)}, u32[]{:S(2)}, u32[]{:S(2)}) collective-permute-start(bf16[16,304,128]{2,1,0:T(8,128)(2,1)} %get-tuple-element.71), channel_id=1, source_target_pairs={{0,8},{8,0},{16,24},{24,16},{1,9},{9,1},{17,25},{25,17},{2,10},{10... | collective-permute-start | bytes 3735560 | tf_op jit(solution)/shard_map/ppermute | solution.py:17
  131.6 11.5 %collective-permute-start.23 = (bf16[16,304,128]{2,1,0:T(8,128)(2,1)}, bf16[16,304,128]{2,1,0:T(8,128)(2,1)}, u32[]{:S(2)}, u32[]{:S(2)}) collective-permute-start(bf16[16,304,128]{2,1,0:T(8,128)(2,1)} %get-tuple-element.69), channel_id=1, source_target_pairs={{0,8},{8,0},{16,24},{24,16},{1,9},{9,1},{17,25},{25,17},{2,10},{10... | collective-permute-start | bytes 3735560 | tf_op jit(solution)/shard_map/ppermute | solution.py:17
  146.4 19.2 %copy-start = (bf16[8,304,128]{2,1,0:T(8,128)(2,1)S(1)}, bf16[8,304,128]{2,1,0:T(8,128)(2,1)}, u32[]{:S(2)}) copy-start(bf16[8,304,128]{2,1,0:T(8,128)(2,1)} %get-tuple-element.101.rest_5_) | copy-start | bytes 1867780
  154.8 4.5 %collective-permute-start.25 = (bf16[4,4,2,1024]{3,2,1,0:T(2,128)(2,1)S(1)}, bf16[4,4,2,1024]{3,2,1,0:T(2,128)(2,1)S(1)}, u32[]{:S(2)}, u32[]{:S(2)}) collective-permute-start(bf16[4,4,2,1024]{3,2,1,0:T(2,128)(2,1)S(1)} %slice.249), channel_id=1, source_target_pairs={{0,1},{1,0},{2,3},{3,2},{4,5},{5,4},{6,7},{7,6},{8,9},{9,8},{10,11... | collective-permute-start | bytes 196616 | tf_op jit(solution)/shard_map/ppermute | solution.py:17
  156.4 16.1 %collective-permute-start.29 = (bf16[8,304,128]{2,1,0:T(8,128)(2,1)}, bf16[8,304,128]{2,1,0:T(8,128)(2,1)S(1)}, u32[]{:S(2)}, u32[]{:S(2)}) collective-permute-start(bf16[8,304,128]{2,1,0:T(8,128)(2,1)} %get-tuple-element.99.rest_7_), channel_id=1, source_target_pairs={{0,1},{1,0},{2,3},{3,2},{4,5},{5,4},{6,7},{7,6},{8,9},{9,8},{10,11... | collective-permute-start | bytes 1867784 | tf_op jit(solution)/shard_map/ppermute | solution.py:17
  159.4 4.0 %collective-permute-start.26 = (bf16[2,4,2,1024]{3,2,1,0:T(2,128)(2,1)S(1)}, bf16[2,4,2,1024]{3,2,1,0:T(2,128)(2,1)S(1)}, u32[]{:S(2)}, u32[]{:S(2)}) collective-permute-start(bf16[2,4,2,1024]{3,2,1,0:T(2,128)(2,1)S(1)} %slice.251), channel_id=1, source_target_pairs={{0,2},{1,3},{2,0},{3,1},{4,6},{5,7},{6,4},{7,5},{8,10},{9,11},{10,... | collective-permute-start | bytes 98312 | tf_op jit(solution)/shard_map/ppermute | solution.py:17
  163.4 4.7 %collective-permute-start.27 = (bf16[1,4,2,1024]{3,2,1,0:T(2,128)(2,1)S(1)}, bf16[1,4,2,1024]{3,2,1,0:T(2,128)(2,1)S(1)}, u32[]{:S(2)}, u32[]{:S(2)}) collective-permute-start(bf16[1,4,2,1024]{3,2,1,0:T(2,128)(2,1)S(1)} %slice.253), channel_id=1, source_target_pairs={{0,4},{1,5},{2,6},{3,7},{4,0},{5,1},{6,2},{7,3},{8,12},{9,13},{10,... | collective-permute-start | bytes 49160 | tf_op jit(solution)/shard_map/ppermute | solution.py:17
  165.6 13.6 %collective-permute-start.28 = (bf16[8,304,128]{2,1,0:T(8,128)(2,1)S(1)}, bf16[8,304,128]{2,1,0:T(8,128)(2,1)S(1)}, u32[]{:S(2)}, u32[]{:S(2)}) collective-permute-start(bf16[8,304,128]{2,1,0:T(8,128)(2,1)S(1)} %copy-done), channel_id=1, source_target_pairs={{0,16},{8,24},{16,0},{24,8},{1,17},{9,25},{17,1},{25,9},{2,18},{10... | collective-permute-start | bytes 1867784 | tf_op jit(solution)/shard_map/ppermute | solution.py:17
  180.2 12.2 %copy-start.5 = (bf16[4,304,128]{2,1,0:T(8,128)(2,1)S(1)}, bf16[4,304,128]{2,1,0:T(8,128)(2,1)}, u32[]{:S(2)}) copy-start(bf16[4,304,128]{2,1,0:T(8,128)(2,1)} %get-tuple-element.109.rest_1_) | copy-start | bytes 933892
  190.8 3.2 %collective-permute-start.35 = (bf16[16,112,128]{2,1,0:T(8,128)(2,1)}, bf16[16,112,128]{2,1,0:T(8,128)(2,1)S(1)}, u32[]{:S(2)}, u32[]{:S(2)}) collective-permute-start(bf16[16,112,128]{2,1,0:T(8,128)(2,1)} %get-tuple-element.84), channel_id=1, source_target_pairs={{0,8},{8,0},{16,24},{24,16},{1,9},{9,1},{17,25},{25,17},{2,10},{10... | collective-permute-start | bytes 1376264 | tf_op jit(solution)/shard_map/ppermute | solution.py:17
  190.8 19.4 %collective-permute-start.31 = (bf16[4,304,128]{2,1,0:T(8,128)(2,1)S(1)}, bf16[4,304,128]{2,1,0:T(8,128)(2,1)S(1)}, u32[]{:S(2)}, u32[]{:S(2)}) collective-permute-start(bf16[4,304,128]{2,1,0:T(8,128)(2,1)S(1)} %copy-done.4), channel_id=1, source_target_pairs={{0,16},{8,24},{16,0},{24,8},{1,17},{9,25},{17,1},{25,9},{2,18},{10... | collective-permute-start | bytes 933896 | tf_op jit(solution)/shard_map/ppermute | solution.py:17
  192.4 17.9 %collective-permute-start.30 = (bf16[4,304,128]{2,1,0:T(8,128)(2,1)S(1)}, bf16[4,304,128]{2,1,0:T(8,128)(2,1)S(1)}, u32[]{:S(2)}, u32[]{:S(2)}) collective-permute-start(bf16[4,304,128]{2,1,0:T(8,128)(2,1)S(1)} %copy-done.5), channel_id=1, source_target_pairs={{0,1},{1,0},{2,3},{3,2},{4,5},{5,4},{6,7},{7,6},{8,9},{9,8},{10,11... | collective-permute-start | bytes 933896 | tf_op jit(solution)/shard_map/ppermute | solution.py:17
  193.9 2.6 %collective-permute-start.32 = (bf16[16,112,128]{2,1,0:T(8,128)(2,1)}, bf16[16,112,128]{2,1,0:T(8,128)(2,1)S(1)}, u32[]{:S(2)}, u32[]{:S(2)}) collective-permute-start(bf16[16,112,128]{2,1,0:T(8,128)(2,1)} %get-tuple-element.82), channel_id=1, source_target_pairs={{0,8},{8,0},{16,24},{24,16},{1,9},{9,1},{17,25},{25,17},{2,10},{10... | collective-permute-start | bytes 1376264 | tf_op jit(solution)/shard_map/ppermute | solution.py:17
  196.0 10.8 %collective-permute-start.36 = (bf16[8,112,128]{2,1,0:T(8,128)(2,1)S(1)}, bf16[8,112,128]{2,1,0:T(8,128)(2,1)S(1)}, u32[]{:S(2)}, u32[]{:S(2)}) collective-permute-start(bf16[8,112,128]{2,1,0:T(8,128)(2,1)S(1)} %pad_maximum_fusion.6), channel_id=1, source_target_pairs={{0,1},{1,0},{2,3},{3,2},{4,5},{5,4},{6,7},{7,6},{8,9},{9,8},{10,11... | collective-permute-start | bytes 688136 | tf_op jit(solution)/shard_map/ppermute | solution.py:17
  196.7 11.3 %collective-permute-start.33 = (bf16[8,112,128]{2,1,0:T(8,128)(2,1)S(1)}, bf16[8,112,128]{2,1,0:T(8,128)(2,1)S(1)}, u32[]{:S(2)}, u32[]{:S(2)}) collective-permute-start(bf16[8,112,128]{2,1,0:T(8,128)(2,1)S(1)} %slice.265), channel_id=1, source_target_pairs={{0,16},{8,24},{16,0},{24,8},{1,17},{9,25},{17,1},{25,9},{2,18},{10... | collective-permute-start | bytes 688136 | tf_op jit(solution)/shard_map/ppermute | solution.py:17
  207.5 4.8 %collective-permute-start.37 = (bf16[4,112,128]{2,1,0:T(8,128)(2,1)S(1)}, bf16[4,112,128]{2,1,0:T(8,128)(2,1)S(1)}, u32[]{:S(2)}, u32[]{:S(2)}) collective-permute-start(bf16[4,112,128]{2,1,0:T(8,128)(2,1)S(1)} %get-tuple-element.115), channel_id=1, source_target_pairs={{0,16},{8,24},{16,0},{24,8},{1,17},{9,25},{17,1},{25,9},{2,18},{10... | collective-permute-start | bytes 344072 | tf_op jit(solution)/shard_map/ppermute | solution.py:17
  208.8 4.8 %collective-permute-start.34 = (bf16[4,112,128]{2,1,0:T(8,128)(2,1)S(1)}, bf16[4,112,128]{2,1,0:T(8,128)(2,1)S(1)}, u32[]{:S(2)}, u32[]{:S(2)}) collective-permute-start(bf16[4,112,128]{2,1,0:T(8,128)(2,1)S(1)} %get-tuple-element.117), channel_id=1, source_target_pairs={{0,1},{1,0},{2,3},{3,2},{4,5},{5,4},{6,7},{7,6},{8,9},{9,8},{10,11... | collective-permute-start | bytes 344072 | tf_op jit(solution)/shard_map/ppermute | solution.py:17
  216.6 10.1 %collective-permute-start.38 = (bf16[2,832,128]{2,1,0:T(8,128)(2,1)}, bf16[2,832,128]{2,1,0:T(8,128)(2,1)S(1)}, u32[]{:S(2)}, u32[]{:S(2)}) collective-permute-start(bf16[2,832,128]{2,1,0:T(8,128)(2,1)} %get-tuple-element.86), channel_id=1, source_target_pairs={{0,2},{1,3},{2,0},{3,1},{4,6},{5,7},{6,4},{7,5},{8,10},{9,11},{10,... | collective-permute-start | bytes 1277960 | tf_op jit(solution)/shard_map/ppermute | solution.py:17
  229.4 10.1 %collective-permute-start.39 = (bf16[1,832,128]{2,1,0:T(8,128)(2,1)}, bf16[1,832,128]{2,1,0:T(8,128)(2,1)S(1)}, u32[]{:S(2)}, u32[]{:S(2)}) collective-permute-start(bf16[1,832,128]{2,1,0:T(8,128)(2,1)} %get-tuple-element.88), channel_id=1, source_target_pairs={{0,4},{1,5},{2,6},{3,7},{4,0},{5,1},{6,2},{7,3},{8,12},{9,13},{10,... | collective-permute-start | bytes 638984 | tf_op jit(solution)/shard_map/ppermute | solution.py:17
  (20 other events, 73.7 us)

commit v2 on v1

--- a/solution.py
+++ b/solution.py
@@ -4,6 +4,7 @@
 from jax.experimental import pallas as pl
 from jax.experimental.pallas import tpu as pltpu
 from jax.sharding import PartitionSpec as P
+
 
 HEADS = 8
 HEAD = 64
@@ -186,6 +187,7 @@
     arrays = [array for kept, theirs, _ in couples for array in (kept, theirs)]
     return pl.pallas_call(
         kernel,
+        cost_estimate=cost(2),
         out_shape=[jax.ShapeDtypeStruct((count // 2, rows, 128), BF16)] * 2,
         in_specs=[pl.BlockSpec(memory_space=pltpu.VMEM)] * len(arrays),
         out_specs=[pl.BlockSpec(memory_space=pltpu.VMEM)] * 2,
@@ -209,52 +211,65 @@
 
     return pl.pallas_call(
         kernel,
+        cost_estimate=cost(2),
         out_shape=[jax.ShapeDtypeStruct((count // 2, rows, 128), BF16)] * 2,
         in_specs=[pl.BlockSpec(memory_space=pltpu.VMEM)] * 2,
         out_specs=[pl.BlockSpec(memory_space=pltpu.VMEM)] * 2,
     )(kept, theirs)
 
 
-def finish(kept, theirs, parts, spans, shapes):
-    def kernel(mine_ref, theirs_ref, *outs):
+def finish(kept, theirs, parts, spans, shapes, sizes):
+    def kernel(spot, mine_ref, theirs_ref, *outs):
         total, pairs = sum_rows(mine_ref[0], theirs_ref[0], spans)
         for number, row, left, at, size in parts:
             outs[number][row : row + size, left : left + 128] = total[at : at + size]
-        for k, pair in enumerate(pairs):
-            outs[len(shapes) + k][...] = pair
+        (pair,) = pairs
+        row = 0
+        for out, size in zip(outs[len(shapes) :], sizes):
+            if size < 128:
+                line = pair[row : row + 1]
+                found = line[:, :size]
+                for k in range(1, 128 // size):
+                    part = line[:, k * size : (k + 1) * size]
+                    found = jnp.where(spot[0] % (128 // size) == k, part, found)
+                out[...] = found.reshape(size)
+                row += 1
+            else:
+                for at in range(0, size, 128):
+                    out[at : at + 128] = pair[row : row + 1].reshape(128)
+                    row += 1
 
     return pl.pallas_call(
         kernel,
+        cost_estimate=cost(2),
         out_shape=[jax.ShapeDtypeStruct(shape, F32) for shape in shapes]
-        + [jax.ShapeDtypeStruct((VEC_ROWS // 2, 128), F32)] * len(spans),
-        in_specs=[pl.BlockSpec(memory_space=pltpu.VMEM)] * 2,
-        out_specs=[pl.BlockSpec(memory_space=pltpu.VMEM)] * (len(shapes) + len(spans)),
-    )(kept, theirs)
-
-
-def reduce_end(groups, weights):
-    couples = []
+        + [jax.ShapeDtypeStruct((size,), F32) for size in sizes],
+        in_specs=[pl.BlockSpec(memory_space=pltpu.SMEM)]
+        + [pl.BlockSpec(memory_space=pltpu.VMEM)] * 2,
+        out_specs=[pl.BlockSpec(memory_space=pltpu.VMEM)] * (len(shapes) + len(sizes)),
+    )(place(), kept, theirs)
+
+
+def reduce_end(halves, weights, sizes):
+    segments = columns(weights) + [("vec", VEC_ROWS)]
     parts = []
     spans = []
     at = 0
-    for numbers, halves in groups:
-        segments = columns([weights[n] for n in numbers]) + [("vec", VEC_ROWS)]
-        for k, (kept, theirs) in enumerate(halves):
-            couples.append((kept, theirs, k == 1))
-            half = kept.shape[1]
-            for name, row, here, size in cuts(segments, k * half, half):
-                if name == "vec":
-                    spans.append(at + here)
-                else:
-                    parts.append((numbers[name[0]], row, name[1] * 128, at + here, size))
-            at += half
-    kept, sent = joined_sum(couples)
+    for k, (kept, _) in enumerate(halves):
+        half = kept.shape[1]
+        for name, row, here, size in cuts(segments, k * half, half):
+            if name == "vec":
+                spans.append(at + here)
+            else:
+                parts.append((name[0], row, name[1] * 128, at + here, size))
+        at += half
+    kept, sent = joined_sum([(kept, theirs, k == 1) for k, (kept, theirs) in enumerate(halves)])
     stages = outer_stages()[::-1]
     for k, stage in enumerate(stages):
         theirs = swap(sent, *stage)
         if k < len(stages) - 1:
             kept, sent = again(kept, theirs, spans)
-    return finish(kept, theirs, parts, spans, [w.shape for w in weights])
+    return list(finish(kept, theirs, parts, spans, [w.shape for w in weights], sizes))
 
 
 def seq_stages():
@@ -293,12 +308,6 @@
     ]
 
 
-def packed(weights):
-    return [
-        weight[:, c : c + 128] for weight in weights for c in range(0, weight.shape[1], 128)
-    ]
-
-
 def spots(weights):
     def targets(name, row, s, b):
         if name == "vec":
@@ -308,12 +317,6 @@
         return (i, s * rows + row, b * width + c * 128)
 
     return targets
-
-
-def whole(weights):
-    return [
-        (w.shape[0] * lax.axis_size("seq"), w.shape[1] * lax.axis_size("batch")) for w in weights
-    ]
 
 
 def pack_shards(weights, vectors, after=None):
@@ -362,21 +365,7 @@
     return wide, [lax.all_gather(v, "seq", axis=0, tiled=True).astype(F32) for v in vectors]
 
 
-def own_parts(lanes, sizes):
-    outs = []
-    row = 0
-    for size in sizes:
-        if size < 128:
-            part = lax.axis_index("seq") % (128 // size)
-            outs.append(lax.dynamic_slice(lanes[row], (part * size,), (size,)))
-            row += 1
-        else:
-            outs.append(lanes[row : row + size // 128].reshape(-1))
-            row += size // 128
-    return outs
-
-
-def reduce_plain(weights, grads, vectors):
+def reduce_plain(grads, vectors):
     outs = [
         lax.psum_scatter(g.astype(BF16), "batch", scatter_dimension=1, tiled=True).astype(F32)
         for g in grads
@@ -422,6 +411,14 @@
 
 
 NARROW = 8
+
+
+def cost(micros):
+    return pl.CostEstimate(flops=int(micros * 1e9), transcendentals=0, bytes_accessed=1 << 20)
+
+
+def spread(shape, first=0):
+    return pl.BlockSpec((shape[0], 1) + tuple(shape[2:]), lambda i: (0, i + first, 0, 0))
 
 
 def project(inputs, shards, slices, pieces, wide, lines, tiles):
@@ -478,6 +475,7 @@
     square = (width, width)
     return pl.pallas_call(
         kernel,
+        cost_estimate=cost(6),
         grid=(count,),
         in_specs=[pl.BlockSpec(memory_space=pltpu.SMEM), each(inputs.shape)]
         + [pl.BlockSpec(memory_space=pltpu.VMEM)] * len(arrays),
@@ -498,32 +496,41 @@
     return jnp.where(head_mask(array.shape[0], lane_half), array, jnp.zeros_like(array))
 
 
+def seen_rows(seq, far, rows):
+    row = lax.broadcasted_iota(jnp.int32, (far, rows), 0) // 2
+    seen = jnp.zeros((far, rows), F32)
+    for p, (rel, _) in enumerate(relative_ids(seq_stages())):
+        seen = jnp.where(row == p, jnp.where((seq ^ rel) < seq, 1.0, 0.0), seen)
+    return seen
+
+
 def scores_of(keys, query, visible, rows):
     scores = dot(keys, query, 1, 1) * HEAD ** (-0.5)
     far = jnp.where(visible > 0, scores[rows:], -1e30)
     return jnp.concatenate([scores[:rows], far], 0)
 
 
-def attend(qkv, summaries, visible):
+def attend(qkv, summaries):
     count, rows, width = qkv.shape[0], qkv.shape[1], qkv.shape[2] // 3
-    far = summaries.shape[1]
-
-    def kernel(qkv_ref, sum_ref, vis_ref, mixed_ref, lse_ref):
-        seen = vis_ref[...]
+    far = 2 * summaries.shape[0]
+
+    def kernel(spot, qkv_ref, sum_ref, mixed_ref, lse_ref):
+        seen = seen_rows(spot[0], far, rows)
+        spans = jnp.concatenate([sum_ref[p, 0] for p in range(far // 2)], 0)
         for pair in range(HEADS // 2):
             at = pair * 2 * HEAD
             query = qkv_ref[0, :, at : at + 2 * HEAD]
             keys = jnp.concatenate(
                 [
                     qkv_ref[0, :, width + at : width + at + 2 * HEAD],
-                    sum_ref[0, :, at : at + 2 * HEAD],
+                    spans[:, at : at + 2 * HEAD],
                 ],
                 0,
             )
             values = jnp.concatenate(
                 [
                     qkv_ref[0, :, 2 * width + at : 2 * width + at + 2 * HEAD],
-                    sum_ref[0, :, width + at : width + at + 2 * HEAD],
+                    spans[:, width + at : width + at + 2 * HEAD],
                 ],
                 0,
             )
@@ -543,18 +550,19 @@
     block = (count, rows, width)
     return pl.pallas_call(
         kernel,
+        cost_estimate=cost(8),
         grid=(count,),
         in_specs=[
+            pl.BlockSpec(memory_space=pltpu.SMEM),
             each(qkv.shape),
-            each(summaries.shape),
-            full((far, rows)),
+            spread(summaries.shape),
         ],
         out_specs=[each(block), each((count, HEADS, rows))],
         out_shape=[
             jax.ShapeDtypeStruct(block, BF16),
             jax.ShapeDtypeStruct((count, HEADS, rows), F32),
         ],
-    )(qkv, summaries, visible)
+    )(place(), qkv, summaries)
 
 
 def split_rows(total):
@@ -579,7 +587,7 @@
 
 
 def feed(inputs, cotangent, mixed, narrow, long_bias, pieces, wide, shards, tiles):
-    count, rows, width = inputs.shape
+    count, _, width = inputs.shape
     hidden_width = long_bias.shape[1]
     arrays = [piece for piece, _, _ in pieces] if tiles else list(wide)
     step = 512
@@ -684,6 +692,7 @@
         out_specs += [full(shape) for shape in grads]
     return pl.pallas_call(
         kernel,
+        cost_estimate=cost(35),
         grid=(count,),
         in_specs=[pl.BlockSpec(memory_space=pltpu.SMEM)]
         + [each(block)] * 3
@@ -695,9 +704,9 @@
     )(place(), inputs, cotangent, mixed, narrow, long_bias, *arrays)
 
 
-def attend_back(qkv, summaries, visible, lse, mixed_grad, first, number, before=(), after=()):
-    count, rows, width = mixed_grad.shape
-    far = summaries.shape[1]
+def attend_back(qkv, summaries, lse, mixed_grad, first, number, before=(), after=()):
+    _, rows, width = mixed_grad.shape
+    far = 2 * summaries.shape[0]
     extra = list(before) + list(after)
 
     def each(shape):
@@ -705,21 +714,22 @@
             (1,) + tuple(shape[1:]), lambda i: (i + first,) + (0,) * (len(shape) - 1)
         )
 
-    def kernel(qkv_ref, sum_ref, vis_ref, lse_ref, grad_ref, *rest):
+    def kernel(spot, qkv_ref, sum_ref, lse_ref, grad_ref, *rest):
         dq_ref, dk_ref, dv_ref, far_ref = rest[len(extra) :]
-        seen = vis_ref[...]
+        seen = seen_rows(spot[0], far, rows)
+        spans = jnp.concatenate([sum_ref[p, 0] for p in range(far // 2)], 0)
         for pair in range(HEADS // 2):
             at = pair * 2 * HEAD
             lanes = slice(at, at + 2 * HEAD)
             query = qkv_ref[0, :, lanes]
             pull = grad_ref[0, :, lanes]
             keys = jnp.concatenate(
-                [qkv_ref[0, :, width + at : width + at + 2 * HEAD], sum_ref[0, :, lanes]], 0
+                [qkv_ref[0, :, width + at : width + at + 2 * HEAD], spans[:, lanes]], 0
             )
             values = jnp.concatenate(
                 [
                     qkv_ref[0, :, 2 * width + at : 2 * width + at + 2 * HEAD],
-                    sum_ref[0, :, width + at : width + at + 2 * HEAD],
+                    spans[:, width + at : width + at + 2 * HEAD],
                 ],
                 0,
             )
@@ -740,22 +750,26 @@
             dq_ref[0, :, lanes] = (d_query * HEAD ** (-0.5)).T.astype(BF16)
             dk_ref[0, :, lanes] = d_keys[:rows]
             dv_ref[0, :, lanes] = d_values[:rows]
-            far_ref[0, :, lanes] = d_keys[rows:].astype(BF16)
-            far_ref[0, :, width + at : width + at + 2 * HEAD] = d_values[rows:].astype(BF16)
+            for k, terms in enumerate((d_keys, d_values)):
+                left = k * width + at
+                for p in range(far // 2):
+                    part = terms[rows + 2 * p : rows + 2 * p + 2].astype(BF16)
+                    far_ref[p, 0, :, left : left + 2 * HEAD] = part
 
     block = mixed_grad.shape
     return pl.pallas_call(
         kernel,
+        cost_estimate=cost(7),
         grid=(number,),
         in_specs=[
+            pl.BlockSpec(memory_space=pltpu.SMEM),
             each(qkv.shape),
-            each(summaries.shape),
-            full((far, rows)),
+            spread(summaries.shape, first),
             each(lse.shape),
             each(block),
         ]
         + [pl.BlockSpec(memory_space=pl.ANY)] * len(extra),
-        out_specs=[each(block)] * 3 + [each(summaries.shape)],
+        out_specs=[each(block)] * 3 + [spread(summaries.shape, first)],
         out_shape=[
             jax.ShapeDtypeStruct(block, BF16),
             jax.ShapeDtypeStruct(block, F32),
@@ -763,7 +777,7 @@
             jax.ShapeDtypeStruct(summaries.shape, BF16),
         ],
         input_output_aliases={5 + k: k for k in range(len(before))},
-    )(qkv, summaries, visible, lse, mixed_grad, *extra)
+    )(place(), qkv, summaries, lse, mixed_grad, *extra)
 
 
 def project_back(
@@ -845,6 +859,7 @@
         out_specs += [full(square)] * 3
     return pl.pallas_call(
         kernel,
+        cost_estimate=cost(10),
         grid=(count,),
         in_specs=[pl.BlockSpec(memory_space=pltpu.SMEM)]
         + [each(block)] * 4
@@ -858,7 +873,7 @@
     )(place(), inputs, d_query, d_keys, d_values, owned, *weights, narrow, middle_grad, *after)
 
 
-def local(
+def layer(
     inputs,
     cotangent,
     query_weight,
@@ -878,7 +893,7 @@
     shards = [query_weight, key_weight, value_weight, out_weight, up_weight, down_weight]
     slices = [norm1_gain, norm1_bias, norm2_gain, norm2_bias, out_bias, up_bias, down_bias]
     tiles = whole_tiles(shards, slices)
-    count, rows, width = inputs.shape
+    count, _, width = inputs.shape
     wide, lines, early, late = [None] * 6, (), (), ()
     if tiles:
         state = gather_outer(pack_shards(shards[:3], slices))
@@ -895,12 +910,8 @@
     qkv, pooled, w_query, w_key, w_value, narrow, long_bias = project(
         inputs, shards[:3], slices, early, wide[:3], lines, tiles
     )
-    summaries = jnp.transpose(gather_seq(pooled), (1, 0, 2, 3)).reshape(count, -1, 2 * width)
-    here = lax.axis_index("seq")
-    marks = jnp.array([s for s, _ in relative_ids(seq_stages())], jnp.int32)
-    visible = jnp.repeat((marks ^ here) < here, 2).astype(F32)
-    visible = jnp.broadcast_to(visible[:, None], (visible.shape[0], rows))
-    mixed, lse = attend(qkv, summaries, visible)
+    summaries = gather_seq(pooled)
+    mixed, lse = attend(qkv, summaries)
     outputs, middle_grad, mixed_grad, narrow_two, wide_two, *second = feed(
         inputs, cotangent, mixed, narrow, long_bias, late, wide[3:], shards[3:], tiles
     )
@@ -908,14 +919,13 @@
     if tiles:
         second = reduce_step([tuple(second[:2]), tuple(second[2:])], 0)
         ties = [member for couple in second for member in couple]
-    begun = attend_back(qkv, summaries, visible, lse, mixed_grad, 0, count // 2)
+    begun = attend_back(qkv, summaries, lse, mixed_grad, 0, count // 2)
     d_query, d_keys, d_values, terms = attend_back(
-        qkv, summaries, visible, lse, mixed_grad, count // 2, count - count // 2, begun, ties
+        qkv, summaries, lse, mixed_grad, count // 2, count - count // 2, begun, ties
     )
     if tiles:
         second = reduce_step(second, 1)
         ties = [member for couple in second for member in couple]
-    terms = jnp.transpose(terms.reshape(count, -1, 2, 2 * width), (1, 0, 2, 3))
     owned = reduce_seq(terms)
     input_grad, narrow_one, *first = project_back(
         inputs,
@@ -931,14 +941,14 @@
         ties,
     )
     if tiles:
+        size = norm1_gain.shape[0]
         second = reduce_step(second, 2, True)
         first = reduce_step([tuple(first[:2]), tuple(first[2:])], 0)
         first = reduce_step(reduce_step(first, 1), 2, True)
-        *matrices, lines_two, lines_one = reduce_end([((3, 4, 5), second), ((0, 1, 2), first)], shards)
-        size = norm1_gain.shape[0]
-        tail = own_parts(lines_two, [size] * 4 + [up_bias.shape[0]])
-        front = own_parts(lines_one, [size] * 2)
-        vectors = front + tail[:3] + [tail[4], tail[3]]
+        tail = reduce_end(second, shards[3:], [size] * 4 + [up_bias.shape[0]])
+        front = reduce_end(first, shards[:3], [size] * 2)
+        matrices = front[:3] + tail[:3]
+        vectors = front[3:] + tail[3:6] + [tail[7], tail[6]]
     else:
         vectors = [
             narrow_one[0],
@@ -949,7 +959,7 @@
             wide_two[0],
             narrow_two[3],
         ]
-        reduced = reduce_plain(shards, list(first) + list(second), vectors)
+        reduced = reduce_plain(list(first) + list(second), vectors)
         matrices, vectors = reduced[:6], reduced[6:]
     return (outputs, input_grad, *matrices, *vectors)
 
@@ -973,7 +983,7 @@
         P("seq"),
     )
     return jax.shard_map(
-        local,
+        layer,
         mesh=mesh,
         in_specs=placed,
         out_specs=(

time: 249 us -> 224 us (0.90)
  waiting for transfers between devices: 88.5 us -> 56.9 us
  starting transfers between devices: 40.4 us -> 48.3 us
  local copies, waits for them, and re-layouts: 19.8 us -> 14.9 us
  Pallas kernels: 83.5 us -> 87.9 us
    ppermute x40 -> x42, waiting for transfers between devices: 88.5 us -> 56.9 us  [swap(): return lax.ppermute(array, axis, [(i, i ^ bit) for i in range(count)])]
    ppermute x40 -> x42, starting transfers between devices: 40.4 us -> 48.3 us  [swap(): return lax.ppermute(array, axis, [(i, i ^ bit) for i in range(count)])]
    pallas_call x9 -> x12, Pallas kernels: 80.4 us -> 84.8 us  [the longest x1 35.2 us: feed(): pl.pallas_call(kernel, cost_estimate=cost(35), grid=(count,), in_specs=[p...]
    dynamic_slice x6 -> x0, local copies, waits for them, and re-layouts: 3.48 us -> none  [own_parts(): outs.append(lax.dynamic_slice(lanes[row], (part * size,), (size,)))]
    unnamed x56 -> x60, local copies, waits for them, and re-layouts: 5.96 us -> 8.8 us
  transfers between devices with their start and end apart: 40 -> 42, of which waited for: 23 -> 18; matrix products, arithmetic and copies ran while one was open for 5% -> 5% of each run, Pallas kernels for 9% -> 18%
where the time goes in v2:
time: 224 us; the launch traced here: 223 us
  Pallas kernels  87.9 us (39%)
  waiting for transfers between devices  56.9 us (25%)
  starting transfers between devices  48.3 us (22%)
  local copies, waits for them, and re-layouts  14.9 us (7%)
  other arithmetic  13.8 us (6%)
    ppermute x42, waiting for transfers between devices, swap(): return lax.ppermute(array, axis, [(i, i ^ bit) for i in range(count)])  56.9 us
    ppermute x42, starting transfers between devices, swap(): return lax.ppermute(array, axis, [(i, i ^ bit) for i in range(count)])  48.3 us
    pallas_call x1, Pallas kernels, feed(): pl.pallas_call(kernel, cost_estimate=cost(35), grid=(count,), in_specs=[p...  35.2 us
    pallas_call x2, Pallas kernels, attend_back(): pl.pallas_call(kernel, cost_estimate=cost(7), grid=(number,), in_specs=[p...  14.3 us
    pallas_call x1, Pallas kernels, project_back(): pl.pallas_call(kernel, cost_estimate=cost(10), grid=(count,), in_specs=[p...  10.5 us
    unnamed x60, local copies, waits for them, and re-layouts  8.8 us
    pallas_call x1, Pallas kernels, attend(): pl.pallas_call(kernel, cost_estimate=cost(8), grid=(count,), in_specs=[pl...  7.5 us
    pallas_call x1, Pallas kernels, project(): pl.pallas_call(kernel, cost_estimate=cost(6), grid=(count,), in_specs=[pl...  6.6 us
  transfers between devices with their start and end apart: 42, of which 18 were waited for; matrix products, arithmetic and copies ran while one was open for 5% of the time, Pallas kernels for 18%

profile of v2, /device:TPU:0, one launch (start us, length us, event | category | flops | bytes accessed | tf_op | source)
XLA Modules:
  0.0 223.0 jit_solution(3670090869401778228)
XLA Ops:
  2.8 4.1 %collective-permute-start = (bf16[1,224,128]{2,1,0:T(8,128)(2,1)}, bf16[1,224,128]{2,1,0:T(8,128)(2,1)S(1)}, u32[]{:S(2)}, u32[]{:S(2)}) collective-permute-start(bf16[1,224,128]{2,1,0:T(8,128)(2,1)} %shard_map.262), channel_id=1, source_target_pairs={{0,4},{1,5},{2,6},{3,7},{4,0},{5,1},{6,2},{7,3},{8,12},{9,13},{10,... | collective-permute-start | bytes 172040 | tf_op jit(solution)/shard_map/ppermute | solution.py:18
  6.8 3.0 %collective-permute-done = bf16[1,224,128]{2,1,0:T(8,128)(2,1)S(1)} collective-permute-done((bf16[1,224,128]{2,1,0:T(8,128)(2,1)}, bf16[1,224,128]{2,1,0:T(8,128)(2,1)S(1)}, u32[]{:S(2)}, u32[]{:S(2)}) %collective-permute-start) | collective-permute-done | bytes 57376 | tf_op jit(solution)/shard_map/ppermute | solution.py:18
  12.0 3.5 %collective-permute-done.1 = bf16[2,224,128]{2,1,0:T(8,128)(2,1)S(1)} collective-permute-done((bf16[2,224,128]{2,1,0:T(8,128)(2,1)S(1)}, bf16[2,224,128]{2,1,0:T(8,128)(2,1)S(1)}, u32[]{:S(2)}, u32[]{:S(2)}) %collective-permute-start.1) | collective-permute-done | bytes 114720 | tf_op jit(solution)/shard_map/ppermute | solution.py:18
  17.0 1.6 shard_map.265
  18.6 2.5 %collective-permute-start.13 = (bf16[1,576,128]{2,1,0:T(8,128)(2,1)}, bf16[1,576,128]{2,1,0:T(8,128)(2,1)S(1)}, u32[]{:S(2)}, u32[]{:S(2)}) collective-permute-start(bf16[1,576,128]{2,1,0:T(8,128)(2,1)} %shard_map.265), channel_id=1, source_target_pairs={{0,4},{1,5},{2,6},{3,7},{4,0},{5,1},{6,2},{7,3},{8,12},{9,13},{10,... | collective-permute-start | bytes 442376 | tf_op jit(solution)/shard_map/ppermute | solution.py:18
  21.1 5.4 %collective-permute-done.13 = bf16[1,576,128]{2,1,0:T(8,128)(2,1)S(1)} collective-permute-done((bf16[1,576,128]{2,1,0:T(8,128)(2,1)}, bf16[1,576,128]{2,1,0:T(8,128)(2,1)S(1)}, u32[]{:S(2)}, u32[]{:S(2)}) %collective-permute-start.13) | collective-permute-done | bytes 147488 | tf_op jit(solution)/shard_map/ppermute | solution.py:18
  28.1 1.6 collective-permute-start.2
  31.2 2.2 collective-permute-done.2
  33.5 1.7 collective-permute-start.4
  35.3 1.6 collective-permute-start.15
  38.3 2.2 collective-permute-done.4.refs_2_
  40.5 4.1 %collective-permute-done.8.refs_6_ = bf16[8,112,128]{2,1,0:T(8,128)(2,1)S(1)} collective-permute-done((bf16[8,112,128]{2,1,0:T(8,128)(2,1)S(1)}, bf16[8,112,128]{2,1,0:T(8,128)(2,1)S(1)}, u32[]{:S(2)}, u32[]{:S(2)}) %collective-permute-start.8) | collective-permute-done | bytes 229408 | tf_op jit(solution)/shard_map/ppermute | solution.py:18
  46.5 1.6 collective-permute-start.21
  49.5 6.6 %shard_map.263 = (bf16[4,256,1536]{2,1,0:T(8,128)(2,1)}, bf16[4,2,1024]{2,1,0:T(2,128)(2,1)}, bf16[512,512]{1,0:T(8,128)(2,1)}, bf16[512,512]{1,0:T(8,128)(2,1)}...) custom-call(s32[2]{0:T(128)} %pad_add_fusion.spot, bf16[4,256,512]{2,1,0:T(8,128)(2,1)} %x_ref.5, ...), custom_call_target="tpu_custom_call" | custom-call | flops 6000000000 | bytes 1048576 | tf_op jit(solution)/shard_map/pallas_call | solution.py:476
  56.1 2.9 %collective-permute-start.10 = (bf16[1,4,2,1024]{3,2,1,0:T(2,128)(2,1)}, bf16[1,4,2,1024]{3,2,1,0:T(2,128)(2,1)S(1)}, u32[]{:S(2)}, u32[]{:S(2)}) collective-permute-start(bf16[1,4,2,1024]{3,2,1,0:T(2,128)(2,1)} %bitcast.5), channel_id=1, source_target_pairs={{0,4},{1,5},{2,6},{3,7},{4,0},{5,1},{6,2},{7,3},{8,12},{9,13},{10,... | collective-permute-start | bytes 49160 | tf_op jit(solution)/shard_map/ppermute | solution.py:18
  59.0 2.0 collective-permute-done.10
  61.8 1.7 collective-permute-start.11
  63.4 2.3 %collective-permute-done.11 = bf16[2,4,2,1024]{3,2,1,0:T(2,128)(2,1)S(1)} collective-permute-done((bf16[2,4,2,1024]{3,2,1,0:T(2,128)(2,1)S(1)}, bf16[2,4,2,1024]{3,2,1,0:T(2,128)(2,1)S(1)}, u32[]{:S(2)}, u32[]{:S(2)}) %collective-permute-start.11) | collective-permute-done | bytes 32800 | tf_op jit(solution)/shard_map/ppermute | solution.py:18
  66.6 1.9 collective-permute-start.12
  68.5 2.4 %collective-permute-done.12 = bf16[4,4,2,1024]{3,2,1,0:T(2,128)(2,1)S(1)} collective-permute-done((bf16[4,4,2,1024]{3,2,1,0:T(2,128)(2,1)S(1)}, bf16[4,4,2,1024]{3,2,1,0:T(2,128)(2,1)S(1)}, u32[]{:S(2)}, u32[]{:S(2)}) %collective-permute-start.12) | collective-permute-done | bytes 65568 | tf_op jit(solution)/shard_map/ppermute | solution.py:18
  70.9 1.6 pad_maximum_fusion.12.sum_ref
  73.5 7.5 %shard_map.264 = (bf16[4,256,512]{2,1,0:T(8,128)(2,1)}, f32[4,8,256]{2,1,0:T(8,128)}) custom-call(s32[2]{0:T(128)} %pad_add_fusion.spot, bf16[4,256,1536]{2,1,0:T(8,128)(2,1)} %get-tuple-element.65.qkv_ref, bf16[8,4,2,1024]{3,2,1,0:T(2,128)(2,1)} %pad_maximum_fusion.12.sum_ref), custom_call_target="tpu_custom_call" | custom-call | flops 8000000000 | bytes 1048576 | tf_op jit(solution)/shard_map/pallas_call | solution.py:551
  81.9 35.2 %shard_map.266 = (bf16[4,256,512]{2,1,0:T(8,128)(2,1)}, f32[4,256,512]{2,1,0:T(8,128)}, bf16[4,256,512]{2,1,0:T(8,128)(2,1)}, f32[8,512]{1,0:T(8,128)}, f32[8,20...) custom-call(s32[2]{0:T(128)} %pad_add_fusion.spot, ...), custom_call_target="tpu_custom_call" | custom-call | flops 35000000512 | bytes 1048576 | tf_op jit(solution)/shard_map/pallas_call | solution.py:693
  117.7 7.2 %shard_map.267 = (bf16[4,256,512]{2,1,0:T(8,128)(2,1)}, f32[4,256,512]{2,1,0:T(8,128)}, f32[4,256,512]{2,1,0:T(8,128)}, bf16[8,4,2,1024]{3,2,1,0:T(2,128)(2,1)}) custom-call(s32[2]{0:T(128)} %pad_add_fusion.spot, bf16[4,256,1536]{2,1,0:T(8,128)(2,1)} %get-tuple-element.65.qkv_ref, bf16[8,4,2,1024]{3,2,1,0:T(2,128)(2,1)} %pad_maximum_fusion.12.sum_ref, ...), custom_call_target="tpu_custom_call" | custom-call | flops 7000000000 | bytes 1048576 | tf_op jit(solution)/shard_map/pallas_call | solution.py:760
  126.0 1.6 add_convert_fusion
  130.3 1.6 add_convert_fusion.1
  133.1 7.0 %shard_map.268 = (bf16[4,256,512]{2,1,0:T(8,128)(2,1)}, f32[4,256,512]{2,1,0:T(8,128)}, f32[4,256,512]{2,1,0:T(8,128)}, bf16[8,4,2,1024]{3,2,1,0:T(2,128)(2,1)}) custom-call(s32[2]{0:T(128)} %pad_add_fusion.spot, bf16[4,256,1536]{2,1,0:T(8,128)(2,1)} %get-tuple-element.65.qkv_ref, ...), custom_call_target="tpu_custom_call", output_to_operand_aliasing={{0}: (5, {}), {1}: (6, {}), {2}: (7, {}), {3}: (8, {})} | custom-call | flops 7000000000 | bytes 1048576 | tf_op jit(solution)/shard_map/pallas_call | solution.py:760
  141.0 1.9 collective-permute-start.25
  143.5 1.9 collective-permute-done.25
  146.4 1.6 collective-permute-start.26
  148.0 2.3 %collective-permute-done.26 = bf16[2,4,2,1024]{3,2,1,0:T(2,128)(2,1)S(1)} collective-permute-done((bf16[2,4,2,1024]{3,2,1,0:T(2,128)(2,1)S(1)}, bf16[2,4,2,1024]{3,2,1,0:T(2,128)(2,1)S(1)}, u32[]{:S(2)}, u32[]{:S(2)}) %collective-permute-start.26) | collective-permute-done | bytes 32800 | tf_op jit(solution)/shard_map/ppermute | solution.py:18
  150.4 3.0 %collective-permute-start.27 = (bf16[1,4,2,1024]{3,2,1,0:T(2,128)(2,1)S(1)}, bf16[1,4,2,1024]{3,2,1,0:T(2,128)(2,1)S(1)}, u32[]{:S(2)}, u32[]{:S(2)}) collective-permute-start(bf16[1,4,2,1024]{3,2,1,0:T(2,128)(2,1)S(1)} %slice.223), channel_id=1, source_target_pairs={{0,4},{1,5},{2,6},{3,7},{4,0},{5,1},{6,2},{7,3},{8,12},{9,13},{10,... | collective-permute-start | bytes 49160 | tf_op jit(solution)/shard_map/ppermute | solution.py:18
  153.4 1.8 collective-permute-start.29
  155.8 3.0 %collective-permute-done.28 = bf16[8,304,128]{2,1,0:T(8,128)(2,1)S(1)} collective-permute-done((bf16[8,304,128]{2,1,0:T(8,128)(2,1)S(1)}, bf16[8,304,128]{2,1,0:T(8,128)(2,1)S(1)}, u32[]{:S(2)}, u32[]{:S(2)}) %collective-permute-start.28) | collective-permute-done | bytes 622624 | tf_op jit(solution)/shard_map/ppermute | solution.py:18
  160.1 10.4 %collective-permute-done.29 = bf16[8,304,128]{2,1,0:T(8,128)(2,1)S(1)} collective-permute-done((bf16[8,304,128]{2,1,0:T(8,128)(2,1)}, bf16[8,304,128]{2,1,0:T(8,128)(2,1)S(1)}, u32[]{:S(2)}, u32[]{:S(2)}) %collective-permute-start.29) | collective-permute-done | bytes 622624 | tf_op jit(solution)/shard_map/ppermute | solution.py:18
  172.2 10.5 %shard_map.269 = (f32[4,256,512]{2,1,0:T(8,128)}, f32[8,512]{1,0:T(8,128)}, bf16[16,112,128]{2,1,0:T(8,128)(2,1)}, bf16[16,112,128]{2,1,0:T(8,128)(2,1)}, bf16[1...) custom-call(s32[2]{0:T(128)} %pad_add_fusion.spot, bf16[4,256,512]{2,1,0:T(8,128)(2,1)} %x_ref.5, ...), custom_call_target="tpu_custom_call" | custom-call | flops 10000000000 | bytes 1048576 | tf_op jit(solution)/shard_map/pallas_call | solution.py:860
  184.7 2.1 shard_map.273
  190.5 4.3 %collective-permute-done.31 = bf16[8,112,128]{2,1,0:T(8,128)(2,1)S(1)} collective-permute-done((bf16[8,112,128]{2,1,0:T(8,128)(2,1)S(1)}, bf16[8,112,128]{2,1,0:T(8,128)(2,1)S(1)}, u32[]{:S(2)}, u32[]{:S(2)}) %collective-permute-start.31) | collective-permute-done | bytes 229408 | tf_op jit(solution)/shard_map/ppermute | solution.py:18
  195.5 1.7 collective-permute-start.32
  200.3 2.5 %collective-permute-done.35.refs_3_ = bf16[4,112,128]{2,1,0:T(8,128)(2,1)S(1)} collective-permute-done((bf16[4,112,128]{2,1,0:T(8,128)(2,1)S(1)}, bf16[4,112,128]{2,1,0:T(8,128)(2,1)S(1)}, u32[]{:S(2)}, u32[]{:S(2)}) %collective-permute-start.35) | collective-permute-done | bytes 114720 | tf_op jit(solution)/shard_map/ppermute | solution.py:18
  203.5 1.8 shard_map.270
  205.3 1.7 collective-permute-start.36
  207.7 1.8 shard_map.274
  211.0 1.6 shard_map.271
  212.7 2.1 collective-permute-start.37
  214.7 3.6 %collective-permute-done.41.theirs_ref = bf16[1,608,128]{2,1,0:T(8,128)(2,1)S(1)} collective-permute-done((bf16[1,608,128]{2,1,0:T(8,128)(2,1)}, bf16[1,608,128]{2,1,0:T(8,128)(2,1)S(1)}, u32[]{:S(2)}, u32[]{:S(2)}) %collective-permute-start.41) | collective-permute-done | bytes 155680 | tf_op jit(solution)/shard_map/ppermute | solution.py:18
  219.0 1.8 shard_map.275
  221.5 1.6 shard_map.272
  (153 shorter events, 42.4 us)
Async XLA Ops:
  2.8 7.0 %collective-permute-start = (bf16[1,224,128]{2,1,0:T(8,128)(2,1)}, bf16[1,224,128]{2,1,0:T(8,128)(2,1)S(1)}, u32[]{:S(2)}, u32[]{:S(2)}) collective-permute-start(bf16[1,224,128]{2,1,0:T(8,128)(2,1)} %shard_map.262), channel_id=1, source_target_pairs={{0,4},{1,5},{2,6},{3,7},{4,0},{5,1},{6,2},{7,3},{8,12},{9,13},{10,... | collective-permute-start | bytes 172040 | tf_op jit(solution)/shard_map/ppermute | solution.py:18
  10.6 4.9 %collective-permute-start.1 = (bf16[2,224,128]{2,1,0:T(8,128)(2,1)S(1)}, bf16[2,224,128]{2,1,0:T(8,128)(2,1)S(1)}, u32[]{:S(2)}, u32[]{:S(2)}) collective-permute-start(bf16[2,224,128]{2,1,0:T(8,128)(2,1)S(1)} %pad_maximum_fusion.13), channel_id=1, source_target_pairs={{0,2},{1,3},{2,0},{3,1},{4,6},{5,7},{6,4},{7,5},{8,10},{9,11},{10,... | collective-permute-start | bytes 344072 | tf_op jit(solution)/shard_map/ppermute | solution.py:18
  17.0 11.1 %copy-start = (bf16[4,224,128]{2,1,0:T(8,128)(2,1)S(1)}, bf16[4,224,128]{2,1,0:T(8,128)(2,1)}, u32[]{:S(2)}) copy-start(bf16[4,224,128]{2,1,0:T(8,128)(2,1)} %pad_maximum_fusion.8.refs_3_) | copy-start | bytes 688132
  18.6 16.6 %copy-start.1 = (bf16[1,576,128]{2,1,0:T(8,128)(2,1)S(1)}, bf16[1,576,128]{2,1,0:T(8,128)(2,1)}, u32[]{:S(2)}) copy-start(bf16[1,576,128]{2,1,0:T(8,128)(2,1)} %shard_map.265) | copy-start | bytes 442372
  18.6 7.8 %collective-permute-start.13 = (bf16[1,576,128]{2,1,0:T(8,128)(2,1)}, bf16[1,576,128]{2,1,0:T(8,128)(2,1)S(1)}, u32[]{:S(2)}, u32[]{:S(2)}) collective-permute-start(bf16[1,576,128]{2,1,0:T(8,128)(2,1)} %shard_map.265), channel_id=1, source_target_pairs={{0,4},{1,5},{2,6},{3,7},{4,0},{5,1},{6,2},{7,3},{8,12},{9,13},{10,... | collective-permute-start | bytes 442376 | tf_op jit(solution)/shard_map/ppermute | solution.py:18
  27.4 7.8 %collective-permute-start.14 = (bf16[2,576,128]{2,1,0:T(8,128)(2,1)S(1)}, bf16[2,576,128]{2,1,0:T(8,128)(2,1)S(1)}, u32[]{:S(2)}, u32[]{:S(2)}) collective-permute-start(bf16[2,576,128]{2,1,0:T(8,128)(2,1)S(1)} %pad_maximum_fusion.5), channel_id=1, source_target_pairs={{0,2},{1,3},{2,0},{3,1},{4,6},{5,7},{6,4},{7,5},{8,10},{9,11},{10,... | collective-permute-start | bytes 884744 | tf_op jit(solution)/shard_map/ppermute | solution.py:18
  28.1 5.3 %collective-permute-start.2 = (bf16[4,112,128]{2,1,0:T(8,128)(2,1)S(1)}, bf16[4,112,128]{2,1,0:T(8,128)(2,1)S(1)}, u32[]{:S(2)}, u32[]{:S(2)}) collective-permute-start(bf16[4,112,128]{2,1,0:T(8,128)(2,1)S(1)} %get-tuple-element.138), channel_id=1, source_target_pairs={{0,16},{8,24},{16,0},{24,8},{1,17},{9,25},{17,1},{25,9},{2,18},{10... | collective-permute-start | bytes 344072 | tf_op jit(solution)/shard_map/ppermute | solution.py:18
  29.7 7.2 %collective-permute-start.6 = (bf16[4,112,128]{2,1,0:T(8,128)(2,1)S(1)}, bf16[4,112,128]{2,1,0:T(8,128)(2,1)S(1)}, u32[]{:S(2)}, u32[]{:S(2)}) collective-permute-start(bf16[4,112,128]{2,1,0:T(8,128)(2,1)S(1)} %get-tuple-element.137), channel_id=1, source_target_pairs={{0,1},{1,0},{2,3},{3,2},{4,5},{5,4},{6,7},{7,6},{8,9},{9,8},{10,11... | collective-permute-start | bytes 344072 | tf_op jit(solution)/shard_map/ppermute | solution.py:18
  33.5 7.0 %collective-permute-start.4 = (bf16[8,112,128]{2,1,0:T(8,128)(2,1)S(1)}, bf16[8,112,128]{2,1,0:T(8,128)(2,1)S(1)}, u32[]{:S(2)}, u32[]{:S(2)}) collective-permute-start(bf16[8,112,128]{2,1,0:T(8,128)(2,1)S(1)} %pad_maximum_fusion.9.refs_0_), channel_id=1, source_target_pairs={{0,1},{1,0},{2,3},{3,2},{4,5},{5,4},{6,7},{7,6},{8,9},{9,8},{10,11... | collective-permute-start | bytes 688136 | tf_op jit(solution)/shard_map/ppermute | solution.py:18
  35.3 9.3 %collective-permute-start.15 = (bf16[4,288,128]{2,1,0:T(8,128)(2,1)S(1)}, bf16[4,288,128]{2,1,0:T(8,128)(2,1)S(1)}, u32[]{:S(2)}, u32[]{:S(2)}) collective-permute-start(bf16[4,288,128]{2,1,0:T(8,128)(2,1)S(1)} %get-tuple-element.130), channel_id=1, source_target_pairs={{0,16},{8,24},{16,0},{24,8},{1,17},{9,25},{17,1},{25,9},{2,18},{10... | collective-permute-start | bytes 884744 | tf_op jit(solution)/shard_map/ppermute | solution.py:18
  36.9 12.6 %copy-start.13 = (bf16[8,112,128]{2,1,0:T(8,128)(2,1)}, bf16[8,112,128]{2,1,0:T(8,128)(2,1)S(1)}, u32[]{:S(2)}) copy-start(bf16[8,112,128]{2,1,0:T(8,128)(2,1)S(1)} %pad_maximum_fusion.10.refs_4_) | copy-start | bytes 688132
  36.9 7.7 %collective-permute-start.8 = (bf16[8,112,128]{2,1,0:T(8,128)(2,1)S(1)}, bf16[8,112,128]{2,1,0:T(8,128)(2,1)S(1)}, u32[]{:S(2)}, u32[]{:S(2)}) collective-permute-start(bf16[8,112,128]{2,1,0:T(8,128)(2,1)S(1)} %pad_maximum_fusion.10.refs_4_), channel_id=1, source_target_pairs={{0,16},{8,24},{16,0},{24,8},{1,17},{9,25},{17,1},{25,9},{2,18},{10... | collective-permute-start | bytes 688136 | tf_op jit(solution)/shard_map/ppermute | solution.py:18
  37.5 7.6 %collective-permute-start.19 = (bf16[4,288,128]{2,1,0:T(8,128)(2,1)S(1)}, bf16[4,288,128]{2,1,0:T(8,128)(2,1)S(1)}, u32[]{:S(2)}, u32[]{:S(2)}) collective-permute-start(bf16[4,288,128]{2,1,0:T(8,128)(2,1)S(1)} %get-tuple-element.129), channel_id=1, source_target_pairs={{0,1},{1,0},{2,3},{3,2},{4,5},{5,4},{6,7},{7,6},{8,9},{9,8},{10,11... | collective-permute-start | bytes 884744 | tf_op jit(solution)/shard_map/ppermute | solution.py:18
  38.3 8.2 %collective-permute-start.3 = (bf16[8,112,128]{2,1,0:T(8,128)(2,1)S(1)}, bf16[8,112,128]{2,1,0:T(8,128)(2,1)S(1)}, u32[]{:S(2)}, u32[]{:S(2)}) collective-permute-start(bf16[8,112,128]{2,1,0:T(8,128)(2,1)S(1)} %pad_maximum_fusion.9.refs_0_), channel_id=1, source_target_pairs={{0,8},{8,0},{16,24},{24,16},{1,9},{9,1},{17,25},{25,17},{2,10},{10... | collective-permute-start | bytes 688136 | tf_op jit(solution)/shard_map/ppermute | solution.py:18
  40.5 7.6 %collective-permute-start.7 = (bf16[8,112,128]{2,1,0:T(8,128)(2,1)S(1)}, bf16[8,112,128]{2,1,0:T(8,128)(2,1)S(1)}, u32[]{:S(2)}, u32[]{:S(2)}) collective-permute-start(bf16[8,112,128]{2,1,0:T(8,128)(2,1)S(1)} %pad_maximum_fusion.10.refs_4_), channel_id=1, source_target_pairs={{0,8},{8,0},{16,24},{24,16},{1,9},{9,1},{17,25},{25,17},{2,10},{10... | collective-permute-start | bytes 688136 | tf_op jit(solution)/shard_map/ppermute | solution.py:18
  44.5 3.5 %collective-permute-start.5 = (bf16[8,112,128]{2,1,0:T(8,128)(2,1)S(1)}, bf16[8,112,128]{2,1,0:T(8,128)(2,1)S(1)}, u32[]{:S(2)}, u32[]{:S(2)}) collective-permute-start(bf16[8,112,128]{2,1,0:T(8,128)(2,1)S(1)} %collective-permute-done.4.refs_2_), channel_id=1, source_target_pairs={{0,8},{8,0},{16,24},{24,16},{1,9},{9,1},{17,25},{25,17},{2,10},{10... | collective-permute-start | bytes 688136 | tf_op jit(solution)/shard_map/ppermute | solution.py:18
  44.6 4.9 %collective-permute-start.9 = (bf16[8,112,128]{2,1,0:T(8,128)(2,1)S(1)}, bf16[8,112,128]{2,1,0:T(8,128)(2,1)}, u32[]{:S(2)}, u32[]{:S(2)}) collective-permute-start(bf16[8,112,128]{2,1,0:T(8,128)(2,1)S(1)} %collective-permute-done.8.refs_6_), channel_id=1, source_target_pairs={{0,8},{8,0},{16,24},{24,16},{1,9},{9,1},{17,25},{25,17},{2,10},{10... | collective-permute-start | bytes 688136 | tf_op jit(solution)/shard_map/ppermute | solution.py:18
  45.1 27.3 %copy-start.6 = (bf16[8,288,128]{2,1,0:T(8,128)(2,1)}, bf16[8,288,128]{2,1,0:T(8,128)(2,1)S(1)}, u32[]{:S(2)}) copy-start(bf16[8,288,128]{2,1,0:T(8,128)(2,1)S(1)} %pad_maximum_fusion.3.rest_0_) | copy-start | bytes 1769476
  45.1 27.8 %collective-permute-start.17 = (bf16[8,288,128]{2,1,0:T(8,128)(2,1)S(1)}, bf16[8,288,128]{2,1,0:T(8,128)(2,1)S(1)}, u32[]{:S(2)}, u32[]{:S(2)}) collective-permute-start(bf16[8,288,128]{2,1,0:T(8,128)(2,1)S(1)} %pad_maximum_fusion.3.rest_0_), channel_id=1, source_target_pairs={{0,1},{1,0},{2,3},{3,2},{4,5},{5,4},{6,7},{7,6},{8,9},{9,8},{10,11... | collective-permute-start | bytes 1769480 | tf_op jit(solution)/shard_map/ppermute | solution.py:18
  46.5 26.0 %copy-start.7 = (bf16[8,288,128]{2,1,0:T(8,128)(2,1)}, bf16[8,288,128]{2,1,0:T(8,128)(2,1)S(1)}, u32[]{:S(2)}) copy-start(bf16[8,288,128]{2,1,0:T(8,128)(2,1)S(1)} %pad_maximum_fusion.4.rest_4_) | copy-start | bytes 1769476
  46.5 26.6 %collective-permute-start.21 = (bf16[8,288,128]{2,1,0:T(8,128)(2,1)S(1)}, bf16[8,288,128]{2,1,0:T(8,128)(2,1)S(1)}, u32[]{:S(2)}, u32[]{:S(2)}) collective-permute-start(bf16[8,288,128]{2,1,0:T(8,128)(2,1)S(1)} %pad_maximum_fusion.4.rest_4_), channel_id=1, source_target_pairs={{0,16},{8,24},{16,0},{24,8},{1,17},{9,25},{17,1},{25,9},{2,18},{10... | collective-permute-start | bytes 1769480 | tf_op jit(solution)/shard_map/ppermute | solution.py:18
  56.1 4.9 %collective-permute-start.10 = (bf16[1,4,2,1024]{3,2,1,0:T(2,128)(2,1)}, bf16[1,4,2,1024]{3,2,1,0:T(2,128)(2,1)S(1)}, u32[]{:S(2)}, u32[]{:S(2)}) collective-permute-start(bf16[1,4,2,1024]{3,2,1,0:T(2,128)(2,1)} %bitcast.5), channel_id=1, source_target_pairs={{0,4},{1,5},{2,6},{3,7},{4,0},{5,1},{6,2},{7,3},{8,12},{9,13},{10,... | collective-permute-start | bytes 49160 | tf_op jit(solution)/shard_map/ppermute | solution.py:18
  61.8 4.0 %collective-permute-start.11 = (bf16[2,4,2,1024]{3,2,1,0:T(2,128)(2,1)S(1)}, bf16[2,4,2,1024]{3,2,1,0:T(2,128)(2,1)S(1)}, u32[]{:S(2)}, u32[]{:S(2)}) collective-permute-start(bf16[2,4,2,1024]{3,2,1,0:T(2,128)(2,1)S(1)} %pad_maximum_fusion.15), channel_id=1, source_target_pairs={{0,2},{1,3},{2,0},{3,1},{4,6},{5,7},{6,4},{7,5},{8,10},{9,11},{10,... | collective-permute-start | bytes 98312 | tf_op jit(solution)/shard_map/ppermute | solution.py:18
  66.6 4.3 %collective-permute-start.12 = (bf16[4,4,2,1024]{3,2,1,0:T(2,128)(2,1)S(1)}, bf16[4,4,2,1024]{3,2,1,0:T(2,128)(2,1)S(1)}, u32[]{:S(2)}, u32[]{:S(2)}) collective-permute-start(bf16[4,4,2,1024]{3,2,1,0:T(2,128)(2,1)S(1)} %pad_maximum_fusion.14), channel_id=1, source_target_pairs={{0,1},{1,0},{2,3},{3,2},{4,5},{5,4},{6,7},{7,6},{8,9},{9,8},{10,11... | collective-permute-start | bytes 196616 | tf_op jit(solution)/shard_map/ppermute | solution.py:18
  72.5 8.6 %collective-permute-start.16 = (bf16[8,288,128]{2,1,0:T(8,128)(2,1)S(1)}, bf16[8,288,128]{2,1,0:T(8,128)(2,1)S(1)}, u32[]{:S(2)}, u32[]{:S(2)}) collective-permute-start(bf16[8,288,128]{2,1,0:T(8,128)(2,1)S(1)} %pad_maximum_fusion.3.rest_0_), channel_id=1, source_target_pairs={{0,8},{8,0},{16,24},{24,16},{1,9},{9,1},{17,25},{25,17},{2,10},{10... | collective-permute-start | bytes 1769480 | tf_op jit(solution)/shard_map/ppermute | solution.py:18
  72.5 8.6 %collective-permute-start.20 = (bf16[8,288,128]{2,1,0:T(8,128)(2,1)S(1)}, bf16[8,288,128]{2,1,0:T(8,128)(2,1)}, u32[]{:S(2)}, u32[]{:S(2)}) collective-permute-start(bf16[8,288,128]{2,1,0:T(8,128)(2,1)S(1)} %pad_maximum_fusion.4.rest_4_), channel_id=1, source_target_pairs={{0,8},{8,0},{16,24},{24,16},{1,9},{9,1},{17,25},{25,17},{2,10},{10... | collective-permute-start | bytes 1769480 | tf_op jit(solution)/shard_map/ppermute | solution.py:18
  73.0 8.1 %collective-permute-start.18 = (bf16[8,288,128]{2,1,0:T(8,128)(2,1)S(1)}, bf16[8,288,128]{2,1,0:T(8,128)(2,1)}, u32[]{:S(2)}, u32[]{:S(2)}) collective-permute-start(bf16[8,288,128]{2,1,0:T(8,128)(2,1)S(1)} %collective-permute-done.17.rest_2_), channel_id=1, source_target_pairs={{0,8},{8,0},{16,24},{24,16},{1,9},{9,1},{17,25},{25,17},{2,10},{10... | collective-permute-start | bytes 1769480 | tf_op jit(solution)/shard_map/ppermute | solution.py:18
  73.1 8.0 %collective-permute-start.22 = (bf16[8,288,128]{2,1,0:T(8,128)(2,1)S(1)}, bf16[8,288,128]{2,1,0:T(8,128)(2,1)}, u32[]{:S(2)}, u32[]{:S(2)}) collective-permute-start(bf16[8,288,128]{2,1,0:T(8,128)(2,1)S(1)} %collective-permute-done.21.rest_6_), channel_id=1, source_target_pairs={{0,8},{8,0},{16,24},{24,16},{1,9},{9,1},{17,25},{25,17},{2,10},{10... | collective-permute-start | bytes 1769480 | tf_op jit(solution)/shard_map/ppermute | solution.py:18
  117.1 7.8 %collective-permute-start.23 = (bf16[16,304,128]{2,1,0:T(8,128)(2,1)}, bf16[16,304,128]{2,1,0:T(8,128)(2,1)S(1)}, u32[]{:S(2)}, u32[]{:S(2)}) collective-permute-start(bf16[16,304,128]{2,1,0:T(8,128)(2,1)} %get-tuple-element.78), channel_id=1, source_target_pairs={{0,8},{8,0},{16,24},{24,16},{1,9},{9,1},{17,25},{25,17},{2,10},{10... | collective-permute-start | bytes 3735560 | tf_op jit(solution)/shard_map/ppermute | solution.py:18
  117.4 11.3 %collective-permute-start.24 = (bf16[16,304,128]{2,1,0:T(8,128)(2,1)}, bf16[16,304,128]{2,1,0:T(8,128)(2,1)}, u32[]{:S(2)}, u32[]{:S(2)}) collective-permute-start(bf16[16,304,128]{2,1,0:T(8,128)(2,1)} %get-tuple-element.80), channel_id=1, source_target_pairs={{0,8},{8,0},{16,24},{24,16},{1,9},{9,1},{17,25},{25,17},{2,10},{10... | collective-permute-start | bytes 3735560 | tf_op jit(solution)/shard_map/ppermute | solution.py:18
  141.0 4.4 %collective-permute-start.25 = (bf16[4,4,2,1024]{3,2,1,0:T(2,128)(2,1)S(1)}, bf16[4,4,2,1024]{3,2,1,0:T(2,128)(2,1)S(1)}, u32[]{:S(2)}, u32[]{:S(2)}) collective-permute-start(bf16[4,4,2,1024]{3,2,1,0:T(2,128)(2,1)S(1)} %slice.175), channel_id=1, source_target_pairs={{0,1},{1,0},{2,3},{3,2},{4,5},{5,4},{6,7},{7,6},{8,9},{9,8},{10,11... | collective-permute-start | bytes 196616 | tf_op jit(solution)/shard_map/ppermute | solution.py:18
  142.9 15.9 %collective-permute-start.28 = (bf16[8,304,128]{2,1,0:T(8,128)(2,1)S(1)}, bf16[8,304,128]{2,1,0:T(8,128)(2,1)S(1)}, u32[]{:S(2)}, u32[]{:S(2)}) collective-permute-start(bf16[8,304,128]{2,1,0:T(8,128)(2,1)S(1)} %copy-done.5), channel_id=1, source_target_pairs={{0,16},{8,24},{16,0},{24,8},{1,17},{9,25},{17,1},{25,9},{2,18},{10... | collective-permute-start | bytes 1867784 | tf_op jit(solution)/shard_map/ppermute | solution.py:18
  146.4 4.0 %collective-permute-start.26 = (bf16[2,4,2,1024]{3,2,1,0:T(2,128)(2,1)S(1)}, bf16[2,4,2,1024]{3,2,1,0:T(2,128)(2,1)S(1)}, u32[]{:S(2)}, u32[]{:S(2)}) collective-permute-start(bf16[2,4,2,1024]{3,2,1,0:T(2,128)(2,1)S(1)} %slice.221), channel_id=1, source_target_pairs={{0,2},{1,3},{2,0},{3,1},{4,6},{5,7},{6,4},{7,5},{8,10},{9,11},{10,... | collective-permute-start | bytes 98312 | tf_op jit(solution)/shard_map/ppermute | solution.py:18
  150.4 4.8 %collective-permute-start.27 = (bf16[1,4,2,1024]{3,2,1,0:T(2,128)(2,1)S(1)}, bf16[1,4,2,1024]{3,2,1,0:T(2,128)(2,1)S(1)}, u32[]{:S(2)}, u32[]{:S(2)}) collective-permute-start(bf16[1,4,2,1024]{3,2,1,0:T(2,128)(2,1)S(1)} %slice.223), channel_id=1, source_target_pairs={{0,4},{1,5},{2,6},{3,7},{4,0},{5,1},{6,2},{7,3},{8,12},{9,13},{10,... | collective-permute-start | bytes 49160 | tf_op jit(solution)/shard_map/ppermute | solution.py:18
  153.4 17.1 %collective-permute-start.29 = (bf16[8,304,128]{2,1,0:T(8,128)(2,1)}, bf16[8,304,128]{2,1,0:T(8,128)(2,1)S(1)}, u32[]{:S(2)}, u32[]{:S(2)}) collective-permute-start(bf16[8,304,128]{2,1,0:T(8,128)(2,1)} %get-tuple-element.117.rest_7_), channel_id=1, source_target_pairs={{0,1},{1,0},{2,3},{3,2},{4,5},{5,4},{6,7},{7,6},{8,9},{9,8},{10,11... | collective-permute-start | bytes 1867784 | tf_op jit(solution)/shard_map/ppermute | solution.py:18
  159.7 11.0 %copy-start.10 = (bf16[4,304,128]{2,1,0:T(8,128)(2,1)}, bf16[4,304,128]{2,1,0:T(8,128)(2,1)S(1)}, u32[]{:S(2)}) copy-start(bf16[4,304,128]{2,1,0:T(8,128)(2,1)S(1)} %get-tuple-element.127.rest_1_) | copy-start | bytes 933892
  159.7 23.5 %collective-permute-start.38 = (bf16[4,304,128]{2,1,0:T(8,128)(2,1)S(1)}, bf16[4,304,128]{2,1,0:T(8,128)(2,1)S(1)}, u32[]{:S(2)}, u32[]{:S(2)}) collective-permute-start(bf16[4,304,128]{2,1,0:T(8,128)(2,1)S(1)} %get-tuple-element.127.rest_1_), channel_id=1, source_target_pairs={{0,1},{1,0},{2,3},{3,2},{4,5},{5,4},{6,7},{7,6},{8,9},{9,8},{10,11... | collective-permute-start | bytes 933896 | tf_op jit(solution)/shard_map/ppermute | solution.py:18
  171.5 11.8 %collective-permute-start.39 = (bf16[4,304,128]{2,1,0:T(8,128)(2,1)S(1)}, bf16[4,304,128]{2,1,0:T(8,128)(2,1)S(1)}, u32[]{:S(2)}, u32[]{:S(2)}) collective-permute-start(bf16[4,304,128]{2,1,0:T(8,128)(2,1)S(1)} %get-tuple-element.125.rest_3_), channel_id=1, source_target_pairs={{0,16},{8,24},{16,0},{24,8},{1,17},{9,25},{17,1},{25,9},{2,18},{10... | collective-permute-start | bytes 933896 | tf_op jit(solution)/shard_map/ppermute | solution.py:18
  182.7 4.6 %collective-permute-start.30 = (bf16[16,112,128]{2,1,0:T(8,128)(2,1)}, bf16[16,112,128]{2,1,0:T(8,128)(2,1)S(1)}, u32[]{:S(2)}, u32[]{:S(2)}) collective-permute-start(bf16[16,112,128]{2,1,0:T(8,128)(2,1)} %get-tuple-element.91), channel_id=1, source_target_pairs={{0,8},{8,0},{16,24},{24,16},{1,9},{9,1},{17,25},{25,17},{2,10},{10... | collective-permute-start | bytes 1376264 | tf_op jit(solution)/shard_map/ppermute | solution.py:18
  182.8 6.0 %collective-permute-start.33 = (bf16[16,112,128]{2,1,0:T(8,128)(2,1)}, bf16[16,112,128]{2,1,0:T(8,128)(2,1)S(1)}, u32[]{:S(2)}, u32[]{:S(2)}) collective-permute-start(bf16[16,112,128]{2,1,0:T(8,128)(2,1)} %get-tuple-element.93), channel_id=1, source_target_pairs={{0,8},{8,0},{16,24},{24,16},{1,9},{9,1},{17,25},{25,17},{2,10},{10... | collective-permute-start | bytes 1376264 | tf_op jit(solution)/shard_map/ppermute | solution.py:18
  186.9 20.1 %collective-permute-start.40 = (bf16[2,608,128]{2,1,0:T(8,128)(2,1)}, bf16[2,608,128]{2,1,0:T(8,128)(2,1)S(1)}, u32[]{:S(2)}, u32[]{:S(2)}) collective-permute-start(bf16[2,608,128]{2,1,0:T(8,128)(2,1)} %get-tuple-element.102), channel_id=1, source_target_pairs={{0,2},{1,3},{2,0},{3,1},{4,6},{5,7},{6,4},{7,5},{8,10},{9,11},{10,... | collective-permute-start | bytes 933896 | tf_op jit(solution)/shard_map/ppermute | solution.py:18
  187.4 7.4 %collective-permute-start.31 = (bf16[8,112,128]{2,1,0:T(8,128)(2,1)S(1)}, bf16[8,112,128]{2,1,0:T(8,128)(2,1)S(1)}, u32[]{:S(2)}, u32[]{:S(2)}) collective-permute-start(bf16[8,112,128]{2,1,0:T(8,128)(2,1)S(1)} %slice.235), channel_id=1, source_target_pairs={{0,16},{8,24},{16,0},{24,8},{1,17},{9,25},{17,1},{25,9},{2,18},{10... | collective-permute-start | bytes 688136 | tf_op jit(solution)/shard_map/ppermute | solution.py:18
  189.0 8.3 %collective-permute-start.34 = (bf16[8,112,128]{2,1,0:T(8,128)(2,1)S(1)}, bf16[8,112,128]{2,1,0:T(8,128)(2,1)S(1)}, u32[]{:S(2)}, u32[]{:S(2)}) collective-permute-start(bf16[8,112,128]{2,1,0:T(8,128)(2,1)S(1)} %pad_maximum_fusion.6), channel_id=1, source_target_pairs={{0,1},{1,0},{2,3},{3,2},{4,5},{5,4},{6,7},{7,6},{8,9},{9,8},{10,11... | collective-permute-start | bytes 688136 | tf_op jit(solution)/shard_map/ppermute | solution.py:18
  195.5 4.8 %collective-permute-start.32 = (bf16[4,112,128]{2,1,0:T(8,128)(2,1)S(1)}, bf16[4,112,128]{2,1,0:T(8,128)(2,1)S(1)}, u32[]{:S(2)}, u32[]{:S(2)}) collective-permute-start(bf16[4,112,128]{2,1,0:T(8,128)(2,1)S(1)} %get-tuple-element.135), channel_id=1, source_target_pairs={{0,1},{1,0},{2,3},{3,2},{4,5},{5,4},{6,7},{7,6},{8,9},{9,8},{10,11... | collective-permute-start | bytes 344072 | tf_op jit(solution)/shard_map/ppermute | solution.py:18
  198.0 4.8 %collective-permute-start.35 = (bf16[4,112,128]{2,1,0:T(8,128)(2,1)S(1)}, bf16[4,112,128]{2,1,0:T(8,128)(2,1)S(1)}, u32[]{:S(2)}, u32[]{:S(2)}) collective-permute-start(bf16[4,112,128]{2,1,0:T(8,128)(2,1)S(1)} %get-tuple-element.133), channel_id=1, source_target_pairs={{0,16},{8,24},{16,0},{24,8},{1,17},{9,25},{17,1},{25,9},{2,18},{10... | collective-permute-start | bytes 344072 | tf_op jit(solution)/shard_map/ppermute | solution.py:18
  205.3 5.1 %collective-permute-start.36 = (bf16[2,224,128]{2,1,0:T(8,128)(2,1)}, bf16[2,224,128]{2,1,0:T(8,128)(2,1)S(1)}, u32[]{:S(2)}, u32[]{:S(2)}) collective-permute-start(bf16[2,224,128]{2,1,0:T(8,128)(2,1)} %get-tuple-element.95), channel_id=1, source_target_pairs={{0,2},{1,3},{2,0},{3,1},{4,6},{5,7},{6,4},{7,5},{8,10},{9,11},{10,... | collective-permute-start | bytes 344072 | tf_op jit(solution)/shard_map/ppermute | solution.py:18
  209.5 8.8 %collective-permute-start.41 = (bf16[1,608,128]{2,1,0:T(8,128)(2,1)}, bf16[1,608,128]{2,1,0:T(8,128)(2,1)S(1)}, u32[]{:S(2)}, u32[]{:S(2)}) collective-permute-start(bf16[1,608,128]{2,1,0:T(8,128)(2,1)} %get-tuple-element.104), channel_id=1, source_target_pairs={{0,4},{1,5},{2,6},{3,7},{4,0},{5,1},{6,2},{7,3},{8,12},{9,13},{10,... | collective-permute-start | bytes 466952 | tf_op jit(solution)/shard_map/ppermute | solution.py:18
  212.7 8.2 %collective-permute-start.37 = (bf16[1,224,128]{2,1,0:T(8,128)(2,1)}, bf16[1,224,128]{2,1,0:T(8,128)(2,1)S(1)}, u32[]{:S(2)}, u32[]{:S(2)}) collective-permute-start(bf16[1,224,128]{2,1,0:T(8,128)(2,1)} %get-tuple-element.97), channel_id=1, source_target_pairs={{0,4},{1,5},{2,6},{3,7},{4,0},{5,1},{6,2},{7,3},{8,12},{9,13},{10,... | collective-permute-start | bytes 172040 | tf_op jit(solution)/shard_map/ppermute | solution.py:18
  (24 other events, 75.3 us)

commit v3 on v2

--- a/solution.py
+++ b/solution.py
@@ -43,7 +43,8 @@
 
 def gather_outer(state):
     for stage in outer_stages():
-        state = jnp.concatenate([state, swap(state, *stage)], 0)
+        theirs = swap(state, *stage)
+        state = jnp.concatenate([state, theirs], 0)
     return state
 
 
@@ -51,9 +52,11 @@
     half = state.shape[1] // 2
     outer = outer_stages()
     pieces = []
-    for first, order in ((0, (X_STAGE, Y_STAGE)), (half, (Y_STAGE, X_STAGE))):
+    for k, order in enumerate(((X_STAGE, Y_STAGE), (Y_STAGE, X_STAGE))):
+        first = k * half
         part = state[:, first : first + half]
-        part = jnp.concatenate([part, swap(part, *order[0])], 0)
+        theirs = swap(part, *order[0])
+        part = jnp.concatenate([part, theirs], 0)
         far = swap(part, *order[1])
         ids = relative_ids(outer + [order[0]])
         full = relative_ids(outer + list(order))
@@ -421,18 +424,47 @@
     return pl.BlockSpec((shape[0], 1) + tuple(shape[2:]), lambda i: (0, i + first, 0, 0))
 
 
-def project(inputs, shards, slices, pieces, wide, lines, tiles):
+def span_means(inputs):
     count, rows, width = inputs.shape
     half = rows // 2
+
+    def kernel(x_ref, out_ref):
+        unit, _ = norm_parts(x_ref[0].astype(F32))
+        for j in range(2):
+            mean = jnp.sum(unit[j * half : (j + 1) * half], 0, keepdims=True) / half
+            high = mean.astype(BF16)
+            out_ref[0, j : j + 1, :width] = high
+            out_ref[0, j : j + 1, width:] = (mean - high.astype(F32)).astype(BF16)
+
+    shape = (count, 2, 2 * width)
+    return pl.pallas_call(
+        kernel,
+        cost_estimate=cost(3),
+        grid=(count,),
+        in_specs=[each(inputs.shape)],
+        out_specs=each(shape),
+        out_shape=jax.ShapeDtypeStruct(shape, BF16),
+    )(inputs)
+
+
+def far_means(ref):
+    rows = jnp.concatenate([ref[p, 0].astype(F32) for p in range(ref.shape[0])], 0)
+    width = rows.shape[1] // 2
+    return rows[:, :width] + rows[:, width:]
+
+
+def project(inputs, means, shards, slices, pieces, wide, lines, tiles):
+    count, rows, width = inputs.shape
+    far = 2 * means.shape[0]
     hidden = slices[5].shape[0] * lax.axis_size("seq")
     segments = columns(shards) + [("vec", VEC_ROWS)]
     targets = spots(shards)
     order = (0, 1, 2, 3, 4, 6)
     arrays = [piece for piece, _, _ in pieces] if tiles else list(wide) + list(lines)
 
-    def kernel(spot, x_ref, *refs):
+    def kernel(spot, x_ref, means_ref, *refs):
         ins = refs[: len(arrays)]
-        out_ref, pooled_ref, q_ref, k_ref, v_ref, narrow_ref, wide_ref = refs[len(arrays) :]
+        out_ref, sums_ref, q_ref, k_ref, v_ref, narrow_ref, wide_ref = refs[len(arrays) :]
 
         @pl.when(pl.program_id(0) == 0)
         def _():
@@ -464,27 +496,34 @@
         unit, _ = norm_parts(x_ref[0].astype(F32))
         normed = (unit * narrow_ref[0:1, :] + narrow_ref[1:2, :]).astype(BF16)
         out_ref[0, :, :width] = dot(normed, q_ref[...]).astype(BF16)
+        mean = far_means(means_ref) * narrow_ref[0:1, :] + narrow_ref[1:2, :]
+        high = mean.astype(BF16)
+        low = (mean - high.astype(F32)).astype(BF16)
+        joined = jnp.concatenate([normed, high, low], 0)
         for k, ref in enumerate((k_ref, v_ref)):
-            product = dot(normed, ref[...])
-            out_ref[0, :, (k + 1) * width : (k + 2) * width] = product.astype(BF16)
-            for j in range(2):
-                mean = jnp.sum(product[j * half : (j + 1) * half], 0, keepdims=True) / half
-                pooled_ref[0, j : j + 1, k * width : (k + 1) * width] = mean.astype(BF16)
-
-    shapes = [(count, rows, 3 * width), (count, 2, 2 * width)]
+            product = dot(joined, ref[...])
+            out_ref[0, :, (k + 1) * width : (k + 2) * width] = product[:rows].astype(BF16)
+            total = product[rows : rows + far] + product[rows + far :]
+            sums_ref[0, :, k * width : (k + 1) * width] = total.astype(BF16)
+
+    shapes = [(count, rows, 3 * width), (count, far, 2 * width)]
     square = (width, width)
     return pl.pallas_call(
         kernel,
         cost_estimate=cost(6),
         grid=(count,),
-        in_specs=[pl.BlockSpec(memory_space=pltpu.SMEM), each(inputs.shape)]
+        in_specs=[
+            pl.BlockSpec(memory_space=pltpu.SMEM),
+            each(inputs.shape),
+            spread(means.shape),
+        ]
         + [pl.BlockSpec(memory_space=pltpu.VMEM)] * len(arrays),
         out_specs=[each(shape) for shape in shapes]
         + [full(square)] * 3
         + [full((NARROW, width)), full((1, hidden))],
         out_shape=[jax.ShapeDtypeStruct(shape, BF16) for shape in shapes + [square] * 3]
         + [jax.ShapeDtypeStruct((NARROW, width), F32), jax.ShapeDtypeStruct((1, hidden), F32)],
-    )(place(), inputs, *arrays)
+    )(place(), inputs, means, *arrays)
 
 
 def head_mask(rows, lane_half):
@@ -512,11 +551,11 @@
 
 def attend(qkv, summaries):
     count, rows, width = qkv.shape[0], qkv.shape[1], qkv.shape[2] // 3
-    far = 2 * summaries.shape[0]
+    far = summaries.shape[1]
 
     def kernel(spot, qkv_ref, sum_ref, mixed_ref, lse_ref):
         seen = seen_rows(spot[0], far, rows)
-        spans = jnp.concatenate([sum_ref[p, 0] for p in range(far // 2)], 0)
+        spans = sum_ref[0]
         for pair in range(HEADS // 2):
             at = pair * 2 * HEAD
             query = qkv_ref[0, :, at : at + 2 * HEAD]
@@ -555,7 +594,7 @@
         in_specs=[
             pl.BlockSpec(memory_space=pltpu.SMEM),
             each(qkv.shape),
-            spread(summaries.shape),
+            each(summaries.shape),
         ],
         out_specs=[each(block), each((count, HEADS, rows))],
         out_shape=[
@@ -706,7 +745,7 @@
 
 def attend_back(qkv, summaries, lse, mixed_grad, first, number, before=(), after=()):
     _, rows, width = mixed_grad.shape
-    far = 2 * summaries.shape[0]
+    far = summaries.shape[1]
     extra = list(before) + list(after)
 
     def each(shape):
@@ -717,7 +756,7 @@
     def kernel(spot, qkv_ref, sum_ref, lse_ref, grad_ref, *rest):
         dq_ref, dk_ref, dv_ref, far_ref = rest[len(extra) :]
         seen = seen_rows(spot[0], far, rows)
-        spans = jnp.concatenate([sum_ref[p, 0] for p in range(far // 2)], 0)
+        spans = sum_ref[0]
         for pair in range(HEADS // 2):
             at = pair * 2 * HEAD
             lanes = slice(at, at + 2 * HEAD)
@@ -748,13 +787,11 @@
                 d_query = d_query + dot(only(keys, side), slope, 0, 0)
             d_keys = d_keys * HEAD ** (-0.5)
             dq_ref[0, :, lanes] = (d_query * HEAD ** (-0.5)).T.astype(BF16)
-            dk_ref[0, :, lanes] = d_keys[:rows]
-            dv_ref[0, :, lanes] = d_values[:rows]
+            dk_ref[0, :, lanes] = d_keys[:rows].astype(BF16)
+            dv_ref[0, :, lanes] = d_values[:rows].astype(BF16)
             for k, terms in enumerate((d_keys, d_values)):
                 left = k * width + at
-                for p in range(far // 2):
-                    part = terms[rows + 2 * p : rows + 2 * p + 2].astype(BF16)
-                    far_ref[p, 0, :, left : left + 2 * HEAD] = part
+                far_ref[0, :, left : left + 2 * HEAD] = terms[rows:].astype(BF16)
 
     block = mixed_grad.shape
     return pl.pallas_call(
@@ -764,16 +801,16 @@
         in_specs=[
             pl.BlockSpec(memory_space=pltpu.SMEM),
             each(qkv.shape),
-            spread(summaries.shape, first),
+            each(summaries.shape),
             each(lse.shape),
             each(block),
         ]
         + [pl.BlockSpec(memory_space=pl.ANY)] * len(extra),
-        out_specs=[each(block)] * 3 + [spread(summaries.shape, first)],
+        out_specs=[each(block)] * 3 + [each(summaries.shape)],
         out_shape=[
             jax.ShapeDtypeStruct(block, BF16),
-            jax.ShapeDtypeStruct(block, F32),
-            jax.ShapeDtypeStruct(block, F32),
+            jax.ShapeDtypeStruct(block, BF16),
+            jax.ShapeDtypeStruct(block, BF16),
             jax.ShapeDtypeStruct(summaries.shape, BF16),
         ],
         input_output_aliases={5 + k: k for k in range(len(before))},
@@ -781,19 +818,17 @@
 
 
 def project_back(
-    inputs, d_query, d_keys, d_values, owned, weights, narrow, middle_grad, shards, tiles, after
+    inputs, d_query, d_keys, d_values, terms, means, weights, narrow, shards, tiles
 ):
     count, rows, width = inputs.shape
-    half_span = rows // 2
     segments = columns(shards) + [("vec", VEC_ROWS)]
     targets = spots(shards)
     orders = pack_order() if tiles else None
     half = sum(size for _, size in segments) // 2
     per = width // lax.axis_size("seq")
 
-    def kernel(spot, x_ref, dq_ref, dk_ref, dv_ref, own_ref, wq_ref, wk_ref, wv_ref,
-               lines_ref, mgrad_ref, *rest):
-        igrad_ref, narrow_ref, *rest = rest[len(after) :]
+    def kernel(spot, x_ref, dq_ref, dk_ref, dv_ref, terms_ref, means_ref, wq_ref, wk_ref, wv_ref,
+               lines_ref, back_ref, far_ref, narrow_ref, *rest):
         gain, shift = lines_ref[0:1, :], lines_ref[1:2, :]
         if tiles:
             packs, (gq_ref, gk_ref, gv_ref, high_ref) = rest[:4], rest[4:]
@@ -806,26 +841,30 @@
             for ref in (gq_ref, gk_ref, gv_ref, narrow_ref):
                 ref[...] = jnp.zeros_like(ref)
 
-        unit, scale = norm_parts(x_ref[0].astype(F32))
-        flipped = (unit * gain + shift).astype(BF16).T
-        back = dot(dq_ref[0], wq_ref[...], 1, 1)
-        gq_ref[...] += dot(flipped, dq_ref[0])
+        unit, _ = norm_parts(x_ref[0].astype(F32))
+        unit_far = far_means(means_ref)
+        joined = jnp.concatenate([unit, unit_far], 0)
+        flipped = (joined * gain + shift).astype(BF16).T
+        gq_ref[...] += dot(flipped[:, :rows], dq_ref[0])
+        both = None
         for k, (direct, w_ref, g_ref) in enumerate(
             ((dk_ref, wk_ref, gk_ref), (dv_ref, wv_ref, gv_ref))
         ):
-            act = jnp.concatenate(
-                [
-                    direct[0, j * half_span : (j + 1) * half_span, :]
-                    + own_ref[0, j : j + 1, k * width : (k + 1) * width] / half_span
-                    for j in range(2)
-                ],
-                0,
-            ).astype(BF16)
+            act = jnp.concatenate([direct[0], terms_ref[0, :, k * width : (k + 1) * width]], 0)
             g_ref[...] += dot(flipped, act)
-            back = back + dot(act, w_ref[...], 1, 1)
-        narrow_ref[0:1, :] += jnp.sum(back * unit, 0, keepdims=True)
-        narrow_ref[1:2, :] += jnp.sum(back, 0, keepdims=True)
-        igrad_ref[0] = mgrad_ref[0] + norm_back(back, unit, scale, gain)
+            part = dot(act, w_ref[...], 1, 1)
+            both = part if both is None else both + part
+        back = both[:rows] + dot(dq_ref[0], wq_ref[...], 1, 1)
+        far = both[rows:]
+        back_ref[0] = back
+        for p in range(far.shape[0] // 2):
+            far_ref[p, 0] = far[2 * p : 2 * p + 2].astype(BF16)
+        narrow_ref[0:1, :] += jnp.sum(back * unit, 0, keepdims=True) + jnp.sum(
+            far * unit_far, 0, keepdims=True
+        )
+        narrow_ref[1:2, :] += jnp.sum(both, 0, keepdims=True) + jnp.sum(
+            back - both[:rows], 0, keepdims=True
+        )
 
         if tiles:
 
@@ -846,8 +885,13 @@
 
     block = inputs.shape
     square = (width, width)
-    out_shape = [jax.ShapeDtypeStruct(block, F32), jax.ShapeDtypeStruct((8, width), F32)]
-    out_specs = [each(block), full((8, width))]
+    sent = means.shape[:3] + (width,)
+    out_shape = [
+        jax.ShapeDtypeStruct(block, F32),
+        jax.ShapeDtypeStruct(sent, BF16),
+        jax.ShapeDtypeStruct((8, width), F32),
+    ]
+    out_specs = [each(block), spread(sent), full((8, width))]
     scratch = []
     if tiles:
         packed_shapes = [(len(names) // 2, half, 128) for names in orders for _ in range(2)]
@@ -863,14 +907,39 @@
         grid=(count,),
         in_specs=[pl.BlockSpec(memory_space=pltpu.SMEM)]
         + [each(block)] * 4
-        + [each(owned.shape)]
+        + [each(terms.shape), spread(means.shape)]
         + [full(square)] * 3
-        + [full(narrow.shape), each(block)]
-        + [pl.BlockSpec(memory_space=pl.ANY)] * len(after),
+        + [full(narrow.shape)],
         out_specs=out_specs,
         out_shape=out_shape,
         scratch_shapes=scratch,
-    )(place(), inputs, d_query, d_keys, d_values, owned, *weights, narrow, middle_grad, *after)
+    )(place(), inputs, d_query, d_keys, d_values, terms, means, *weights, narrow)
+
+
+def input_back(inputs, back, owned, narrow, middle_grad):
+    count, rows, _ = inputs.shape
+    half = rows // 2
+
+    def kernel(x_ref, back_ref, own_ref, lines_ref, mgrad_ref, out_ref):
+        unit, scale = norm_parts(x_ref[0].astype(F32))
+        back = jnp.concatenate(
+            [
+                back_ref[0, j * half : (j + 1) * half, :] + own_ref[0, j : j + 1, :] / half
+                for j in range(2)
+            ],
+            0,
+        )
+        out_ref[0] = mgrad_ref[0] + norm_back(back, unit, scale, lines_ref[0:1, :])
+
+    return pl.pallas_call(
+        kernel,
+        cost_estimate=cost(4),
+        grid=(count,),
+        in_specs=[each(inputs.shape)] * 2
+        + [each(owned.shape), full(narrow.shape), each(inputs.shape)],
+        out_specs=each(inputs.shape),
+        out_shape=jax.ShapeDtypeStruct(inputs.shape, F32),
+    )(inputs, back, owned, narrow, middle_grad)
 
 
 def layer(
@@ -907,10 +976,10 @@
             jnp.concatenate([jnp.stack([members[k] for k in (0, 1, 2, 3, 4, 6)]), blank]),
             members[5][None],
         )
-    qkv, pooled, w_query, w_key, w_value, narrow, long_bias = project(
-        inputs, shards[:3], slices, early, wide[:3], lines, tiles
+    means = gather_seq(span_means(inputs))
+    qkv, summaries, w_query, w_key, w_value, narrow, long_bias = project(
+        inputs, means, shards[:3], slices, early, wide[:3], lines, tiles
     )
-    summaries = gather_seq(pooled)
     mixed, lse = attend(qkv, summaries)
     outputs, middle_grad, mixed_grad, narrow_two, wide_two, *second = feed(
         inputs, cotangent, mixed, narrow, long_bias, late, wide[3:], shards[3:], tiles
@@ -923,26 +992,23 @@
     d_query, d_keys, d_values, terms = attend_back(
         qkv, summaries, lse, mixed_grad, count // 2, count - count // 2, begun, ties
     )
-    if tiles:
-        second = reduce_step(second, 1)
-        ties = [member for couple in second for member in couple]
-    owned = reduce_seq(terms)
-    input_grad, narrow_one, *first = project_back(
+    back, far_back, narrow_one, *first = project_back(
         inputs,
         d_query,
         d_keys,
         d_values,
-        owned,
+        terms,
+        means,
         (w_query, w_key, w_value),
         narrow,
-        middle_grad,
         shards[:3],
         tiles,
-        ties,
     )
+    owned = reduce_seq(far_back)
+    input_grad = input_back(inputs, back, owned, narrow, middle_grad)
     if tiles:
         size = norm1_gain.shape[0]
-        second = reduce_step(second, 2, True)
+        second = reduce_step(reduce_step(second, 1), 2, True)
         first = reduce_step([tuple(first[:2]), tuple(first[2:])], 0)
         first = reduce_step(reduce_step(first, 1), 2, True)
         tail = reduce_end(second, shards[3:], [size] * 4 + [up_bias.shape[0]])

time: 224 us -> 211 us (0.942)
  starting transfers between devices: 48.3 us -> 37.1 us
  Pallas kernels: 87.9 us -> 96.9 us
  waiting for transfers between devices: 56.9 us -> 48.4 us
    ppermute x42, starting transfers between devices: 48.3 us -> 37.1 us  [swap(): return lax.ppermute(array, axis, [(i, i ^ bit) for i in range(count)])]
    pallas_call x0 -> x2, Pallas kernels: none -> 8.71 us  [the longest x1 5.08 us: input_back(): pl.pallas_call(kernel, cost_estimate=cost(4), grid=(count,), in_specs=[ea...]
    ppermute x42, waiting for transfers between devices: 56.9 us -> 48.4 us  [swap(): return lax.ppermute(array, axis, [(i, i ^ bit) for i in range(count)])]
    unnamed x60 -> x56, local copies, waits for them, and re-layouts: 8.8 us -> 8.01 us
  transfers between devices with their start and end apart: 42 -> 42, of which waited for: 18 -> 18; matrix products, arithmetic and copies ran while one was open for 5% -> 5% of each run, Pallas kernels for 18% -> 19%
where the time goes in v3:
time: 211 us; the launch traced here: 210 us
  Pallas kernels  96.9 us (46%)
  waiting for transfers between devices  48.4 us (23%)
  starting transfers between devices  37.1 us (18%)
  local copies, waits for them, and re-layouts  14 us (7%)
  other arithmetic  12.4 us (6%)
    ppermute x42, waiting for transfers between devices, swap(): return lax.ppermute(array, axis, [(i, i ^ bit) for i in range(count)])  48.4 us
    ppermute x42, starting transfers between devices, swap(): return lax.ppermute(array, axis, [(i, i ^ bit) for i in range(count)])  37.1 us
    pallas_call x1, Pallas kernels, feed(): pl.pallas_call(kernel, cost_estimate=cost(35), grid=(count,), in_specs=[p...  35.4 us
    pallas_call x2, Pallas kernels, attend_back(): pl.pallas_call(kernel, cost_estimate=cost(7), grid=(number,), in_specs=[p...  13.9 us
    pallas_call x1, Pallas kernels, project_back(): pl.pallas_call(kernel, cost_estimate=cost(10), grid=(count,), in_specs=[p...  10.6 us
    unnamed x56, local copies, waits for them, and re-layouts  8.01 us
    pallas_call x1, Pallas kernels, attend(): pl.pallas_call(kernel, cost_estimate=cost(8), grid=(count,), in_specs=[pl...  7.72 us
    pallas_call x1, Pallas kernels, project(): pl.pallas_call(kernel, cost_estimate=cost(6), grid=(count,), in_specs=[pl...  6.71 us
  transfers between devices with their start and end apart: 42, of which 18 were waited for; matrix products, arithmetic and copies ran while one was open for 5% of the time, Pallas kernels for 19%

profile of v3, /device:TPU:0, one launch (start us, length us, event | category | flops | bytes accessed | tf_op | source)
XLA Modules:
  0.0 210.0 jit_solution(969188740103566340)
XLA Ops:
  1.3 1.5 shard_map.263
  2.8 4.1 %collective-permute-start.3 = (bf16[1,224,128]{2,1,0:T(8,128)(2,1)}, bf16[1,224,128]{2,1,0:T(8,128)(2,1)S(1)}, u32[]{:S(2)}, u32[]{:S(2)}) collective-permute-start(bf16[1,224,128]{2,1,0:T(8,128)(2,1)} %shard_map.263), channel_id=1, source_target_pairs={{0,4},{1,5},{2,6},{3,7},{4,0},{5,1},{6,2},{7,3},{8,12},{9,13},{10,... | collective-permute-start | bytes 172040 | tf_op jit(solution)/shard_map/ppermute | solution.py:18
  6.9 3.0 %collective-permute-done.3 = bf16[1,224,128]{2,1,0:T(8,128)(2,1)S(1)} collective-permute-done((bf16[1,224,128]{2,1,0:T(8,128)(2,1)}, bf16[1,224,128]{2,1,0:T(8,128)(2,1)S(1)}, u32[]{:S(2)}, u32[]{:S(2)}) %collective-permute-start.3) | collective-permute-done | bytes 57376 | tf_op jit(solution)/shard_map/ppermute | solution.py:18
  10.7 1.4 collective-permute-start.4
  12.1 3.5 %collective-permute-done.4 = bf16[2,224,128]{2,1,0:T(8,128)(2,1)S(1)} collective-permute-done((bf16[2,224,128]{2,1,0:T(8,128)(2,1)S(1)}, bf16[2,224,128]{2,1,0:T(8,128)(2,1)S(1)}, u32[]{:S(2)}, u32[]{:S(2)}) %collective-permute-start.4) | collective-permute-done | bytes 114720 | tf_op jit(solution)/shard_map/ppermute | solution.py:18
  15.6 1.5 pad_maximum_fusion.8.refs_3_
  17.1 1.6 shard_map.266
  18.7 2.5 %collective-permute-start.13 = (bf16[1,576,128]{2,1,0:T(8,128)(2,1)}, bf16[1,576,128]{2,1,0:T(8,128)(2,1)S(1)}, u32[]{:S(2)}, u32[]{:S(2)}) collective-permute-start(bf16[1,576,128]{2,1,0:T(8,128)(2,1)} %shard_map.266), channel_id=1, source_target_pairs={{0,4},{1,5},{2,6},{3,7},{4,0},{5,1},{6,2},{7,3},{8,12},{9,13},{10,... | collective-permute-start | bytes 442376 | tf_op jit(solution)/shard_map/ppermute | solution.py:18
  21.1 3.6 %shard_map.262 = bf16[4,2,1024]{2,1,0:T(2,128)(2,1)} custom-call(bf16[4,256,512]{2,1,0:T(8,128)(2,1)} %x_ref.9), custom_call_target="tpu_custom_call" | custom-call | flops 3000000000 | bytes 1048576 | tf_op jit(solution)/shard_map/pallas_call | solution.py:440
  25.2 1.6 collective-permute-done.13
  27.6 2.0 collective-permute-done
  30.4 2.2 %collective-permute-start.1 = (bf16[2,4,2,1024]{3,2,1,0:T(2,128)(2,1)S(1)}, bf16[2,4,2,1024]{3,2,1,0:T(2,128)(2,1)S(1)}, u32[]{:S(2)}, u32[]{:S(2)}) collective-permute-start(bf16[2,4,2,1024]{3,2,1,0:T(2,128)(2,1)S(1)} %pad_maximum_fusion.15), channel_id=1, source_target_pairs={{0,2},{1,3},{2,0},{3,1},{4,6},{5,7},{6,4},{7,5},{8,10},{9,11},{10,... | collective-permute-start | bytes 98312 | tf_op jit(solution)/shard_map/ppermute | solution.py:18
  32.6 1.6 collective-permute-start.9
  34.1 1.5 collective-permute-start.5
  36.3 3.8 %collective-permute-done.5 = bf16[4,112,128]{2,1,0:T(8,128)(2,1)S(1)} collective-permute-done((bf16[4,112,128]{2,1,0:T(8,128)(2,1)S(1)}, bf16[4,112,128]{2,1,0:T(8,128)(2,1)S(1)}, u32[]{:S(2)}, u32[]{:S(2)}) %collective-permute-start.5) | collective-permute-done | bytes 114720 | tf_op jit(solution)/shard_map/ppermute | solution.py:18
  40.8 1.5 collective-permute-start.15
  43.0 1.6 collective-permute-start.2
  44.7 2.0 collective-permute-done.7.refs_2_
  46.7 3.3 %collective-permute-done.11.refs_6_ = bf16[8,112,128]{2,1,0:T(8,128)(2,1)S(1)} collective-permute-done((bf16[8,112,128]{2,1,0:T(8,128)(2,1)S(1)}, bf16[8,112,128]{2,1,0:T(8,128)(2,1)S(1)}, u32[]{:S(2)}, u32[]{:S(2)}) %collective-permute-start.11) | collective-permute-done | bytes 229408 | tf_op jit(solution)/shard_map/ppermute | solution.py:18
  50.6 1.6 collective-permute-start.17
  52.2 1.5 collective-permute-start.21
  55.9 6.7 %shard_map.264 = (bf16[4,256,1536]{2,1,0:T(8,128)(2,1)}, bf16[4,16,1024]{2,1,0:T(8,128)(2,1)}, bf16[512,512]{1,0:T(8,128)(2,1)}, bf16[512,512]{1,0:T(8,128)(2,1)...) custom-call(s32[2]{0:T(128)} %pad_add_fusion.spot, bf16[4,256,512]{2,1,0:T(8,128)(2,1)} %x_ref.9, ...), custom_call_target="tpu_custom_call" | custom-call | flops 6000000000 | bytes 1048576 | tf_op jit(solution)/shard_map/pallas_call | solution.py:511
  63.2 2.7 %collective-permute-done.17.rest_2_ = bf16[8,288,128]{2,1,0:T(8,128)(2,1)S(1)} collective-permute-done((bf16[8,288,128]{2,1,0:T(8,128)(2,1)S(1)}, bf16[8,288,128]{2,1,0:T(8,128)(2,1)S(1)}, u32[]{:S(2)}, u32[]{:S(2)}) %collective-permute-start.17) | collective-permute-done | bytes 589856 | tf_op jit(solution)/shard_map/ppermute | solution.py:18
  67.2 7.7 %shard_map.265 = (bf16[4,256,512]{2,1,0:T(8,128)(2,1)}, f32[4,8,256]{2,1,0:T(8,128)}) custom-call(s32[2]{0:T(128)} %pad_add_fusion.spot, bf16[4,256,1536]{2,1,0:T(8,128)(2,1)} %get-tuple-element.66.qkv_ref, bf16[4,16,1024]{2,1,0:T(8,128)(2,1)} %get-tuple-element.67.sum_ref), custom_call_target="tpu_custom_call" | custom-call | flops 8000000000 | bytes 1048576 | tf_op jit(solution)/shard_map/pallas_call | solution.py:590
  75.7 35.4 %shard_map.267 = (bf16[4,256,512]{2,1,0:T(8,128)(2,1)}, f32[4,256,512]{2,1,0:T(8,128)}, bf16[4,256,512]{2,1,0:T(8,128)(2,1)}, f32[8,512]{1,0:T(8,128)}, f32[8,20...) custom-call(s32[2]{0:T(128)} %pad_add_fusion.spot, ...), custom_call_target="tpu_custom_call" | custom-call | flops 35000000512 | bytes 1048576 | tf_op jit(solution)/shard_map/pallas_call | solution.py:732
  111.8 6.9 %shard_map.268 = (bf16[4,256,512]{2,1,0:T(8,128)(2,1)}, bf16[4,256,512]{2,1,0:T(8,128)(2,1)}, bf16[4,256,512]{2,1,0:T(8,128)(2,1)}, bf16[4,16,1024]{2,1,0:T(8,128)(2,1)}) custom-call(s32[2]{0:T(128)} %pad_add_fusion.spot, bf16[4,256,1536]{2,1,0:T(8,128)(2,1)} %get-tuple-element.66.qkv_ref, bf16[4,16,1024]{2,1,0:T(8,128)(2,1)} %get-tuple-element.67.sum_ref, ...), custom_call_target="tpu_custom_call" | custom-call | flops 7000000000 | bytes 1048576 | tf_op jit(solution)/shard_map/pallas_call | solution.py:797
  119.7 1.6 add_convert_fusion
  124.0 1.6 add_convert_fusion.1
  126.8 7.0 %shard_map.269 = (bf16[4,256,512]{2,1,0:T(8,128)(2,1)}, bf16[4,256,512]{2,1,0:T(8,128)(2,1)}, bf16[4,256,512]{2,1,0:T(8,128)(2,1)}, bf16[4,16,1024]{2,1,0:T(8,128)(2,1)}) custom-call(s32[2]{0:T(128)} %pad_add_fusion.spot, bf16[4,256,1536]{2,1,0:T(8,128)(2,1)} %get-tuple-element.66.qkv_ref, ...), custom_call_target="tpu_custom_call", output_to_operand_aliasing={{0}: (5, {}), {1}: (6, {}), {2}: (7, {}), {3}: (8, {})} | custom-call | flops 7000000000 | bytes 1048576 | tf_op jit(solution)/shard_map/pallas_call | solution.py:797
  133.8 10.6 %shard_map.270 = (f32[4,256,512]{2,1,0:T(8,128)}, bf16[8,4,2,512]{3,2,1,0:T(2,128)(2,1)}, f32[8,512]{1,0:T(8,128)}, bf16[16,112,128]{2,1,0:T(8,128)(2,1)}, bf16[...) custom-call(s32[2]{0:T(128)} %pad_add_fusion.spot, ...), custom_call_target="tpu_custom_call" | custom-call | flops 10000000000 | bytes 1048576 | tf_op jit(solution)/shard_map/pallas_call | solution.py:904
  145.9 3.3 %collective-permute-done.25 = bf16[4,4,2,512]{3,2,1,0:T(2,128)(2,1)S(1)} collective-permute-done((bf16[4,4,2,512]{3,2,1,0:T(2,128)(2,1)S(1)}, bf16[4,4,2,512]{3,2,1,0:T(2,128)(2,1)S(1)}, u32[]{:S(2)}, u32[]{:S(2)}) %collective-permute-start.25) | collective-permute-done | bytes 32800 | tf_op jit(solution)/shard_map/ppermute | solution.py:18
  150.1 1.5 collective-permute-start.36
  152.3 1.6 collective-permute-done.26
  155.1 1.6 collective-permute-start.29
  157.7 9.4 %collective-permute-done.36 = bf16[8,304,128]{2,1,0:T(8,128)(2,1)S(1)} collective-permute-done((bf16[8,304,128]{2,1,0:T(8,128)(2,1)S(1)}, bf16[8,304,128]{2,1,0:T(8,128)(2,1)S(1)}, u32[]{:S(2)}, u32[]{:S(2)}) %collective-permute-start.36) | collective-permute-done | bytes 622624 | tf_op jit(solution)/shard_map/ppermute | solution.py:18
  169.8 1.3 collective-permute-start.39
  175.6 5.1 %collective-permute-done.30.refs_1_ = bf16[4,112,128]{2,1,0:T(8,128)(2,1)S(1)} collective-permute-done((bf16[4,112,128]{2,1,0:T(8,128)(2,1)S(1)}, bf16[4,112,128]{2,1,0:T(8,128)(2,1)S(1)}, u32[]{:S(2)}, u32[]{:S(2)}) %collective-permute-start.30) | collective-permute-done | bytes 114720 | tf_op jit(solution)/shard_map/ppermute | solution.py:18
  181.4 1.8 shard_map.272
  183.2 1.7 collective-permute-start.34
  185.7 2.2 %shard_map.275 = (bf16[2,608,128]{2,1,0:T(8,128)(2,1)}, bf16[2,608,128]{2,1,0:T(8,128)(2,1)}) custom-call(bf16[4,304,128]{2,1,0:T(8,128)(2,1)} %get-tuple-element.130.refs_0_, bf16[4,304,128]{2,1,0:T(8,128)(2,1)} %copy-done.15, bf16[4,304,128]{2,1,0:T(8,128)(2,1)} %get-tuple-element.128.refs_2_, bf16[4,304,128]{2,1,0:T(8,128)(2,1)} %copy-done.16), custom_call_target="tpu_custom_call" | custom-call | flops 2000000000 | bytes 1048576 | tf_op jit(solution)/shard_map/pallas_call | solution.py:191
  188.3 5.1 %shard_map.271 = f32[4,256,512]{2,1,0:T(8,128)} custom-call(bf16[4,256,512]{2,1,0:T(8,128)(2,1)} %x_ref.9, f32[4,256,512]{2,1,0:T(8,128)} %get-tuple-element.89.back_ref, f32[4,2,512]{2,1,0:T(2,128)} %add_bitcast_fusion.own_ref, f32[8,512]{1,0:T(8,128)} %get-tuple-element.69.lines_ref, f32[4,256,512]{2,1,0:T(8,128)} %get-tuple-element.91.mgrad_ref), custom_call_target="tpu_custom_call" | custom-call | flops 4000000000 | bytes 1048576 | tf_op jit(solution)/shard_map/pallas_call | solution.py:934
  194.0 1.6 shard_map.273
  197.2 1.8 shard_map.276
  199.1 2.0 collective-permute-start.41
  201.1 2.7 %collective-permute-done.35.theirs_ref = bf16[1,224,128]{2,1,0:T(8,128)(2,1)S(1)} collective-permute-done((bf16[1,224,128]{2,1,0:T(8,128)(2,1)}, bf16[1,224,128]{2,1,0:T(8,128)(2,1)S(1)}, u32[]{:S(2)}, u32[]{:S(2)}) %collective-permute-start.35) | collective-permute-done | bytes 57376 | tf_op jit(solution)/shard_map/ppermute | solution.py:18
  204.4 1.6 shard_map.274
  206.0 1.6 collective-permute-done.41.theirs_ref
  208.2 1.8 shard_map.277
  (151 shorter events, 34.4 us)
Async XLA Ops:
  2.8 7.0 %collective-permute-start.3 = (bf16[1,224,128]{2,1,0:T(8,128)(2,1)}, bf16[1,224,128]{2,1,0:T(8,128)(2,1)S(1)}, u32[]{:S(2)}, u32[]{:S(2)}) collective-permute-start(bf16[1,224,128]{2,1,0:T(8,128)(2,1)} %shard_map.263), channel_id=1, source_target_pairs={{0,4},{1,5},{2,6},{3,7},{4,0},{5,1},{6,2},{7,3},{8,12},{9,13},{10,... | collective-permute-start | bytes 172040 | tf_op jit(solution)/shard_map/ppermute | solution.py:18
  10.7 4.9 %collective-permute-start.4 = (bf16[2,224,128]{2,1,0:T(8,128)(2,1)S(1)}, bf16[2,224,128]{2,1,0:T(8,128)(2,1)S(1)}, u32[]{:S(2)}, u32[]{:S(2)}) collective-permute-start(bf16[2,224,128]{2,1,0:T(8,128)(2,1)S(1)} %pad_maximum_fusion.13), channel_id=1, source_target_pairs={{0,2},{1,3},{2,0},{3,1},{4,6},{5,7},{6,4},{7,5},{8,10},{9,11},{10,... | collective-permute-start | bytes 344072 | tf_op jit(solution)/shard_map/ppermute | solution.py:18
  18.7 13.9 %copy-start = (bf16[4,224,128]{2,1,0:T(8,128)(2,1)S(1)}, bf16[4,224,128]{2,1,0:T(8,128)(2,1)}, u32[]{:S(2)}) copy-start(bf16[4,224,128]{2,1,0:T(8,128)(2,1)} %pad_maximum_fusion.8.refs_3_) | copy-start | bytes 688132
  18.7 8.1 %collective-permute-start.13 = (bf16[1,576,128]{2,1,0:T(8,128)(2,1)}, bf16[1,576,128]{2,1,0:T(8,128)(2,1)S(1)}, u32[]{:S(2)}, u32[]{:S(2)}) collective-permute-start(bf16[1,576,128]{2,1,0:T(8,128)(2,1)} %shard_map.266), channel_id=1, source_target_pairs={{0,4},{1,5},{2,6},{3,7},{4,0},{5,1},{6,2},{7,3},{8,12},{9,13},{10,... | collective-permute-start | bytes 442376 | tf_op jit(solution)/shard_map/ppermute | solution.py:18
  24.7 4.8 %collective-permute-start = (bf16[1,4,2,1024]{3,2,1,0:T(2,128)(2,1)}, bf16[1,4,2,1024]{3,2,1,0:T(2,128)(2,1)S(1)}, u32[]{:S(2)}, u32[]{:S(2)}) collective-permute-start(bf16[1,4,2,1024]{3,2,1,0:T(2,128)(2,1)} %bitcast.5), channel_id=1, source_target_pairs={{0,4},{1,5},{2,6},{3,7},{4,0},{5,1},{6,2},{7,3},{8,12},{9,13},{10,... | collective-permute-start | bytes 49160 | tf_op jit(solution)/shard_map/ppermute | solution.py:18
  26.8 8.8 %collective-permute-start.14 = (bf16[2,576,128]{2,1,0:T(8,128)(2,1)S(1)}, bf16[2,576,128]{2,1,0:T(8,128)(2,1)S(1)}, u32[]{:S(2)}, u32[]{:S(2)}) collective-permute-start(bf16[2,576,128]{2,1,0:T(8,128)(2,1)S(1)} %pad_maximum_fusion.5), channel_id=1, source_target_pairs={{0,2},{1,3},{2,0},{3,1},{4,6},{5,7},{6,4},{7,5},{8,10},{9,11},{10,... | collective-permute-start | bytes 884744 | tf_op jit(solution)/shard_map/ppermute | solution.py:18
  30.4 12.5 %collective-permute-start.1 = (bf16[2,4,2,1024]{3,2,1,0:T(2,128)(2,1)S(1)}, bf16[2,4,2,1024]{3,2,1,0:T(2,128)(2,1)S(1)}, u32[]{:S(2)}, u32[]{:S(2)}) collective-permute-start(bf16[2,4,2,1024]{3,2,1,0:T(2,128)(2,1)S(1)} %pad_maximum_fusion.15), channel_id=1, source_target_pairs={{0,2},{1,3},{2,0},{3,1},{4,6},{5,7},{6,4},{7,5},{8,10},{9,11},{10,... | collective-permute-start | bytes 98312 | tf_op jit(solution)/shard_map/ppermute | solution.py:18
  32.6 9.7 %collective-permute-start.9 = (bf16[4,112,128]{2,1,0:T(8,128)(2,1)S(1)}, bf16[4,112,128]{2,1,0:T(8,128)(2,1)S(1)}, u32[]{:S(2)}, u32[]{:S(2)}) collective-permute-start(bf16[4,112,128]{2,1,0:T(8,128)(2,1)S(1)} %get-tuple-element.139), channel_id=1, source_target_pairs={{0,1},{1,0},{2,3},{3,2},{4,5},{5,4},{6,7},{7,6},{8,9},{9,8},{10,11... | collective-permute-start | bytes 344072 | tf_op jit(solution)/shard_map/ppermute | solution.py:18
  34.1 6.0 %collective-permute-start.5 = (bf16[4,112,128]{2,1,0:T(8,128)(2,1)S(1)}, bf16[4,112,128]{2,1,0:T(8,128)(2,1)S(1)}, u32[]{:S(2)}, u32[]{:S(2)}) collective-permute-start(bf16[4,112,128]{2,1,0:T(8,128)(2,1)S(1)} %get-tuple-element.140), channel_id=1, source_target_pairs={{0,16},{8,24},{16,0},{24,8},{1,17},{9,25},{17,1},{25,9},{2,18},{10... | collective-permute-start | bytes 344072 | tf_op jit(solution)/shard_map/ppermute | solution.py:18
  35.8 8.8 %collective-permute-start.19 = (bf16[4,288,128]{2,1,0:T(8,128)(2,1)S(1)}, bf16[4,288,128]{2,1,0:T(8,128)(2,1)S(1)}, u32[]{:S(2)}, u32[]{:S(2)}) collective-permute-start(bf16[4,288,128]{2,1,0:T(8,128)(2,1)S(1)} %get-tuple-element.131), channel_id=1, source_target_pairs={{0,1},{1,0},{2,3},{3,2},{4,5},{5,4},{6,7},{7,6},{8,9},{9,8},{10,11... | collective-permute-start | bytes 884744 | tf_op jit(solution)/shard_map/ppermute | solution.py:18
  40.2 10.3 %copy-start.9 = (bf16[8,112,128]{2,1,0:T(8,128)(2,1)}, bf16[8,112,128]{2,1,0:T(8,128)(2,1)S(1)}, u32[]{:S(2)}) copy-start(bf16[8,112,128]{2,1,0:T(8,128)(2,1)S(1)} %pad_maximum_fusion.9.refs_0_) | copy-start | bytes 688132
  40.2 6.5 %collective-permute-start.7 = (bf16[8,112,128]{2,1,0:T(8,128)(2,1)S(1)}, bf16[8,112,128]{2,1,0:T(8,128)(2,1)S(1)}, u32[]{:S(2)}, u32[]{:S(2)}) collective-permute-start(bf16[8,112,128]{2,1,0:T(8,128)(2,1)S(1)} %pad_maximum_fusion.9.refs_0_), channel_id=1, source_target_pairs={{0,1},{1,0},{2,3},{3,2},{4,5},{5,4},{6,7},{7,6},{8,9},{9,8},{10,11... | collective-permute-start | bytes 688136 | tf_op jit(solution)/shard_map/ppermute | solution.py:18
  40.8 9.2 %collective-permute-start.15 = (bf16[4,288,128]{2,1,0:T(8,128)(2,1)S(1)}, bf16[4,288,128]{2,1,0:T(8,128)(2,1)S(1)}, u32[]{:S(2)}, u32[]{:S(2)}) collective-permute-start(bf16[4,288,128]{2,1,0:T(8,128)(2,1)S(1)} %get-tuple-element.132), channel_id=1, source_target_pairs={{0,16},{8,24},{16,0},{24,8},{1,17},{9,25},{17,1},{25,9},{2,18},{10... | collective-permute-start | bytes 884744 | tf_op jit(solution)/shard_map/ppermute | solution.py:18
  42.3 7.7 %collective-permute-start.11 = (bf16[8,112,128]{2,1,0:T(8,128)(2,1)S(1)}, bf16[8,112,128]{2,1,0:T(8,128)(2,1)S(1)}, u32[]{:S(2)}, u32[]{:S(2)}) collective-permute-start(bf16[8,112,128]{2,1,0:T(8,128)(2,1)S(1)} %pad_maximum_fusion.10.refs_4_), channel_id=1, source_target_pairs={{0,16},{8,24},{16,0},{24,8},{1,17},{9,25},{17,1},{25,9},{2,18},{10... | collective-permute-start | bytes 688136 | tf_op jit(solution)/shard_map/ppermute | solution.py:18
  43.0 7.6 %collective-permute-start.2 = (bf16[4,4,2,1024]{3,2,1,0:T(2,128)(2,1)S(1)}, bf16[4,4,2,1024]{3,2,1,0:T(2,128)(2,1)S(1)}, u32[]{:S(2)}, u32[]{:S(2)}) collective-permute-start(bf16[4,4,2,1024]{3,2,1,0:T(2,128)(2,1)S(1)} %pad_maximum_fusion.14), channel_id=1, source_target_pairs={{0,1},{1,0},{2,3},{3,2},{4,5},{5,4},{6,7},{7,6},{8,9},{9,8},{10,11... | collective-permute-start | bytes 196616 | tf_op jit(solution)/shard_map/ppermute | solution.py:18
  44.6 7.6 %collective-permute-start.6 = (bf16[8,112,128]{2,1,0:T(8,128)(2,1)S(1)}, bf16[8,112,128]{2,1,0:T(8,128)(2,1)S(1)}, u32[]{:S(2)}, u32[]{:S(2)}) collective-permute-start(bf16[8,112,128]{2,1,0:T(8,128)(2,1)S(1)} %pad_maximum_fusion.9.refs_0_), channel_id=1, source_target_pairs={{0,8},{8,0},{16,24},{24,16},{1,9},{9,1},{17,25},{25,17},{2,10},{10... | collective-permute-start | bytes 688136 | tf_op jit(solution)/shard_map/ppermute | solution.py:18
  44.7 18.1 %copy-start.6 = (bf16[8,288,128]{2,1,0:T(8,128)(2,1)}, bf16[8,288,128]{2,1,0:T(8,128)(2,1)S(1)}, u32[]{:S(2)}) copy-start(bf16[8,288,128]{2,1,0:T(8,128)(2,1)S(1)} %pad_maximum_fusion.4.rest_4_) | copy-start | bytes 1769476
  46.7 7.8 %collective-permute-start.10 = (bf16[8,112,128]{2,1,0:T(8,128)(2,1)S(1)}, bf16[8,112,128]{2,1,0:T(8,128)(2,1)S(1)}, u32[]{:S(2)}, u32[]{:S(2)}) collective-permute-start(bf16[8,112,128]{2,1,0:T(8,128)(2,1)S(1)} %pad_maximum_fusion.10.refs_4_), channel_id=1, source_target_pairs={{0,8},{8,0},{16,24},{24,16},{1,9},{9,1},{17,25},{25,17},{2,10},{10... | collective-permute-start | bytes 688136 | tf_op jit(solution)/shard_map/ppermute | solution.py:18
  49.9 4.5 %collective-permute-start.8 = (bf16[8,112,128]{2,1,0:T(8,128)(2,1)S(1)}, bf16[8,112,128]{2,1,0:T(8,128)(2,1)S(1)}, u32[]{:S(2)}, u32[]{:S(2)}) collective-permute-start(bf16[8,112,128]{2,1,0:T(8,128)(2,1)S(1)} %collective-permute-done.7.refs_2_), channel_id=1, source_target_pairs={{0,8},{8,0},{16,24},{24,16},{1,9},{9,1},{17,25},{25,17},{2,10},{10... | collective-permute-start | bytes 688136 | tf_op jit(solution)/shard_map/ppermute | solution.py:18
  50.0 5.9 %collective-permute-start.12 = (bf16[8,112,128]{2,1,0:T(8,128)(2,1)S(1)}, bf16[8,112,128]{2,1,0:T(8,128)(2,1)}, u32[]{:S(2)}, u32[]{:S(2)}) collective-permute-start(bf16[8,112,128]{2,1,0:T(8,128)(2,1)S(1)} %collective-permute-done.11.refs_6_), channel_id=1, source_target_pairs={{0,8},{8,0},{16,24},{24,16},{1,9},{9,1},{17,25},{25,17},{2,10},{10... | collective-permute-start | bytes 688136 | tf_op jit(solution)/shard_map/ppermute | solution.py:18
  50.5 12.1 %copy-start.7 = (bf16[8,288,128]{2,1,0:T(8,128)(2,1)}, bf16[8,288,128]{2,1,0:T(8,128)(2,1)S(1)}, u32[]{:S(2)}) copy-start(bf16[8,288,128]{2,1,0:T(8,128)(2,1)S(1)} %pad_maximum_fusion.3.rest_0_) | copy-start | bytes 1769476
  50.6 15.4 %collective-permute-start.17 = (bf16[8,288,128]{2,1,0:T(8,128)(2,1)S(1)}, bf16[8,288,128]{2,1,0:T(8,128)(2,1)S(1)}, u32[]{:S(2)}, u32[]{:S(2)}) collective-permute-start(bf16[8,288,128]{2,1,0:T(8,128)(2,1)S(1)} %pad_maximum_fusion.3.rest_0_), channel_id=1, source_target_pairs={{0,1},{1,0},{2,3},{3,2},{4,5},{5,4},{6,7},{7,6},{8,9},{9,8},{10,11... | collective-permute-start | bytes 1769480 | tf_op jit(solution)/shard_map/ppermute | solution.py:18
  52.2 15.0 %collective-permute-start.21 = (bf16[8,288,128]{2,1,0:T(8,128)(2,1)S(1)}, bf16[8,288,128]{2,1,0:T(8,128)(2,1)S(1)}, u32[]{:S(2)}, u32[]{:S(2)}) collective-permute-start(bf16[8,288,128]{2,1,0:T(8,128)(2,1)S(1)} %pad_maximum_fusion.4.rest_4_), channel_id=1, source_target_pairs={{0,16},{8,24},{16,0},{24,8},{1,17},{9,25},{17,1},{25,9},{2,18},{10... | collective-permute-start | bytes 1769480 | tf_op jit(solution)/shard_map/ppermute | solution.py:18
  62.6 12.3 %collective-permute-start.16 = (bf16[8,288,128]{2,1,0:T(8,128)(2,1)S(1)}, bf16[8,288,128]{2,1,0:T(8,128)(2,1)S(1)}, u32[]{:S(2)}, u32[]{:S(2)}) collective-permute-start(bf16[8,288,128]{2,1,0:T(8,128)(2,1)S(1)} %pad_maximum_fusion.3.rest_0_), channel_id=1, source_target_pairs={{0,8},{8,0},{16,24},{24,16},{1,9},{9,1},{17,25},{25,17},{2,10},{10... | collective-permute-start | bytes 1769480 | tf_op jit(solution)/shard_map/ppermute | solution.py:18
  62.7 12.2 %collective-permute-start.20 = (bf16[8,288,128]{2,1,0:T(8,128)(2,1)S(1)}, bf16[8,288,128]{2,1,0:T(8,128)(2,1)}, u32[]{:S(2)}, u32[]{:S(2)}) collective-permute-start(bf16[8,288,128]{2,1,0:T(8,128)(2,1)S(1)} %pad_maximum_fusion.4.rest_4_), channel_id=1, source_target_pairs={{0,8},{8,0},{16,24},{24,16},{1,9},{9,1},{17,25},{25,17},{2,10},{10... | collective-permute-start | bytes 1769480 | tf_op jit(solution)/shard_map/ppermute | solution.py:18
  65.9 9.0 %collective-permute-start.18 = (bf16[8,288,128]{2,1,0:T(8,128)(2,1)S(1)}, bf16[8,288,128]{2,1,0:T(8,128)(2,1)}, u32[]{:S(2)}, u32[]{:S(2)}) collective-permute-start(bf16[8,288,128]{2,1,0:T(8,128)(2,1)S(1)} %collective-permute-done.17.rest_2_), channel_id=1, source_target_pairs={{0,8},{8,0},{16,24},{24,16},{1,9},{9,1},{17,25},{25,17},{2,10},{10... | collective-permute-start | bytes 1769480 | tf_op jit(solution)/shard_map/ppermute | solution.py:18
  67.2 7.8 %collective-permute-start.22 = (bf16[8,288,128]{2,1,0:T(8,128)(2,1)S(1)}, bf16[8,288,128]{2,1,0:T(8,128)(2,1)}, u32[]{:S(2)}, u32[]{:S(2)}) collective-permute-start(bf16[8,288,128]{2,1,0:T(8,128)(2,1)S(1)} %collective-permute-done.21.rest_6_), channel_id=1, source_target_pairs={{0,8},{8,0},{16,24},{24,16},{1,9},{9,1},{17,25},{25,17},{2,10},{10... | collective-permute-start | bytes 1769480 | tf_op jit(solution)/shard_map/ppermute | solution.py:18
  111.2 7.5 %collective-permute-start.23 = (bf16[16,304,128]{2,1,0:T(8,128)(2,1)}, bf16[16,304,128]{2,1,0:T(8,128)(2,1)S(1)}, u32[]{:S(2)}, u32[]{:S(2)}) collective-permute-start(bf16[16,304,128]{2,1,0:T(8,128)(2,1)} %get-tuple-element.79), channel_id=1, source_target_pairs={{0,8},{8,0},{16,24},{24,16},{1,9},{9,1},{17,25},{25,17},{2,10},{10... | collective-permute-start | bytes 3735560 | tf_op jit(solution)/shard_map/ppermute | solution.py:18
  111.5 10.9 %collective-permute-start.24 = (bf16[16,304,128]{2,1,0:T(8,128)(2,1)}, bf16[16,304,128]{2,1,0:T(8,128)(2,1)}, u32[]{:S(2)}, u32[]{:S(2)}) collective-permute-start(bf16[16,304,128]{2,1,0:T(8,128)(2,1)} %get-tuple-element.81), channel_id=1, source_target_pairs={{0,8},{8,0},{16,24},{24,16},{1,9},{9,1},{17,25},{25,17},{2,10},{10... | collective-permute-start | bytes 3735560 | tf_op jit(solution)/shard_map/ppermute | solution.py:18
  133.8 16.4 %copy-start.5 = (bf16[8,304,128]{2,1,0:T(8,128)(2,1)S(1)}, bf16[8,304,128]{2,1,0:T(8,128)(2,1)}, u32[]{:S(2)}) copy-start(bf16[8,304,128]{2,1,0:T(8,128)(2,1)} %get-tuple-element.121.rest_5_) | copy-start | bytes 1867780
  144.4 12.3 %copy-start.8 = (bf16[16,112,128]{2,1,0:T(8,128)(2,1)S(1)}, bf16[16,112,128]{2,1,0:T(8,128)(2,1)}, u32[]{:S(2)}) copy-start(bf16[16,112,128]{2,1,0:T(8,128)(2,1)} %get-tuple-element.94) | copy-start | bytes 1376260
  145.2 4.0 %collective-permute-start.25 = (bf16[4,4,2,512]{3,2,1,0:T(2,128)(2,1)S(1)}, bf16[4,4,2,512]{3,2,1,0:T(2,128)(2,1)S(1)}, u32[]{:S(2)}, u32[]{:S(2)}) collective-permute-start(bf16[4,4,2,512]{3,2,1,0:T(2,128)(2,1)S(1)} %slice.175), channel_id=1, source_target_pairs={{0,1},{1,0},{2,3},{3,2},{4,5},{5,4},{6,7},{7,6},{8,9},{9,8},{10,11... | collective-permute-start | bytes 98312 | tf_op jit(solution)/shard_map/ppermute | solution.py:18
  145.9 8.1 %collective-permute-start.28 = (bf16[16,112,128]{2,1,0:T(8,128)(2,1)}, bf16[16,112,128]{2,1,0:T(8,128)(2,1)S(1)}, u32[]{:S(2)}, u32[]{:S(2)}) collective-permute-start(bf16[16,112,128]{2,1,0:T(8,128)(2,1)} %get-tuple-element.93), channel_id=1, source_target_pairs={{0,8},{8,0},{16,24},{24,16},{1,9},{9,1},{17,25},{25,17},{2,10},{10... | collective-permute-start | bytes 1376264 | tf_op jit(solution)/shard_map/ppermute | solution.py:18
  150.0 3.8 %collective-permute-start.26 = (bf16[2,4,2,512]{3,2,1,0:T(2,128)(2,1)S(1)}, bf16[2,4,2,512]{3,2,1,0:T(2,128)(2,1)S(1)}, u32[]{:S(2)}, u32[]{:S(2)}) collective-permute-start(bf16[2,4,2,512]{3,2,1,0:T(2,128)(2,1)S(1)} %slice.221), channel_id=1, source_target_pairs={{0,2},{1,3},{2,0},{3,1},{4,6},{5,7},{6,4},{7,5},{8,10},{9,11},{10,... | collective-permute-start | bytes 49160 | tf_op jit(solution)/shard_map/ppermute | solution.py:18
  150.1 17.0 %collective-permute-start.36 = (bf16[8,304,128]{2,1,0:T(8,128)(2,1)S(1)}, bf16[8,304,128]{2,1,0:T(8,128)(2,1)S(1)}, u32[]{:S(2)}, u32[]{:S(2)}) collective-permute-start(bf16[8,304,128]{2,1,0:T(8,128)(2,1)S(1)} %copy-done.5), channel_id=1, source_target_pairs={{0,16},{8,24},{16,0},{24,8},{1,17},{9,25},{17,1},{25,9},{2,18},{10... | collective-permute-start | bytes 1867784 | tf_op jit(solution)/shard_map/ppermute | solution.py:18
  151.7 17.1 %collective-permute-start.38 = (bf16[8,304,128]{2,1,0:T(8,128)(2,1)}, bf16[8,304,128]{2,1,0:T(8,128)(2,1)S(1)}, u32[]{:S(2)}, u32[]{:S(2)}) collective-permute-start(bf16[8,304,128]{2,1,0:T(8,128)(2,1)} %get-tuple-element.119.rest_7_), channel_id=1, source_target_pairs={{0,1},{1,0},{2,3},{3,2},{4,5},{5,4},{6,7},{7,6},{8,9},{9,8},{10,11... | collective-permute-start | bytes 1867784 | tf_op jit(solution)/shard_map/ppermute | solution.py:18
  152.3 4.5 %collective-permute-start.31 = (bf16[16,112,128]{2,1,0:T(8,128)(2,1)}, bf16[16,112,128]{2,1,0:T(8,128)(2,1)S(1)}, u32[]{:S(2)}, u32[]{:S(2)}) collective-permute-start(bf16[16,112,128]{2,1,0:T(8,128)(2,1)} %get-tuple-element.95), channel_id=1, source_target_pairs={{0,8},{8,0},{16,24},{24,16},{1,9},{9,1},{17,25},{25,17},{2,10},{10... | collective-permute-start | bytes 1376264 | tf_op jit(solution)/shard_map/ppermute | solution.py:18
  153.9 21.1 %collective-permute-start.27 = (bf16[1,4,2,512]{3,2,1,0:T(2,128)(2,1)S(1)}, bf16[1,4,2,512]{3,2,1,0:T(2,128)(2,1)S(1)}, u32[]{:S(2)}, u32[]{:S(2)}) collective-permute-start(bf16[1,4,2,512]{3,2,1,0:T(2,128)(2,1)S(1)} %slice.223), channel_id=1, source_target_pairs={{0,4},{1,5},{2,6},{3,7},{4,0},{5,1},{6,2},{7,3},{8,12},{9,13},{10,... | collective-permute-start | bytes 24584 | tf_op jit(solution)/shard_map/ppermute | solution.py:18
  155.1 16.9 %collective-permute-start.29 = (bf16[8,112,128]{2,1,0:T(8,128)(2,1)S(1)}, bf16[8,112,128]{2,1,0:T(8,128)(2,1)S(1)}, u32[]{:S(2)}, u32[]{:S(2)}) collective-permute-start(bf16[8,112,128]{2,1,0:T(8,128)(2,1)S(1)} %slice.225), channel_id=1, source_target_pairs={{0,16},{8,24},{16,0},{24,8},{1,17},{9,25},{17,1},{25,9},{2,18},{10... | collective-permute-start | bytes 688136 | tf_op jit(solution)/shard_map/ppermute | solution.py:18
  156.9 16.8 %collective-permute-start.32 = (bf16[8,112,128]{2,1,0:T(8,128)(2,1)S(1)}, bf16[8,112,128]{2,1,0:T(8,128)(2,1)S(1)}, u32[]{:S(2)}, u32[]{:S(2)}) collective-permute-start(bf16[8,112,128]{2,1,0:T(8,128)(2,1)S(1)} %pad_maximum_fusion.6), channel_id=1, source_target_pairs={{0,1},{1,0},{2,3},{3,2},{4,5},{5,4},{6,7},{7,6},{8,9},{9,8},{10,11... | collective-permute-start | bytes 688136 | tf_op jit(solution)/shard_map/ppermute | solution.py:18
  168.0 16.9 %collective-permute-start.37 = (bf16[4,304,128]{2,1,0:T(8,128)(2,1)S(1)}, bf16[4,304,128]{2,1,0:T(8,128)(2,1)S(1)}, u32[]{:S(2)}, u32[]{:S(2)}) collective-permute-start(bf16[4,304,128]{2,1,0:T(8,128)(2,1)S(1)} %get-tuple-element.129), channel_id=1, source_target_pairs={{0,1},{1,0},{2,3},{3,2},{4,5},{5,4},{6,7},{7,6},{8,9},{9,8},{10,11... | collective-permute-start | bytes 933896 | tf_op jit(solution)/shard_map/ppermute | solution.py:18
  169.8 15.1 %collective-permute-start.39 = (bf16[4,304,128]{2,1,0:T(8,128)(2,1)S(1)}, bf16[4,304,128]{2,1,0:T(8,128)(2,1)S(1)}, u32[]{:S(2)}, u32[]{:S(2)}) collective-permute-start(bf16[4,304,128]{2,1,0:T(8,128)(2,1)S(1)} %get-tuple-element.127), channel_id=1, source_target_pairs={{0,16},{8,24},{16,0},{24,8},{1,17},{9,25},{17,1},{25,9},{2,18},{10... | collective-permute-start | bytes 933896 | tf_op jit(solution)/shard_map/ppermute | solution.py:18
  172.7 8.0 %collective-permute-start.30 = (bf16[4,112,128]{2,1,0:T(8,128)(2,1)S(1)}, bf16[4,112,128]{2,1,0:T(8,128)(2,1)S(1)}, u32[]{:S(2)}, u32[]{:S(2)}) collective-permute-start(bf16[4,112,128]{2,1,0:T(8,128)(2,1)S(1)} %get-tuple-element.137), channel_id=1, source_target_pairs={{0,1},{1,0},{2,3},{3,2},{4,5},{5,4},{6,7},{7,6},{8,9},{9,8},{10,11... | collective-permute-start | bytes 344072 | tf_op jit(solution)/shard_map/ppermute | solution.py:18
  174.5 6.3 %collective-permute-start.33 = (bf16[4,112,128]{2,1,0:T(8,128)(2,1)S(1)}, bf16[4,112,128]{2,1,0:T(8,128)(2,1)S(1)}, u32[]{:S(2)}, u32[]{:S(2)}) collective-permute-start(bf16[4,112,128]{2,1,0:T(8,128)(2,1)S(1)} %get-tuple-element.135), channel_id=1, source_target_pairs={{0,16},{8,24},{16,0},{24,8},{1,17},{9,25},{17,1},{25,9},{2,18},{10... | collective-permute-start | bytes 344072 | tf_op jit(solution)/shard_map/ppermute | solution.py:18
  183.2 10.1 %collective-permute-start.34 = (bf16[2,224,128]{2,1,0:T(8,128)(2,1)}, bf16[2,224,128]{2,1,0:T(8,128)(2,1)S(1)}, u32[]{:S(2)}, u32[]{:S(2)}) collective-permute-start(bf16[2,224,128]{2,1,0:T(8,128)(2,1)} %get-tuple-element.97), channel_id=1, source_target_pairs={{0,2},{1,3},{2,0},{3,1},{4,6},{5,7},{6,4},{7,5},{8,10},{9,11},{10,... | collective-permute-start | bytes 344072 | tf_op jit(solution)/shard_map/ppermute | solution.py:18
  187.9 8.6 %collective-permute-start.40 = (bf16[2,608,128]{2,1,0:T(8,128)(2,1)}, bf16[2,608,128]{2,1,0:T(8,128)(2,1)S(1)}, u32[]{:S(2)}, u32[]{:S(2)}) collective-permute-start(bf16[2,608,128]{2,1,0:T(8,128)(2,1)} %get-tuple-element.104), channel_id=1, source_target_pairs={{0,2},{1,3},{2,0},{3,1},{4,6},{5,7},{6,4},{7,5},{8,10},{9,11},{10,... | collective-permute-start | bytes 933896 | tf_op jit(solution)/shard_map/ppermute | solution.py:18
  195.6 8.2 %collective-permute-start.35 = (bf16[1,224,128]{2,1,0:T(8,128)(2,1)}, bf16[1,224,128]{2,1,0:T(8,128)(2,1)S(1)}, u32[]{:S(2)}, u32[]{:S(2)}) collective-permute-start(bf16[1,224,128]{2,1,0:T(8,128)(2,1)} %get-tuple-element.99), channel_id=1, source_target_pairs={{0,4},{1,5},{2,6},{3,7},{4,0},{5,1},{6,2},{7,3},{8,12},{9,13},{10,... | collective-permute-start | bytes 172040 | tf_op jit(solution)/shard_map/ppermute | solution.py:18
  199.1 8.5 %collective-permute-start.41 = (bf16[1,608,128]{2,1,0:T(8,128)(2,1)}, bf16[1,608,128]{2,1,0:T(8,128)(2,1)S(1)}, u32[]{:S(2)}, u32[]{:S(2)}) collective-permute-start(bf16[1,608,128]{2,1,0:T(8,128)(2,1)} %get-tuple-element.106), channel_id=1, source_target_pairs={{0,4},{1,5},{2,6},{3,7},{4,0},{5,1},{6,2},{7,3},{8,12},{9,13},{10,... | collective-permute-start | bytes 466952 | tf_op jit(solution)/shard_map/ppermute | solution.py:18
  (22 other events, 77.7 us)

commit v4 on v3

--- a/solution.py
+++ b/solution.py
@@ -63,7 +63,8 @@
         far_ids = full[len(ids) :]
         for piece, names in ((part, ids), (far, far_ids)):
             pieces.append((piece, names, first))
-            pieces.append((swap(piece, *CORE), [(s, b ^ 1) for s, b in names], first))
+            theirs = swap(piece, *CORE)
+            pieces.append((theirs, [(s, b ^ 1) for s, b in names], first))
     return pieces
 
 
@@ -122,26 +123,6 @@
                     ].astype(BF16)
 
 
-def add_low(mine, theirs):
-    return (mine.astype(F32) + theirs.astype(F32)).astype(BF16)
-
-
-def join_pair(array):
-    count = VEC_ROWS // 2
-    return array[..., -VEC_ROWS:-count, :].astype(F32) + array[..., -count:, :].astype(F32)
-
-
-def split_pair(total):
-    high = lax.reduce_precision(total, 8, 7)
-    return [high.astype(BF16), (total - high).astype(BF16)]
-
-
-def add_pairs(mine, theirs):
-    total = join_pair(mine) + join_pair(theirs)
-    low = add_low(mine[..., :-VEC_ROWS, :], theirs[..., :-VEC_ROWS, :])
-    return jnp.concatenate([low] + split_pair(total), -2)
-
-
 ORDERS = ((CORE, X_STAGE, Y_STAGE), (CORE, Y_STAGE, X_STAGE))
 
 
@@ -152,9 +133,7 @@
         if last:
             done.append((kept, theirs))
             continue
-        state = (add_pairs if k == 1 else add_low)(kept, theirs)
-        count = state.shape[0] // 2
-        done.append((state[:count], state[count:]))
+        done.append(tuple(joined_sum([(kept, theirs, k == 1)])))
     return done
 
 
@@ -282,7 +261,8 @@
 def gather_seq(array):
     state = array[None]
     for stage in seq_stages():
-        state = jnp.concatenate([state, swap(state, *stage)], 0)
+        theirs = swap(state, *stage)
+        state = jnp.concatenate([state, theirs], 0)
     return state
 
 

time: 211 us -> 212 us (level)
  Pallas kernels: 96.9 us -> 115 us
  waiting for transfers between devices: 48.4 us -> 36.4 us
  other arithmetic: 12.4 us -> 6.34 us
    pallas_call x2 -> x10, Pallas kernels: 3.95 us -> 21.6 us  [joined_sum(): pl.pallas_call(kernel, cost_estimate=cost(2), out_shape=[jax.ShapeDtypeSt...]
    ppermute x42, waiting for transfers between devices: 48.4 us -> 36.4 us  [swap(): return lax.ppermute(array, axis, [(i, i ^ bit) for i in range(count)])]
    convert_element_type x12 -> x0, other arithmetic: 5.88 us -> none  [the longest x8 4.83 us: add_low(): return (mine.astype(F32) + theirs.astype(F32)).astype(BF16)]
    slice x7 -> x0, local copies, waits for them, and re-layouts: 5.1 us -> none  [reduce_step(): done.append((state[:count], state[count:]))]
    unnamed x56 -> x66, local copies, waits for them, and re-layouts: 8.01 us -> 13 us
  transfers between devices with their start and end apart: 42 -> 42, of which waited for: 18 -> 16; matrix products, arithmetic and copies ran while one was open for 5% -> 2% of each run, Pallas kernels for 19% -> 25%
where the time goes in v4:
time: 212 us; the launch traced here: 211 us
  Pallas kernels  115 us (54%)
  starting transfers between devices  38.6 us (18%)
  waiting for transfers between devices  36.4 us (17%)
  local copies, waits for them, and re-layouts  13.9 us (7%)
  other arithmetic  6.34 us (3%)
    ppermute x42, starting transfers between devices, swap(): return lax.ppermute(array, axis, [(i, i ^ bit) for i in range(count)])  38.6 us
    ppermute x42, waiting for transfers between devices, swap(): return lax.ppermute(array, axis, [(i, i ^ bit) for i in range(count)])  36.4 us
    pallas_call x1, Pallas kernels, feed(): pl.pallas_call(kernel, cost_estimate=cost(35), grid=(count,), in_specs=[p...  35.4 us
    pallas_call x10, Pallas kernels, joined_sum(): pl.pallas_call(kernel, cost_estimate=cost(2), out_shape=[jax.ShapeDtypeSt...  21.6 us
    pallas_call x2, Pallas kernels, attend_back(): pl.pallas_call(kernel, cost_estimate=cost(7), grid=(number,), in_specs=[p...  13.8 us
    unnamed x66, local copies, waits for them, and re-layouts  13 us
    pallas_call x1, Pallas kernels, project_back(): pl.pallas_call(kernel, cost_estimate=cost(10), grid=(count,), in_specs=[p...  10.6 us
    pallas_call x1, Pallas kernels, attend(): pl.pallas_call(kernel, cost_estimate=cost(8), grid=(count,), in_specs=[pl...  7.73 us
  transfers between devices with their start and end apart: 42, of which 16 were waited for; matrix products, arithmetic and copies ran while one was open for 2% of the time, Pallas kernels for 25%

profile of v4, /device:TPU:0, one launch (start us, length us, event | category | flops | bytes accessed | tf_op | source)
XLA Modules:
  0.0 210.8 jit_solution(13675247230936078758)
XLA Ops:
  1.3 1.5 shard_map.263
  2.8 4.1 %collective-permute-start.3 = (bf16[1,224,128]{2,1,0:T(8,128)(2,1)}, bf16[1,224,128]{2,1,0:T(8,128)(2,1)S(1)}, u32[]{:S(2)}, u32[]{:S(2)}) collective-permute-start(bf16[1,224,128]{2,1,0:T(8,128)(2,1)} %shard_map.263), channel_id=1, source_target_pairs={{0,4},{1,5},{2,6},{3,7},{4,0},{5,1},{6,2},{7,3},{8,12},{9,13},{10,... | collective-permute-start | bytes 172040 | tf_op jit(solution)/shard_map/ppermute | solution.py:18
  6.8 3.0 %collective-permute-done.3 = bf16[1,224,128]{2,1,0:T(8,128)(2,1)S(1)} collective-permute-done((bf16[1,224,128]{2,1,0:T(8,128)(2,1)}, bf16[1,224,128]{2,1,0:T(8,128)(2,1)S(1)}, u32[]{:S(2)}, u32[]{:S(2)}) %collective-permute-start.3) | collective-permute-done | bytes 57376 | tf_op jit(solution)/shard_map/ppermute | solution.py:18
  12.0 3.5 %collective-permute-done.4 = bf16[2,224,128]{2,1,0:T(8,128)(2,1)S(1)} collective-permute-done((bf16[2,224,128]{2,1,0:T(8,128)(2,1)S(1)}, bf16[2,224,128]{2,1,0:T(8,128)(2,1)S(1)}, u32[]{:S(2)}, u32[]{:S(2)}) %collective-permute-start.4) | collective-permute-done | bytes 114720 | tf_op jit(solution)/shard_map/ppermute | solution.py:18
  15.5 1.5 pad_maximum_fusion.4.refs_3_
  17.0 1.6 shard_map.266
  18.6 2.5 %collective-permute-start.13 = (bf16[1,576,128]{2,1,0:T(8,128)(2,1)}, bf16[1,576,128]{2,1,0:T(8,128)(2,1)S(1)}, u32[]{:S(2)}, u32[]{:S(2)}) collective-permute-start(bf16[1,576,128]{2,1,0:T(8,128)(2,1)} %shard_map.266), channel_id=1, source_target_pairs={{0,4},{1,5},{2,6},{3,7},{4,0},{5,1},{6,2},{7,3},{8,12},{9,13},{10,... | collective-permute-start | bytes 442376 | tf_op jit(solution)/shard_map/ppermute | solution.py:18
  21.1 3.6 %shard_map.262 = bf16[4,2,1024]{2,1,0:T(2,128)(2,1)} custom-call(bf16[4,256,512]{2,1,0:T(8,128)(2,1)} %x_ref.9), custom_call_target="tpu_custom_call" | custom-call | flops 3000000000 | bytes 1048576 | tf_op jit(solution)/shard_map/pallas_call | solution.py:420
  25.2 1.6 collective-permute-done.13
  27.6 2.0 collective-permute-done
  30.3 2.2 %collective-permute-start.1 = (bf16[2,4,2,1024]{3,2,1,0:T(2,128)(2,1)S(1)}, bf16[2,4,2,1024]{3,2,1,0:T(2,128)(2,1)S(1)}, u32[]{:S(2)}, u32[]{:S(2)}) collective-permute-start(bf16[2,4,2,1024]{3,2,1,0:T(2,128)(2,1)S(1)} %pad_maximum_fusion.10), channel_id=1, source_target_pairs={{0,2},{1,3},{2,0},{3,1},{4,6},{5,7},{6,4},{7,5},{8,10},{9,11},{10,... | collective-permute-start | bytes 98312 | tf_op jit(solution)/shard_map/ppermute | solution.py:18
  32.5 1.6 collective-permute-start.9
  34.1 1.5 collective-permute-start.5
  36.3 3.8 %collective-permute-done.5 = bf16[4,112,128]{2,1,0:T(8,128)(2,1)S(1)} collective-permute-done((bf16[4,112,128]{2,1,0:T(8,128)(2,1)S(1)}, bf16[4,112,128]{2,1,0:T(8,128)(2,1)S(1)}, u32[]{:S(2)}, u32[]{:S(2)}) %collective-permute-start.5) | collective-permute-done | bytes 114720 | tf_op jit(solution)/shard_map/ppermute | solution.py:18
  40.7 1.5 collective-permute-start.15
  43.0 1.6 collective-permute-start.2
  44.6 2.0 collective-permute-done.7.refs_2_
  46.7 3.3 %collective-permute-done.11.refs_6_ = bf16[8,112,128]{2,1,0:T(8,128)(2,1)S(1)} collective-permute-done((bf16[8,112,128]{2,1,0:T(8,128)(2,1)S(1)}, bf16[8,112,128]{2,1,0:T(8,128)(2,1)S(1)}, u32[]{:S(2)}, u32[]{:S(2)}) %collective-permute-start.11) | collective-permute-done | bytes 229408 | tf_op jit(solution)/shard_map/ppermute | solution.py:18
  50.5 1.6 collective-permute-start.17
  52.1 1.5 collective-permute-start.21
  55.9 6.7 %shard_map.264 = (bf16[4,256,1536]{2,1,0:T(8,128)(2,1)}, bf16[4,16,1024]{2,1,0:T(8,128)(2,1)}, bf16[512,512]{1,0:T(8,128)(2,1)}, bf16[512,512]{1,0:T(8,128)(2,1)...) custom-call(s32[2]{0:T(128)} %pad_add_fusion.spot, bf16[4,256,512]{2,1,0:T(8,128)(2,1)} %x_ref.9, ...), custom_call_target="tpu_custom_call" | custom-call | flops 6000000000 | bytes 1048576 | tf_op jit(solution)/shard_map/pallas_call | solution.py:491
  63.2 2.7 %collective-permute-done.17.rest_2_ = bf16[8,288,128]{2,1,0:T(8,128)(2,1)S(1)} collective-permute-done((bf16[8,288,128]{2,1,0:T(8,128)(2,1)S(1)}, bf16[8,288,128]{2,1,0:T(8,128)(2,1)S(1)}, u32[]{:S(2)}, u32[]{:S(2)}) %collective-permute-start.17) | collective-permute-done | bytes 589856 | tf_op jit(solution)/shard_map/ppermute | solution.py:18
  67.2 7.7 %shard_map.265 = (bf16[4,256,512]{2,1,0:T(8,128)(2,1)}, f32[4,8,256]{2,1,0:T(8,128)}) custom-call(s32[2]{0:T(128)} %pad_add_fusion.spot, bf16[4,256,1536]{2,1,0:T(8,128)(2,1)} %get-tuple-element.82.qkv_ref, bf16[4,16,1024]{2,1,0:T(8,128)(2,1)} %get-tuple-element.83.sum_ref), custom_call_target="tpu_custom_call" | custom-call | flops 8000000000 | bytes 1048576 | tf_op jit(solution)/shard_map/pallas_call | solution.py:570
  75.7 35.4 %shard_map.267 = (bf16[4,256,512]{2,1,0:T(8,128)(2,1)}, f32[4,256,512]{2,1,0:T(8,128)}, bf16[4,256,512]{2,1,0:T(8,128)(2,1)}, f32[8,512]{1,0:T(8,128)}, f32[8,20...) custom-call(s32[2]{0:T(128)} %pad_add_fusion.spot, ...), custom_call_target="tpu_custom_call" | custom-call | flops 35000000512 | bytes 1048576 | tf_op jit(solution)/shard_map/pallas_call | solution.py:712
  111.7 6.8 %shard_map.268 = (bf16[4,256,512]{2,1,0:T(8,128)(2,1)}, bf16[4,256,512]{2,1,0:T(8,128)(2,1)}, bf16[4,256,512]{2,1,0:T(8,128)(2,1)}, bf16[4,16,1024]{2,1,0:T(8,128)(2,1)}) custom-call(s32[2]{0:T(128)} %pad_add_fusion.spot, bf16[4,256,1536]{2,1,0:T(8,128)(2,1)} %get-tuple-element.82.qkv_ref, bf16[4,16,1024]{2,1,0:T(8,128)(2,1)} %get-tuple-element.83.sum_ref, ...), custom_call_target="tpu_custom_call" | custom-call | flops 7000000000 | bytes 1048576 | tf_op jit(solution)/shard_map/pallas_call | solution.py:777
  119.5 2.9 %shard_map.269 = (bf16[8,304,128]{2,1,0:T(8,128)(2,1)}, bf16[8,304,128]{2,1,0:T(8,128)(2,1)}) custom-call(bf16[16,304,128]{2,1,0:T(8,128)(2,1)} %get-tuple-element.94.refs_0_, bf16[16,304,128]{2,1,0:T(8,128)(2,1)} %copy-done.8), custom_call_target="tpu_custom_call" | custom-call | flops 2000000000 | bytes 1048576 | tf_op jit(solution)/shard_map/pallas_call | solution.py:170
  123.4 2.9 %shard_map.270 = (bf16[8,304,128]{2,1,0:T(8,128)(2,1)}, bf16[8,304,128]{2,1,0:T(8,128)(2,1)}) custom-call(bf16[16,304,128]{2,1,0:T(8,128)(2,1)} %get-tuple-element.98.refs_0_, bf16[16,304,128]{2,1,0:T(8,128)(2,1)} %copy-done.7), custom_call_target="tpu_custom_call" | custom-call | flops 2000000000 | bytes 1048576 | tf_op jit(solution)/shard_map/pallas_call | solution.py:170
  126.4 7.0 %shard_map.271 = (bf16[4,256,512]{2,1,0:T(8,128)(2,1)}, bf16[4,256,512]{2,1,0:T(8,128)(2,1)}, bf16[4,256,512]{2,1,0:T(8,128)(2,1)}, bf16[4,16,1024]{2,1,0:T(8,128)(2,1)}) custom-call(s32[2]{0:T(128)} %pad_add_fusion.spot, bf16[4,256,1536]{2,1,0:T(8,128)(2,1)} %get-tuple-element.82.qkv_ref, ...), custom_call_target="tpu_custom_call", output_to_operand_aliasing={{0}: (5, {}), {1}: (6, {}), {2}: (7, {}), {3}: (8, {})} | custom-call | flops 7000000000 | bytes 1048576 | tf_op jit(solution)/shard_map/pallas_call | solution.py:777
  133.4 10.6 %shard_map.272 = (f32[4,256,512]{2,1,0:T(8,128)}, bf16[8,4,2,512]{3,2,1,0:T(2,128)(2,1)}, f32[8,512]{1,0:T(8,128)}, bf16[16,112,128]{2,1,0:T(8,128)(2,1)}, bf16[...) custom-call(s32[2]{0:T(128)} %pad_add_fusion.spot, ...), custom_call_target="tpu_custom_call" | custom-call | flops 10000000000 | bytes 1048576 | tf_op jit(solution)/shard_map/pallas_call | solution.py:884
  145.5 1.5 collective-permute-start.36
  150.4 3.1 %collective-permute-done.26 = bf16[2,4,2,512]{3,2,1,0:T(2,128)(2,1)S(1)} collective-permute-done((bf16[2,4,2,512]{3,2,1,0:T(2,128)(2,1)S(1)}, bf16[2,4,2,512]{3,2,1,0:T(2,128)(2,1)S(1)}, u32[]{:S(2)}, u32[]{:S(2)}) %collective-permute-start.26) | collective-permute-done | bytes 16416 | tf_op jit(solution)/shard_map/ppermute | solution.py:18
  154.4 2.0 shard_map.274
  158.6 2.0 shard_map.276
  163.2 2.1 %shard_map.281 = (bf16[4,304,128]{2,1,0:T(8,128)(2,1)}, bf16[4,304,128]{2,1,0:T(8,128)(2,1)}) custom-call(bf16[8,304,128]{2,1,0:T(8,128)(2,1)} %get-tuple-element.96.rest_4_.refs_0_, bf16[8,304,128]{2,1,0:T(8,128)(2,1)} %copy-done.11), custom_call_target="tpu_custom_call" | custom-call | flops 2000000000 | bytes 1048576 | tf_op jit(solution)/shard_map/pallas_call | solution.py:170
  167.7 2.2 %shard_map.282 = (bf16[4,304,128]{2,1,0:T(8,128)(2,1)}, bf16[4,304,128]{2,1,0:T(8,128)(2,1)}) custom-call(bf16[8,304,128]{2,1,0:T(8,128)(2,1)} %get-tuple-element.100.rest_6_.refs_0_, bf16[8,304,128]{2,1,0:T(8,128)(2,1)} %copy-done.12), custom_call_target="tpu_custom_call" | custom-call | flops 2000000000 | bytes 1048576 | tf_op jit(solution)/shard_map/pallas_call | solution.py:170
  172.1 1.8 shard_map.275
  175.1 1.8 shard_map.277
  178.9 2.9 %collective-permute-done.33.refs_3_ = bf16[4,112,128]{2,1,0:T(8,128)(2,1)S(1)} collective-permute-done((bf16[4,112,128]{2,1,0:T(8,128)(2,1)}, bf16[4,112,128]{2,1,0:T(8,128)(2,1)S(1)}, u32[]{:S(2)}, u32[]{:S(2)}) %collective-permute-start.33) | collective-permute-done | bytes 114720 | tf_op jit(solution)/shard_map/ppermute | solution.py:18
  182.5 1.8 shard_map.278
  184.3 1.8 collective-permute-start.34
  187.0 2.1 %shard_map.283 = (bf16[2,608,128]{2,1,0:T(8,128)(2,1)}, bf16[2,608,128]{2,1,0:T(8,128)(2,1)}) custom-call(bf16[4,304,128]{2,1,0:T(8,128)(2,1)} %get-tuple-element.131.refs_0_, bf16[4,304,128]{2,1,0:T(8,128)(2,1)} %copy-done.18, bf16[4,304,128]{2,1,0:T(8,128)(2,1)} %get-tuple-element.133.refs_2_, bf16[4,304,128]{2,1,0:T(8,128)(2,1)} %copy-done.19), custom_call_target="tpu_custom_call" | custom-call | flops 2000000000 | bytes 1048576 | tf_op jit(solution)/shard_map/pallas_call | solution.py:170
  189.3 5.1 %shard_map.273 = f32[4,256,512]{2,1,0:T(8,128)} custom-call(bf16[4,256,512]{2,1,0:T(8,128)(2,1)} %x_ref.9, f32[4,256,512]{2,1,0:T(8,128)} %get-tuple-element.109.back_ref, f32[4,2,512]{2,1,0:T(2,128)} %add_bitcast_fusion.own_ref, f32[8,512]{1,0:T(8,128)} %get-tuple-element.85.lines_ref, f32[4,256,512]{2,1,0:T(8,128)} %get-tuple-element.111.mgrad_ref), custom_call_target="tpu_custom_call" | custom-call | flops 4000000000 | bytes 1048576 | tf_op jit(solution)/shard_map/pallas_call | solution.py:914
  195.1 1.6 shard_map.279
  198.5 1.8 shard_map.284
  200.3 1.8 collective-permute-start.41
  204.2 1.6 shard_map.280
  205.7 2.6 %collective-permute-done.41.theirs_ref = bf16[1,608,128]{2,1,0:T(8,128)(2,1)S(1)} collective-permute-done((bf16[1,608,128]{2,1,0:T(8,128)(2,1)}, bf16[1,608,128]{2,1,0:T(8,128)(2,1)S(1)}, u32[]{:S(2)}, u32[]{:S(2)}) %collective-permute-start.41) | collective-permute-done | bytes 155680 | tf_op jit(solution)/shard_map/ppermute | solution.py:18
  209.0 1.8 shard_map.285
  (146 shorter events, 40.2 us)
Async XLA Ops:
  2.8 7.0 %collective-permute-start.3 = (bf16[1,224,128]{2,1,0:T(8,128)(2,1)}, bf16[1,224,128]{2,1,0:T(8,128)(2,1)S(1)}, u32[]{:S(2)}, u32[]{:S(2)}) collective-permute-start(bf16[1,224,128]{2,1,0:T(8,128)(2,1)} %shard_map.263), channel_id=1, source_target_pairs={{0,4},{1,5},{2,6},{3,7},{4,0},{5,1},{6,2},{7,3},{8,12},{9,13},{10,... | collective-permute-start | bytes 172040 | tf_op jit(solution)/shard_map/ppermute | solution.py:18
  10.7 4.9 %collective-permute-start.4 = (bf16[2,224,128]{2,1,0:T(8,128)(2,1)S(1)}, bf16[2,224,128]{2,1,0:T(8,128)(2,1)S(1)}, u32[]{:S(2)}, u32[]{:S(2)}) collective-permute-start(bf16[2,224,128]{2,1,0:T(8,128)(2,1)S(1)} %pad_maximum_fusion.8), channel_id=1, source_target_pairs={{0,2},{1,3},{2,0},{3,1},{4,6},{5,7},{6,4},{7,5},{8,10},{9,11},{10,... | collective-permute-start | bytes 344072 | tf_op jit(solution)/shard_map/ppermute | solution.py:18
  18.6 13.9 %copy-start = (bf16[4,224,128]{2,1,0:T(8,128)(2,1)S(1)}, bf16[4,224,128]{2,1,0:T(8,128)(2,1)}, u32[]{:S(2)}) copy-start(bf16[4,224,128]{2,1,0:T(8,128)(2,1)} %pad_maximum_fusion.4.refs_3_) | copy-start | bytes 688132
  18.6 8.1 %collective-permute-start.13 = (bf16[1,576,128]{2,1,0:T(8,128)(2,1)}, bf16[1,576,128]{2,1,0:T(8,128)(2,1)S(1)}, u32[]{:S(2)}, u32[]{:S(2)}) collective-permute-start(bf16[1,576,128]{2,1,0:T(8,128)(2,1)} %shard_map.266), channel_id=1, source_target_pairs={{0,4},{1,5},{2,6},{3,7},{4,0},{5,1},{6,2},{7,3},{8,12},{9,13},{10,... | collective-permute-start | bytes 442376 | tf_op jit(solution)/shard_map/ppermute | solution.py:18
  24.7 4.8 %collective-permute-start = (bf16[1,4,2,1024]{3,2,1,0:T(2,128)(2,1)}, bf16[1,4,2,1024]{3,2,1,0:T(2,128)(2,1)S(1)}, u32[]{:S(2)}, u32[]{:S(2)}) collective-permute-start(bf16[1,4,2,1024]{3,2,1,0:T(2,128)(2,1)} %bitcast.5), channel_id=1, source_target_pairs={{0,4},{1,5},{2,6},{3,7},{4,0},{5,1},{6,2},{7,3},{8,12},{9,13},{10,... | collective-permute-start | bytes 49160 | tf_op jit(solution)/shard_map/ppermute | solution.py:18
  26.8 8.8 %collective-permute-start.14 = (bf16[2,576,128]{2,1,0:T(8,128)(2,1)S(1)}, bf16[2,576,128]{2,1,0:T(8,128)(2,1)S(1)}, u32[]{:S(2)}, u32[]{:S(2)}) collective-permute-start(bf16[2,576,128]{2,1,0:T(8,128)(2,1)S(1)} %pad_maximum_fusion.3), channel_id=1, source_target_pairs={{0,2},{1,3},{2,0},{3,1},{4,6},{5,7},{6,4},{7,5},{8,10},{9,11},{10,... | collective-permute-start | bytes 884744 | tf_op jit(solution)/shard_map/ppermute | solution.py:18
  30.3 12.5 %collective-permute-start.1 = (bf16[2,4,2,1024]{3,2,1,0:T(2,128)(2,1)S(1)}, bf16[2,4,2,1024]{3,2,1,0:T(2,128)(2,1)S(1)}, u32[]{:S(2)}, u32[]{:S(2)}) collective-permute-start(bf16[2,4,2,1024]{3,2,1,0:T(2,128)(2,1)S(1)} %pad_maximum_fusion.10), channel_id=1, source_target_pairs={{0,2},{1,3},{2,0},{3,1},{4,6},{5,7},{6,4},{7,5},{8,10},{9,11},{10,... | collective-permute-start | bytes 98312 | tf_op jit(solution)/shard_map/ppermute | solution.py:18
  32.5 9.7 %collective-permute-start.9 = (bf16[4,112,128]{2,1,0:T(8,128)(2,1)S(1)}, bf16[4,112,128]{2,1,0:T(8,128)(2,1)S(1)}, u32[]{:S(2)}, u32[]{:S(2)}) collective-permute-start(bf16[4,112,128]{2,1,0:T(8,128)(2,1)S(1)} %get-tuple-element.151), channel_id=1, source_target_pairs={{0,1},{1,0},{2,3},{3,2},{4,5},{5,4},{6,7},{7,6},{8,9},{9,8},{10,11... | collective-permute-start | bytes 344072 | tf_op jit(solution)/shard_map/ppermute | solution.py:18
  34.1 6.0 %collective-permute-start.5 = (bf16[4,112,128]{2,1,0:T(8,128)(2,1)S(1)}, bf16[4,112,128]{2,1,0:T(8,128)(2,1)S(1)}, u32[]{:S(2)}, u32[]{:S(2)}) collective-permute-start(bf16[4,112,128]{2,1,0:T(8,128)(2,1)S(1)} %get-tuple-element.152), channel_id=1, source_target_pairs={{0,16},{8,24},{16,0},{24,8},{1,17},{9,25},{17,1},{25,9},{2,18},{10... | collective-permute-start | bytes 344072 | tf_op jit(solution)/shard_map/ppermute | solution.py:18
  35.7 8.8 %collective-permute-start.19 = (bf16[4,288,128]{2,1,0:T(8,128)(2,1)S(1)}, bf16[4,288,128]{2,1,0:T(8,128)(2,1)S(1)}, u32[]{:S(2)}, u32[]{:S(2)}) collective-permute-start(bf16[4,288,128]{2,1,0:T(8,128)(2,1)S(1)} %get-tuple-element.149), channel_id=1, source_target_pairs={{0,1},{1,0},{2,3},{3,2},{4,5},{5,4},{6,7},{7,6},{8,9},{9,8},{10,11... | collective-permute-start | bytes 884744 | tf_op jit(solution)/shard_map/ppermute | solution.py:18
  40.2 10.3 %copy-start.4 = (bf16[8,112,128]{2,1,0:T(8,128)(2,1)}, bf16[8,112,128]{2,1,0:T(8,128)(2,1)S(1)}, u32[]{:S(2)}) copy-start(bf16[8,112,128]{2,1,0:T(8,128)(2,1)S(1)} %pad_maximum_fusion.5.refs_0_) | copy-start | bytes 688132
  40.2 6.5 %collective-permute-start.7 = (bf16[8,112,128]{2,1,0:T(8,128)(2,1)S(1)}, bf16[8,112,128]{2,1,0:T(8,128)(2,1)S(1)}, u32[]{:S(2)}, u32[]{:S(2)}) collective-permute-start(bf16[8,112,128]{2,1,0:T(8,128)(2,1)S(1)} %pad_maximum_fusion.5.refs_0_), channel_id=1, source_target_pairs={{0,1},{1,0},{2,3},{3,2},{4,5},{5,4},{6,7},{7,6},{8,9},{9,8},{10,11... | collective-permute-start | bytes 688136 | tf_op jit(solution)/shard_map/ppermute | solution.py:18
  40.7 9.2 %collective-permute-start.15 = (bf16[4,288,128]{2,1,0:T(8,128)(2,1)S(1)}, bf16[4,288,128]{2,1,0:T(8,128)(2,1)S(1)}, u32[]{:S(2)}, u32[]{:S(2)}) collective-permute-start(bf16[4,288,128]{2,1,0:T(8,128)(2,1)S(1)} %get-tuple-element.150), channel_id=1, source_target_pairs={{0,16},{8,24},{16,0},{24,8},{1,17},{9,25},{17,1},{25,9},{2,18},{10... | collective-permute-start | bytes 884744 | tf_op jit(solution)/shard_map/ppermute | solution.py:18
  42.3 7.7 %collective-permute-start.11 = (bf16[8,112,128]{2,1,0:T(8,128)(2,1)S(1)}, bf16[8,112,128]{2,1,0:T(8,128)(2,1)S(1)}, u32[]{:S(2)}, u32[]{:S(2)}) collective-permute-start(bf16[8,112,128]{2,1,0:T(8,128)(2,1)S(1)} %pad_maximum_fusion.6.refs_4_), channel_id=1, source_target_pairs={{0,16},{8,24},{16,0},{24,8},{1,17},{9,25},{17,1},{25,9},{2,18},{10... | collective-permute-start | bytes 688136 | tf_op jit(solution)/shard_map/ppermute | solution.py:18
  43.0 7.6 %collective-permute-start.2 = (bf16[4,4,2,1024]{3,2,1,0:T(2,128)(2,1)S(1)}, bf16[4,4,2,1024]{3,2,1,0:T(2,128)(2,1)S(1)}, u32[]{:S(2)}, u32[]{:S(2)}) collective-permute-start(bf16[4,4,2,1024]{3,2,1,0:T(2,128)(2,1)S(1)} %pad_maximum_fusion.9), channel_id=1, source_target_pairs={{0,1},{1,0},{2,3},{3,2},{4,5},{5,4},{6,7},{7,6},{8,9},{9,8},{10,11... | collective-permute-start | bytes 196616 | tf_op jit(solution)/shard_map/ppermute | solution.py:18
  44.6 7.6 %collective-permute-start.6 = (bf16[8,112,128]{2,1,0:T(8,128)(2,1)S(1)}, bf16[8,112,128]{2,1,0:T(8,128)(2,1)S(1)}, u32[]{:S(2)}, u32[]{:S(2)}) collective-permute-start(bf16[8,112,128]{2,1,0:T(8,128)(2,1)S(1)} %pad_maximum_fusion.5.refs_0_), channel_id=1, source_target_pairs={{0,8},{8,0},{16,24},{24,16},{1,9},{9,1},{17,25},{25,17},{2,10},{10... | collective-permute-start | bytes 688136 | tf_op jit(solution)/shard_map/ppermute | solution.py:18
  44.6 18.1 %copy-start.2 = (bf16[8,288,128]{2,1,0:T(8,128)(2,1)}, bf16[8,288,128]{2,1,0:T(8,128)(2,1)S(1)}, u32[]{:S(2)}) copy-start(bf16[8,288,128]{2,1,0:T(8,128)(2,1)S(1)} %pad_maximum_fusion.2.rest_4_) | copy-start | bytes 1769476
  46.7 7.8 %collective-permute-start.10 = (bf16[8,112,128]{2,1,0:T(8,128)(2,1)S(1)}, bf16[8,112,128]{2,1,0:T(8,128)(2,1)S(1)}, u32[]{:S(2)}, u32[]{:S(2)}) collective-permute-start(bf16[8,112,128]{2,1,0:T(8,128)(2,1)S(1)} %pad_maximum_fusion.6.refs_4_), channel_id=1, source_target_pairs={{0,8},{8,0},{16,24},{24,16},{1,9},{9,1},{17,25},{25,17},{2,10},{10... | collective-permute-start | bytes 688136 | tf_op jit(solution)/shard_map/ppermute | solution.py:18
  49.9 4.5 %collective-permute-start.8 = (bf16[8,112,128]{2,1,0:T(8,128)(2,1)S(1)}, bf16[8,112,128]{2,1,0:T(8,128)(2,1)S(1)}, u32[]{:S(2)}, u32[]{:S(2)}) collective-permute-start(bf16[8,112,128]{2,1,0:T(8,128)(2,1)S(1)} %collective-permute-done.7.refs_2_), channel_id=1, source_target_pairs={{0,8},{8,0},{16,24},{24,16},{1,9},{9,1},{17,25},{25,17},{2,10},{10... | collective-permute-start | bytes 688136 | tf_op jit(solution)/shard_map/ppermute | solution.py:18
  49.9 6.0 %collective-permute-start.12 = (bf16[8,112,128]{2,1,0:T(8,128)(2,1)S(1)}, bf16[8,112,128]{2,1,0:T(8,128)(2,1)}, u32[]{:S(2)}, u32[]{:S(2)}) collective-permute-start(bf16[8,112,128]{2,1,0:T(8,128)(2,1)S(1)} %collective-permute-done.11.refs_6_), channel_id=1, source_target_pairs={{0,8},{8,0},{16,24},{24,16},{1,9},{9,1},{17,25},{25,17},{2,10},{10... | collective-permute-start | bytes 688136 | tf_op jit(solution)/shard_map/ppermute | solution.py:18
  50.5 12.1 %copy-start.3 = (bf16[8,288,128]{2,1,0:T(8,128)(2,1)}, bf16[8,288,128]{2,1,0:T(8,128)(2,1)S(1)}, u32[]{:S(2)}) copy-start(bf16[8,288,128]{2,1,0:T(8,128)(2,1)S(1)} %pad_maximum_fusion.1.rest_0_) | copy-start | bytes 1769476
  50.5 15.4 %collective-permute-start.17 = (bf16[8,288,128]{2,1,0:T(8,128)(2,1)S(1)}, bf16[8,288,128]{2,1,0:T(8,128)(2,1)S(1)}, u32[]{:S(2)}, u32[]{:S(2)}) collective-permute-start(bf16[8,288,128]{2,1,0:T(8,128)(2,1)S(1)} %pad_maximum_fusion.1.rest_0_), channel_id=1, source_target_pairs={{0,1},{1,0},{2,3},{3,2},{4,5},{5,4},{6,7},{7,6},{8,9},{9,8},{10,11... | collective-permute-start | bytes 1769480 | tf_op jit(solution)/shard_map/ppermute | solution.py:18
  52.1 15.0 %collective-permute-start.21 = (bf16[8,288,128]{2,1,0:T(8,128)(2,1)S(1)}, bf16[8,288,128]{2,1,0:T(8,128)(2,1)S(1)}, u32[]{:S(2)}, u32[]{:S(2)}) collective-permute-start(bf16[8,288,128]{2,1,0:T(8,128)(2,1)S(1)} %pad_maximum_fusion.2.rest_4_), channel_id=1, source_target_pairs={{0,16},{8,24},{16,0},{24,8},{1,17},{9,25},{17,1},{25,9},{2,18},{10... | collective-permute-start | bytes 1769480 | tf_op jit(solution)/shard_map/ppermute | solution.py:18
  62.6 12.3 %collective-permute-start.16 = (bf16[8,288,128]{2,1,0:T(8,128)(2,1)S(1)}, bf16[8,288,128]{2,1,0:T(8,128)(2,1)S(1)}, u32[]{:S(2)}, u32[]{:S(2)}) collective-permute-start(bf16[8,288,128]{2,1,0:T(8,128)(2,1)S(1)} %pad_maximum_fusion.1.rest_0_), channel_id=1, source_target_pairs={{0,8},{8,0},{16,24},{24,16},{1,9},{9,1},{17,25},{25,17},{2,10},{10... | collective-permute-start | bytes 1769480 | tf_op jit(solution)/shard_map/ppermute | solution.py:18
  62.7 12.2 %collective-permute-start.20 = (bf16[8,288,128]{2,1,0:T(8,128)(2,1)S(1)}, bf16[8,288,128]{2,1,0:T(8,128)(2,1)}, u32[]{:S(2)}, u32[]{:S(2)}) collective-permute-start(bf16[8,288,128]{2,1,0:T(8,128)(2,1)S(1)} %pad_maximum_fusion.2.rest_4_), channel_id=1, source_target_pairs={{0,8},{8,0},{16,24},{24,16},{1,9},{9,1},{17,25},{25,17},{2,10},{10... | collective-permute-start | bytes 1769480 | tf_op jit(solution)/shard_map/ppermute | solution.py:18
  65.9 9.0 %collective-permute-start.18 = (bf16[8,288,128]{2,1,0:T(8,128)(2,1)S(1)}, bf16[8,288,128]{2,1,0:T(8,128)(2,1)}, u32[]{:S(2)}, u32[]{:S(2)}) collective-permute-start(bf16[8,288,128]{2,1,0:T(8,128)(2,1)S(1)} %collective-permute-done.17.rest_2_), channel_id=1, source_target_pairs={{0,8},{8,0},{16,24},{24,16},{1,9},{9,1},{17,25},{25,17},{2,10},{10... | collective-permute-start | bytes 1769480 | tf_op jit(solution)/shard_map/ppermute | solution.py:18
  67.1 7.8 %collective-permute-start.22 = (bf16[8,288,128]{2,1,0:T(8,128)(2,1)S(1)}, bf16[8,288,128]{2,1,0:T(8,128)(2,1)}, u32[]{:S(2)}, u32[]{:S(2)}) collective-permute-start(bf16[8,288,128]{2,1,0:T(8,128)(2,1)S(1)} %collective-permute-done.21.rest_6_), channel_id=1, source_target_pairs={{0,8},{8,0},{16,24},{24,16},{1,9},{9,1},{17,25},{25,17},{2,10},{10... | collective-permute-start | bytes 1769480 | tf_op jit(solution)/shard_map/ppermute | solution.py:18
  111.1 7.4 %collective-permute-start.23 = (bf16[16,304,128]{2,1,0:T(8,128)(2,1)}, bf16[16,304,128]{2,1,0:T(8,128)(2,1)S(1)}, u32[]{:S(2)}, u32[]{:S(2)}) collective-permute-start(bf16[16,304,128]{2,1,0:T(8,128)(2,1)} %get-tuple-element.95), channel_id=1, source_target_pairs={{0,8},{8,0},{16,24},{24,16},{1,9},{9,1},{17,25},{25,17},{2,10},{10... | collective-permute-start | bytes 3735560 | tf_op jit(solution)/shard_map/ppermute | solution.py:18
  111.5 10.9 %collective-permute-start.24 = (bf16[16,304,128]{2,1,0:T(8,128)(2,1)}, bf16[16,304,128]{2,1,0:T(8,128)(2,1)S(1)}, u32[]{:S(2)}, u32[]{:S(2)}) collective-permute-start(bf16[16,304,128]{2,1,0:T(8,128)(2,1)} %get-tuple-element.99), channel_id=1, source_target_pairs={{0,8},{8,0},{16,24},{24,16},{1,9},{9,1},{17,25},{25,17},{2,10},{10... | collective-permute-start | bytes 3735560 | tf_op jit(solution)/shard_map/ppermute | solution.py:18
  133.4 12.1 %copy-start.10 = (bf16[8,304,128]{2,1,0:T(8,128)(2,1)S(1)}, bf16[8,304,128]{2,1,0:T(8,128)(2,1)}, u32[]{:S(2)}) copy-start(bf16[8,304,128]{2,1,0:T(8,128)(2,1)} %get-tuple-element.97.rest_5_) | copy-start | bytes 1867780
  133.4 16.3 %copy-start.9 = (bf16[8,304,128]{2,1,0:T(8,128)(2,1)S(1)}, bf16[8,304,128]{2,1,0:T(8,128)(2,1)}, u32[]{:S(2)}) copy-start(bf16[8,304,128]{2,1,0:T(8,128)(2,1)} %get-tuple-element.101.rest_7_) | copy-start | bytes 1867780
  144.9 4.0 %collective-permute-start.25 = (bf16[4,4,2,512]{3,2,1,0:T(2,128)(2,1)S(1)}, bf16[4,4,2,512]{3,2,1,0:T(2,128)(2,1)S(1)}, u32[]{:S(2)}, u32[]{:S(2)}) collective-permute-start(bf16[4,4,2,512]{3,2,1,0:T(2,128)(2,1)S(1)} %slice.35), channel_id=1, source_target_pairs={{0,1},{1,0},{2,3},{3,2},{4,5},{5,4},{6,7},{7,6},{8,9},{9,8},{10,11... | collective-permute-start | bytes 98312 | tf_op jit(solution)/shard_map/ppermute | solution.py:18
  145.5 16.9 %collective-permute-start.36 = (bf16[8,304,128]{2,1,0:T(8,128)(2,1)S(1)}, bf16[8,304,128]{2,1,0:T(8,128)(2,1)S(1)}, u32[]{:S(2)}, u32[]{:S(2)}) collective-permute-start(bf16[8,304,128]{2,1,0:T(8,128)(2,1)S(1)} %copy-done.10), channel_id=1, source_target_pairs={{0,16},{8,24},{16,0},{24,8},{1,17},{9,25},{17,1},{25,9},{2,18},{10... | collective-permute-start | bytes 1867784 | tf_op jit(solution)/shard_map/ppermute | solution.py:18
  147.0 6.6 %collective-permute-start.28 = (bf16[16,112,128]{2,1,0:T(8,128)(2,1)}, bf16[16,112,128]{2,1,0:T(8,128)(2,1)S(1)}, u32[]{:S(2)}, u32[]{:S(2)}) collective-permute-start(bf16[16,112,128]{2,1,0:T(8,128)(2,1)} %get-tuple-element.113), channel_id=1, source_target_pairs={{0,8},{8,0},{16,24},{24,16},{1,9},{9,1},{17,25},{25,17},{2,10},{10... | collective-permute-start | bytes 1376264 | tf_op jit(solution)/shard_map/ppermute | solution.py:18
  147.0 10.9 %collective-permute-start.31 = (bf16[16,112,128]{2,1,0:T(8,128)(2,1)}, bf16[16,112,128]{2,1,0:T(8,128)(2,1)S(1)}, u32[]{:S(2)}, u32[]{:S(2)}) collective-permute-start(bf16[16,112,128]{2,1,0:T(8,128)(2,1)} %get-tuple-element.119), channel_id=1, source_target_pairs={{0,8},{8,0},{16,24},{24,16},{1,9},{9,1},{17,25},{25,17},{2,10},{10... | collective-permute-start | bytes 1376264 | tf_op jit(solution)/shard_map/ppermute | solution.py:18
  149.7 3.8 %collective-permute-start.26 = (bf16[2,4,2,512]{3,2,1,0:T(2,128)(2,1)S(1)}, bf16[2,4,2,512]{3,2,1,0:T(2,128)(2,1)S(1)}, u32[]{:S(2)}, u32[]{:S(2)}) collective-permute-start(bf16[2,4,2,512]{3,2,1,0:T(2,128)(2,1)S(1)} %slice.45), channel_id=1, source_target_pairs={{0,2},{1,3},{2,0},{3,1},{4,6},{5,7},{6,4},{7,5},{8,10},{9,11},{10,... | collective-permute-start | bytes 49160 | tf_op jit(solution)/shard_map/ppermute | solution.py:18
  149.8 17.1 %collective-permute-start.38 = (bf16[8,304,128]{2,1,0:T(8,128)(2,1)S(1)}, bf16[8,304,128]{2,1,0:T(8,128)(2,1)S(1)}, u32[]{:S(2)}, u32[]{:S(2)}) collective-permute-start(bf16[8,304,128]{2,1,0:T(8,128)(2,1)S(1)} %copy-done.9), channel_id=1, source_target_pairs={{0,1},{1,0},{2,3},{3,2},{4,5},{5,4},{6,7},{7,6},{8,9},{9,8},{10,11... | collective-permute-start | bytes 1867784 | tf_op jit(solution)/shard_map/ppermute | solution.py:18
  153.5 23.9 %collective-permute-start.27 = (bf16[1,4,2,512]{3,2,1,0:T(2,128)(2,1)S(1)}, bf16[1,4,2,512]{3,2,1,0:T(2,128)(2,1)S(1)}, u32[]{:S(2)}, u32[]{:S(2)}) collective-permute-start(bf16[1,4,2,512]{3,2,1,0:T(2,128)(2,1)S(1)} %slice.47), channel_id=1, source_target_pairs={{0,4},{1,5},{2,6},{3,7},{4,0},{5,1},{6,2},{7,3},{8,12},{9,13},{10,... | collective-permute-start | bytes 24584 | tf_op jit(solution)/shard_map/ppermute | solution.py:18
  156.4 15.0 %collective-permute-start.29 = (bf16[8,112,128]{2,1,0:T(8,128)(2,1)}, bf16[8,112,128]{2,1,0:T(8,128)(2,1)S(1)}, u32[]{:S(2)}, u32[]{:S(2)}) collective-permute-start(bf16[8,112,128]{2,1,0:T(8,128)(2,1)} %get-tuple-element.115), channel_id=1, source_target_pairs={{0,16},{8,24},{16,0},{24,8},{1,17},{9,25},{17,1},{25,9},{2,18},{10... | collective-permute-start | bytes 688136 | tf_op jit(solution)/shard_map/ppermute | solution.py:18
  160.6 13.8 %collective-permute-start.32 = (bf16[8,112,128]{2,1,0:T(8,128)(2,1)}, bf16[8,112,128]{2,1,0:T(8,128)(2,1)S(1)}, u32[]{:S(2)}, u32[]{:S(2)}) collective-permute-start(bf16[8,112,128]{2,1,0:T(8,128)(2,1)} %get-tuple-element.121), channel_id=1, source_target_pairs={{0,1},{1,0},{2,3},{3,2},{4,5},{5,4},{6,7},{7,6},{8,9},{9,8},{10,11... | collective-permute-start | bytes 688136 | tf_op jit(solution)/shard_map/ppermute | solution.py:18
  165.4 20.8 %collective-permute-start.37 = (bf16[4,304,128]{2,1,0:T(8,128)(2,1)}, bf16[4,304,128]{2,1,0:T(8,128)(2,1)S(1)}, u32[]{:S(2)}, u32[]{:S(2)}) collective-permute-start(bf16[4,304,128]{2,1,0:T(8,128)(2,1)} %get-tuple-element.132), channel_id=1, source_target_pairs={{0,1},{1,0},{2,3},{3,2},{4,5},{5,4},{6,7},{7,6},{8,9},{9,8},{10,11... | collective-permute-start | bytes 933896 | tf_op jit(solution)/shard_map/ppermute | solution.py:18
  169.9 16.3 %collective-permute-start.39 = (bf16[4,304,128]{2,1,0:T(8,128)(2,1)}, bf16[4,304,128]{2,1,0:T(8,128)(2,1)S(1)}, u32[]{:S(2)}, u32[]{:S(2)}) collective-permute-start(bf16[4,304,128]{2,1,0:T(8,128)(2,1)} %get-tuple-element.134), channel_id=1, source_target_pairs={{0,16},{8,24},{16,0},{24,8},{1,17},{9,25},{17,1},{25,9},{2,18},{10... | collective-permute-start | bytes 933896 | tf_op jit(solution)/shard_map/ppermute | solution.py:18
  173.8 5.1 %collective-permute-start.30 = (bf16[4,112,128]{2,1,0:T(8,128)(2,1)}, bf16[4,112,128]{2,1,0:T(8,128)(2,1)S(1)}, u32[]{:S(2)}, u32[]{:S(2)}) collective-permute-start(bf16[4,112,128]{2,1,0:T(8,128)(2,1)} %get-tuple-element.117), channel_id=1, source_target_pairs={{0,1},{1,0},{2,3},{3,2},{4,5},{5,4},{6,7},{7,6},{8,9},{9,8},{10,11... | collective-permute-start | bytes 344072 | tf_op jit(solution)/shard_map/ppermute | solution.py:18
  176.9 5.0 %collective-permute-start.33 = (bf16[4,112,128]{2,1,0:T(8,128)(2,1)}, bf16[4,112,128]{2,1,0:T(8,128)(2,1)S(1)}, u32[]{:S(2)}, u32[]{:S(2)}) collective-permute-start(bf16[4,112,128]{2,1,0:T(8,128)(2,1)} %get-tuple-element.123), channel_id=1, source_target_pairs={{0,16},{8,24},{16,0},{24,8},{1,17},{9,25},{17,1},{25,9},{2,18},{10... | collective-permute-start | bytes 344072 | tf_op jit(solution)/shard_map/ppermute | solution.py:18
  184.3 10.1 %collective-permute-start.34 = (bf16[2,224,128]{2,1,0:T(8,128)(2,1)}, bf16[2,224,128]{2,1,0:T(8,128)(2,1)S(1)}, u32[]{:S(2)}, u32[]{:S(2)}) collective-permute-start(bf16[2,224,128]{2,1,0:T(8,128)(2,1)} %get-tuple-element.125), channel_id=1, source_target_pairs={{0,2},{1,3},{2,0},{3,1},{4,6},{5,7},{6,4},{7,5},{8,10},{9,11},{10,... | collective-permute-start | bytes 344072 | tf_op jit(solution)/shard_map/ppermute | solution.py:18
  189.1 8.6 %collective-permute-start.40 = (bf16[2,608,128]{2,1,0:T(8,128)(2,1)}, bf16[2,608,128]{2,1,0:T(8,128)(2,1)S(1)}, u32[]{:S(2)}, u32[]{:S(2)}) collective-permute-start(bf16[2,608,128]{2,1,0:T(8,128)(2,1)} %get-tuple-element.136), channel_id=1, source_target_pairs={{0,2},{1,3},{2,0},{3,1},{4,6},{5,7},{6,4},{7,5},{8,10},{9,11},{10,... | collective-permute-start | bytes 933896 | tf_op jit(solution)/shard_map/ppermute | solution.py:18
  196.7 6.9 %collective-permute-start.35 = (bf16[1,224,128]{2,1,0:T(8,128)(2,1)}, bf16[1,224,128]{2,1,0:T(8,128)(2,1)S(1)}, u32[]{:S(2)}, u32[]{:S(2)}) collective-permute-start(bf16[1,224,128]{2,1,0:T(8,128)(2,1)} %get-tuple-element.127), channel_id=1, source_target_pairs={{0,4},{1,5},{2,6},{3,7},{4,0},{5,1},{6,2},{7,3},{8,12},{9,13},{10,... | collective-permute-start | bytes 172040 | tf_op jit(solution)/shard_map/ppermute | solution.py:18
  200.3 8.0 %collective-permute-start.41 = (bf16[1,608,128]{2,1,0:T(8,128)(2,1)}, bf16[1,608,128]{2,1,0:T(8,128)(2,1)S(1)}, u32[]{:S(2)}, u32[]{:S(2)}) collective-permute-start(bf16[1,608,128]{2,1,0:T(8,128)(2,1)} %get-tuple-element.138), channel_id=1, source_target_pairs={{0,4},{1,5},{2,6},{3,7},{4,0},{5,1},{6,2},{7,3},{8,12},{9,13},{10,... | collective-permute-start | bytes 466952 | tf_op jit(solution)/shard_map/ppermute | solution.py:18
  (27 other events, 75.9 us)
